TPU v7x, 256 devices: a whole 4x4x8 slice. The times are simulated.
256 devices in a mesh: dp: 32 (over x, y, core), tensor: 8 (over z).
Axes of the slice: x: 4, y: 4, z: 8, core: 2. Of those that a mesh axis runs over, the one named last changes fastest.
Arguments:
- hidden: bfloat16 [32768, 8192], P(('dp', 'tensor')), may hold values from -50 to 50
- out_weight: bfloat16 [128256, 8192], P(('dp', 'tensor')), may hold values from -1 to 1
- loss_mask: int32 [32768], P(('dp', 'tensor')), may hold values from 0 to 1, as said below
- targets: int32 [32768], P(('dp', 'tensor')), may hold values from 0 to 128255
- kept_count: int32 [256], P(('dp', 'tensor')), may hold values from 0 to 1, as said below
Outputs:
- hidden_grad: bfloat16 [32768, 8192], P(('dp', 'tensor'))
- row_loss: float32 [32768], P(('dp', 'tensor'))
Inputs may be any that keep to these rules, and one draw needn't show every extreme that they name: `loss_mask`: each device's 128 rows hold at least 1 ones. `kept_count`: some entry equals 1 and some entry equals 0.
All inputs are finite; a program needn't handle non-finite values.
Results may differ from a plain program's by a relative error of at most 0.0026.
Values may be sent and summed in bfloat16 or wider, within the bound.
No kernel may reach another device: no remote copies, remote signals or barrier semaphores. Data moves between devices by JAX's collectives and lax.ppermute only.
A program may use at most 128 MiB of HBM per device.

v0:
```python
import jax
import jax.numpy as jnp
from jax import lax
from jax.sharding import PartitionSpec as P

CAP = 1


loss_scale = 128.0


def shards(hidden, out_weight, loss_mask, targets, kept_count):
    order_pos = jnp.cumsum(loss_mask) - 1
    kept_row = (loss_mask == 1) & (order_pos < kept_count[0])
    slot_ids = jnp.arange(CAP, dtype=jnp.int32)
    slot_hits = kept_row[None, :] & (order_pos[None, :] == slot_ids[:, None])
    packed = jnp.dot(
        slot_hits.astype(jnp.bfloat16), hidden, preferred_element_type=jnp.float32
    ).astype(jnp.bfloat16)
    slot_target = jnp.sum(jnp.where(slot_hits, targets[None, :], 0), axis=1)
    packed_target = jnp.where(jnp.any(slot_hits, axis=1), slot_target, -1)
    gathered, gathered_target = (
        lax.all_gather(packed, ("dp", "tensor"), axis=0, tiled=True),
        lax.all_gather(packed_target, ("dp", "tensor"), axis=0, tiled=True),
    )
    filled = gathered_target >= 0
    vocab_rows = out_weight.shape[0]
    device_pos = lax.axis_index(("dp", "tensor"))
    vocab_ids = device_pos * vocab_rows + jnp.arange(vocab_rows, dtype=jnp.int32)
    logits = jnp.einsum("rd,vd->rv", gathered, out_weight, preferred_element_type=jnp.float32)
    target_hit = vocab_ids[None, :] == gathered_target[:, None]
    local_top = jnp.max(logits, axis=1)
    local_pick = jnp.sum(jnp.where(target_hit, logits, 0.0), axis=1)
    row_top = lax.pmax(local_top, ("dp", "tensor"))
    shifted_total = jnp.sum(jnp.exp(logits - row_top[:, None]), axis=1)
    row_total, picked = lax.psum((shifted_total, local_pick), ("dp", "tensor"))
    log_total = row_top + jnp.log(row_total)
    slot_loss = jnp.where(filled, log_total - picked, 0.0)
    probabilities = jnp.exp(logits - log_total[:, None])
    coefficient = jnp.where(
        filled[:, None], probabilities - target_hit.astype(jnp.float32), 0.0
    ).astype(jnp.bfloat16)
    own_grad = lax.psum_scatter(
        jnp.dot(coefficient, out_weight, preferred_element_type=jnp.float32),
        ("dp", "tensor"),
        scatter_dimension=0,
        tiled=True,
    )
    own_grad = own_grad * loss_scale
    own_loss = lax.dynamic_slice_in_dim(slot_loss, device_pos * CAP, CAP, 0)
    slot_pos = jnp.clip(order_pos, 0, CAP - 1)
    hidden_grad = jnp.where(kept_row[:, None], own_grad[slot_pos], 0.0).astype(jnp.bfloat16)
    row_loss = jnp.where(kept_row, own_loss[slot_pos], 0.0)
    return (hidden_grad, row_loss)


def solution(mesh):
    in_specs = (
        P(("dp", "tensor"), None),
        P(("dp", "tensor"), None),
        P(("dp", "tensor")),
        P(("dp", "tensor")),
        P(("dp", "tensor")),
    )
    out_specs = (P(("dp", "tensor"), None), P(("dp", "tensor")))
    return jax.shard_map(shards, mesh=mesh, in_specs=in_specs, out_specs=out_specs, check_vma=False)
```

profile of v0, /device:TPU:2, one launch (start us, length us, event | category | flops | bytes accessed | tf_op | source)
XLA Modules:
  0.0 587.9 jit_solution(10313876143399885499)
XLA Ops:
  7.2 0.0 copy-start
  7.2 0.0 all-gather.3.cloned.1.call-start
  8.0 0.8 copy.9
  8.8 0.2 reduce-window.4
  8.9 0.1 compare_reduce_fusion
  9.1 1.3 select_reduce_fusion
  10.4 0.0 copy-done
  10.4 0.4 fusion.11
  10.8 0.6 convert_element_type.16
  11.4 0.0 all-gather.3.cloned.1.call-update
  11.4 0.0 all-reduce.5.cloned.1.call-start
  11.5 0.6 and_reduce_fusion
  13.4 0.1 dynamic-update-slice
  13.5 79.5 %all-reduce = s32[256]{0:T(256)S(1)} all-reduce(s32[256]{0:T(256)S(1)} %dynamic-update-slice), channel_id=1, replica_groups=mesh['dp'=32,'tensor'=8] {'dp','tensor'}, use_global_device_ids=true, to_apply=%add | all-reduce | flops 256 | bytes 2048
  93.0 37.9 %all-gather.3.cloned.1.call-done = bf16[2097152]{0:T(1024)(128)(2,1)} async-done(((bf16[8192]{0:T(1024)(128)(2,1)}), bf16[2097152]{0:T(1024)(128)(2,1)}) %all-gather.3.cloned.1.call-update) | async-done | bytes 4194320 | tf_op jit(solution)/shard_map/all_gather | solution.py:23
  130.9 7.3 %reshape.49 = bf16[256,8192]{1,0:T(8,128)(2,1)} reshape(bf16[2097152]{0:T(1024)(128)(2,1)} %all-gather.3.cloned.1.call-done) | data formatting | bytes 8388608 | tf_op jit(solution)/shard_map/all_gather | solution.py:23
  138.2 6.3 %fusion.15 = (f32[256]{0:T(256)S(1)}, f32[256,501]{0,1:T(8,128)S(1)}) fusion(bf16[256,8192]{1,0:T(8,128)(2,1)} %reshape.49, bf16[501,8192]{1,0:T(8,128)(2,1)} %param.6), kind=kOutput, calls=%fused_computation.29 | convolution fusion | flops 2101474304 | bytes 12916736 | tf_op jit(solution)/shard_map/rd,vd->rv/dot_general | solution.py:30
  144.5 74.4 %pmax.7 = f32[256]{0:T(256)S(1)} all-reduce(f32[256]{0:T(256)S(1)} %get-tuple-element.13), channel_id=1, replica_groups=mesh['dp'=32,'tensor'=8] {'dp','tensor'}, use_global_device_ids=true, to_apply=%region_4.5 | all-reduce | flops 256 | bytes 2048 | tf_op jit(solution)/shard_map/pmax | solution.py:34
  218.9 0.2 fusion.3
  219.0 73.8 %all-reduce.2 = (f32[256]{0:T(256)S(1)}, f32[256]{0:T(256)S(1)}) all-reduce(f32[256]{0:T(256)S(1)} %get-tuple-element.3, f32[256]{0:T(256)S(1)} %get-tuple-element.2), channel_id=1, replica_groups=mesh['dp'=32,'tensor'=8] {'dp','tensor'}, use_global_device_ids=true, to_apply=%region_6.7 | all-reduce | flops 512 | bytes 4096 | tf_op jit(solution)/shard_map/psum | solution.py:36
  292.8 9.1 %fusion.4 = f32[256,8192]{1,0:T(8,128)} fusion(bf16[501,8192]{1,0:T(8,128)(2,1)} %param.6, f32[256,501]{0,1:T(8,128)S(1)} %get-tuple-element.14, s32[256]{0:T(256)S(1)} %all-reduce, f32[256]{0:T(256)S(1)} %get-tuple-element.10, s32[501]{0:T(512)S(1)} %iota_add_fusion, pred[256]{0:T(512)(128)(4,1)S(1)} %get-tuple-element.9), kind=kOutput, calls=%fused_computation.8 | convolution fusion | flops 2102115840 | bytes 17114324 | tf_op jit(solution)/shard_map/dot_general | solution.py:44
  301.9 0.0 all-reduce.5.cloned.1.call-update
  302.0 0.6 dynamic_slice.5
  302.5 1.2 broadcast_select_fusion
  303.7 274.7 %all-reduce.5.cloned.1.call-done = f32[256,8192]{1,0:T(8,128)} async-done(((f32[256,8192]{1,0:T(8,128)}), f32[256,8192]{1,0:T(8,128)}) %all-reduce.5.cloned.1.call-update) | async-done | bytes 8388624
  578.4 1.0 dynamic-slice_multiply_fusion
  579.4 1.7 select_convert_fusion
  (3 shorter events, 0.0 us)
Async XLA Ops:
  7.2 3.2 copy-start
  7.2 123.8 %all-gather.3.cloned.1.call-start = ((), (), s32[]{:S(2)}) async-start(), calls=%async_computation | async-start | bytes 4210688 | tf_op jit(solution)/shard_map/all_gather | solution.py:23
  11.4 567.0 %all-reduce.5.cloned.1.call-start = ((), (), s32[]{:S(2)}) async-start(), calls=%async_computation.1 | async-start | bytes 16777216
Sparse Core Ops, SparseCore 0:
  12.3 118.6 all-gather.2
  302.1 276.2 all-reduce.4
where the time goes:
time: 589 us; the launch traced here: 588 us
  waiting for transfers between devices  313 us (53%)
  blocking collectives  228 us (39%)
  between operations  16.1 us (3%)
  matrix products  15.7 us (3%)
  local copies, waits for them, and re-layouts  8.79 us (1%)
  other arithmetic  6.82 us (1%)
    unnamed x3, waiting for transfers between devices  275 us
    unnamed x1, blocking collectives  79.5 us
    pmax x1, blocking collectives, shards(): row_top = lax.pmax(local_top, ('dp', 'tensor'))  74.4 us
    psum x1, blocking collectives, shards(): row_total, picked = lax.psum((shifted_total, local_pick), ('dp', 'tensor'))  73.8 us
    all_gather x1, waiting for transfers between devices, shards(): lax.all_gather(packed, ('dp', 'tensor'), axis=0, tiled=True)  37.9 us
  transfers between devices with their start and end apart: 2, of which 2 were waited for; matrix products, arithmetic and copies ran while one was open for 0% of the time, Pallas kernels for 0%

commit v1 on v0

v1 whole, which is shorter than its diff:
```python
import jax
import jax.numpy as jnp
from jax import lax
from jax.sharding import Mesh, PartitionSpec as P

loss_scale = 128.0
send_scale = 32.0
send_type = jnp.float16


def device(x, y, c, z):
    return ((x * 4 + y) * 2 + c) * 8 + z


R4, R8 = range(4), range(8)
along_z = [[device(x, y, c, z) for z in R8] for x in R4 for y in R4 for c in (0, 1)]
along_x = [[[device(x, y, c, z) for x in R4] for y in R4 for z in R8] for c in (0, 1)]
along_y = [[[device(x, y, c, z) for y in R4] for x in R4 for z in R8] for c in (0, 1)]
inner = along_x[0] + along_y[1]
outer = along_y[0] + along_x[1]
same_core = [[device(x, y, c, z) for x in R4 for y in R4 for z in R8] for c in (0, 1)]
partner = [(device(x, y, c, z), device(x, y, 1 - c, z)) for x in R4 for y in R4 for c in (0, 1) for z in R8]


def exchange(value, groups):
    return lax.all_to_all(value, "d", 0, 0, axis_index_groups=groups)


def spread(value, groups):
    count = len(groups[0])
    return exchange(jnp.broadcast_to(value[None], (count,) + value.shape), groups)


def shards(hidden, out_weight, loss_mask, targets, kept_count):
    vocab_rows, width = out_weight.shape
    me = lax.axis_index("d")
    z, c, y, x = me % 8, (me // 8) % 2, (me // 16) % 4, me // 64
    other_weight = lax.ppermute(out_weight, "d", partner)

    positions = lax.broadcasted_iota(jnp.int32, loss_mask.shape, 0)
    first = jnp.min(jnp.where(loss_mask == 1, positions, loss_mask.shape[0]))
    kept_row = (positions == first) & (kept_count[0] > 0)
    code = jnp.sum(jnp.where(kept_row, targets + 1, 0))
    row = lax.dynamic_slice_in_dim(hidden, first, 1, 0)
    row = jnp.where(code > 0, row, jnp.zeros((), row.dtype))
    lane = lax.broadcasted_iota(jnp.int32, (1, 128), 1)
    digits = jnp.where(lane == 0, code % 256, jnp.where(lane == 1, (code // 256) % 256, jnp.where(lane == 2, code // 65536, 0)))
    packed = jnp.concatenate([row, digits.astype(row.dtype)], axis=1)

    rows = spread(packed, along_z).reshape(8, width + 128)
    rows = spread(rows, inner).reshape(32, width + 128)
    rows = spread(rows, outer).reshape(128, width + 128)
    gathered = rows[:, :width]
    digits = rows[:, width:width + 3].astype(jnp.int32)
    gathered_target = digits[:, 0] + 256 * digits[:, 1] + 65536 * digits[:, 2] - 1
    filled = gathered_target >= 0

    local = lax.broadcasted_iota(jnp.int32, (1, vocab_rows), 1)
    weights = (out_weight, other_weight)
    logits = [jnp.einsum("rd,vd->rv", gathered, w, preferred_element_type=jnp.float32) for w in weights]
    hits = [(local + base * vocab_rows) == gathered_target[:, None] for base in (me, me ^ 8)]
    top = jnp.maximum(jnp.max(logits[0], axis=1), jnp.max(logits[1], axis=1))
    total = sum(jnp.sum(jnp.exp(l - top[:, None]), axis=1) for l in logits)
    pick = sum(jnp.sum(jnp.where(h, l, 0.0), axis=1) for h, l in zip(hits, logits))
    stats = spread(jnp.stack([top, total, pick, pick]), same_core)
    row_top = jnp.max(stats[:, 0], axis=0)
    row_total = jnp.sum(stats[:, 1] * jnp.exp(stats[:, 0] - row_top[None]), axis=0)
    picked = jnp.sum(stats[:, 2], axis=0)
    log_total = row_top + jnp.log(row_total)
    slot_loss = jnp.where(filled, log_total - picked, 0.0)

    slot_grad = 0.0
    for l, h, w in zip(logits, hits, weights):
        coefficient = jnp.where(filled[:, None], jnp.exp(l - log_total[:, None]) - h.astype(jnp.float32), 0.0)
        slot_grad += jnp.dot(coefficient.astype(jnp.bfloat16), w, preferred_element_type=jnp.float32)
    part = (slot_grad * (loss_scale * send_scale)).astype(send_type).reshape(4, 32, width)
    part = jnp.sum(exchange(part, outer).astype(jnp.float32), axis=0)
    part = part.astype(send_type).reshape(4, 8, width)
    part = jnp.sum(exchange(part, inner).astype(jnp.float32), axis=0)
    part = part.astype(send_type).reshape(8, 1, width)
    own_grad = jnp.sum(exchange(part, along_z).astype(jnp.float32), axis=0) * (1.0 / send_scale)

    slot = jnp.where(c == 0, y * 4 + x, x * 4 + y) * 8 + z
    own_loss = lax.dynamic_slice_in_dim(slot_loss, slot, 1, 0)
    hidden_grad = jnp.where(kept_row[:, None], own_grad, 0.0).astype(jnp.bfloat16)
    row_loss = jnp.where(kept_row, own_loss, 0.0)
    return hidden_grad, row_loss


def solution(mesh):
    flat = Mesh(mesh.devices.reshape(-1), ("d",))
    rows = P("d", None)
    vector = P("d")
    return jax.shard_map(
        shards, mesh=flat, in_specs=(rows, rows, vector, vector, vector), out_specs=(rows, vector), check_vma=False
    )
```

time: 589 us -> 155 us (0.26)
  waiting for transfers between devices: 313 us -> 35.4 us
  blocking collectives: 228 us -> 60 us
  starting transfers between devices: 0.08 us -> 14.8 us
  between operations: 16.1 us -> 6.35 us
  matrix products: 15.7 us -> 21.8 us
    unnamed x3 -> x0, waiting for transfers between devices: 275 us -> none
    unnamed x1 -> x0, blocking collectives: 79.5 us -> none
    pmax x1 -> x0, blocking collectives: 74.4 us -> none  [shards(): row_top = lax.pmax(local_top, ('dp', 'tensor'))]
    psum x1 -> x0, blocking collectives: 73.8 us -> none  [shards(): row_total, picked = lax.psum((shifted_total, local_pick), ('dp', 'tensor'))]
    all_to_all x0 -> x4, blocking collectives: none -> 60 us  [exchange(): return lax.all_to_all(value, 'd', 0, 0, axis_index_groups=groups)]
    all_gather x1 -> x0, waiting for transfers between devices: 37.9 us -> none  [shards(): lax.all_gather(packed, ('dp', 'tensor'), axis=0, tiled=True)]
    all_to_all x0 -> x3, waiting for transfers between devices: none -> 35.4 us  [exchange(): return lax.all_to_all(value, 'd', 0, 0, axis_index_groups=groups)]
    all_to_all x0 -> x3, starting transfers between devices: none -> 14.7 us  [exchange(): return lax.all_to_all(value, 'd', 0, 0, axis_index_groups=groups)]
  transfers between devices with their start and end apart: 2 -> 4, of which waited for: 2 -> 3; matrix products, arithmetic and copies ran while one was open for 0% -> 10% of each run, Pallas kernels for 0% -> 0%
where the time goes in v1:
time: 155 us
  blocking collectives  60 us (39%)
  waiting for transfers between devices  35.4 us (23%)
  matrix products  21.8 us (14%)
  starting transfers between devices  14.8 us (10%)
  other arithmetic  10.8 us (7%)
  between operations  6.35 us (4%)
  local copies, waits for them, and re-layouts  5.45 us (4%)
    all_to_all x4, blocking collectives, exchange(): return lax.all_to_all(value, 'd', 0, 0, axis_index_groups=groups)  60 us
    all_to_all x3, waiting for transfers between devices, exchange(): return lax.all_to_all(value, 'd', 0, 0, axis_index_groups=groups)  35.4 us
    all_to_all x3, starting transfers between devices, exchange(): return lax.all_to_all(value, 'd', 0, 0, axis_index_groups=groups)  14.7 us
    dot_general x2, matrix products, shards(): jnp.einsum('rd,vd->rv', gathered, w, preferred_element_type=jnp.float32)  11.3 us
    dot_general x2, matrix products, shards(): jnp.dot(coefficient.astype(jnp.bfloat16), w, preferred_element_type=jnp.f...  10.5 us
  transfers between devices with their start and end apart: 4, of which 3 were waited for; matrix products, arithmetic and copies ran while one was open for 10% of the time, Pallas kernels for 0%

profile of v1, /device:TPU:2, one launch (start us, length us, event | category | flops | bytes accessed | tf_op | source)
XLA Modules:
  0.0 154.6 jit_solution(11964239914323487857)
XLA Ops:
  0.6 0.1 collective-permute-start
  1.4 1.3 fusion.30
  2.7 1.9 %select_reduce_fusion = (s32[]{:T(128)}, pred[128]{0:T(512)(128)(4,1)S(1)}) fusion(s32[128]{0:T(128)} %param.8, pred[]{:T(512)} %bitcast, s32[]{:T(128)} %fusion.30), kind=kLoop, calls=%fused_computation.64 | loop fusion | flops 639 | bytes 649 | tf_op jit(solution)/shard_map/reduce_sum | solution.py:43
  9.4 1.0 broadcast_select_fusion
  10.4 0.1 maximum_reduce_fusion
  10.5 0.1 broadcast_in_dim.129
  10.7 0.5 broadcast.123
  11.2 1.4 reduce.9
  12.6 0.1 reshape.151
  12.7 18.1 %all_to_all.35 = bf16[8,2,4160]{2,1,0:T(2,128)(2,1)S(1)} all-to-all(bf16[8,2,4160]{2,1,0:T(2,128)(2,1)S(1)} %reshape.151), channel_id=1, replica_groups={{0,1,2,3,4,5,6,7},{8,9,10,11,12,13,14,15},{16,17,18,19,20,21,22,23},{24..., dimensions={0} | all-to-all | bytes 266240 | tf_op jit(solution)/shard_map/all_to_all | solution.py:26
  30.8 0.1 reshape.152
  31.0 11.3 %all_to_all.36 = bf16[4,8,8320]{2,1,0:T(8,128)(2,1)S(1)} all-to-all(bf16[4,8,8320]{2,1,0:T(8,128)(2,1)S(1)} %broadcast_in_dim.131), channel_id=1, replica_groups={{0,64,128,192},{1,65,129,193},{2,66,130,194},{3,67,131,195},{4,68,132,1..., dimensions={0} | all-to-all | bytes 1064960 | tf_op jit(solution)/shard_map/all_to_all | solution.py:26
  42.3 1.5 broadcast_in_dim.133
  43.8 4.5 %all-to-all-start.2 = ((bf16[4,32,8320]{2,1,0:T(8,128)(2,1)}), bf16[4,32,8320]{2,1,0:T(8,128)(2,1)S(1)}, u32[]{:S(2)}, u32[]{:S(2)}) async-start(bf16[4,32,8320]{2,1,0:T(8,128)(2,1)} %broadcast_in_dim.133), calls=%async_computation.2 | async-start | bytes 4259840 | tf_op jit(solution)/shard_map/all_to_all | solution.py:26
  48.3 16.7 %all-to-all-done.2 = bf16[4,32,8320]{2,1,0:T(8,128)(2,1)S(1)} async-done(((bf16[4,32,8320]{2,1,0:T(8,128)(2,1)}), bf16[4,32,8320]{2,1,0:T(8,128)(2,1)S(1)}, u32[]{:S(2)}, u32[]{:S(2)}) %all-to-all-start.2) | async-done | bytes 2129952 | tf_op jit(solution)/shard_map/all_to_all | solution.py:26
  65.0 0.2 fusion.34
  65.2 5.7 %fusion.36 = (f32[128]{0:T(128)S(1)}, f32[128,501]{0,1:T(8,128)S(1)}) fusion(bf16[501,8192]{1,0:T(8,128)(2,1)} %param.6, bf16[128,8320]{1,0:T(8,128)(2,1)S(1)} %bitcast.27), kind=kOutput, calls=%fused_computation.70 | convolution fusion | flops 1050737152 | bytes 10562560 | tf_op jit(solution)/shard_map/rd,vd->rv/dot_general | solution.py:60
  70.8 0.0 collective-permute-done
  70.9 5.7 %fusion.37 = (f32[128]{0:T(128)S(1)}, f32[128,501]{0,1:T(8,128)S(1)}) fusion(bf16[501,8192]{1,0:T(8,128)(2,1)} %collective-permute-done, bf16[128,8320]{1,0:T(8,128)(2,1)S(1)} %bitcast.28), kind=kOutput, calls=%fused_computation.71 | convolution fusion | flops 1050737152 | bytes 10562560 | tf_op jit(solution)/shard_map/rd,vd->rv/dot_general | solution.py:60
  76.5 0.2 exponential_reduce_fusion.1
  76.8 0.7 broadcast_in_dim.138
  77.5 6.9 %all-to-all-start.3 = ((f32[128,4,128]{2,1,0:T(4,128)}), f32[128,4,128]{2,1,0:T(4,128)S(1)}, u32[]{:S(2)}, u32[]{:S(2)}) async-start(f32[128,4,128]{2,1,0:T(4,128)} %broadcast_in_dim.138), calls=%async_computation.3 | async-start | bytes 524288 | tf_op jit(solution)/shard_map/all_to_all | solution.py:26
  84.4 0.2 compare_reduce_fusion
  84.6 11.6 %all-to-all-done.3 = f32[128,4,128]{2,1,0:T(4,128)S(1)} async-done(((f32[128,4,128]{2,1,0:T(4,128)}), f32[128,4,128]{2,1,0:T(4,128)S(1)}, u32[]{:S(2)}, u32[]{:S(2)}) %all-to-all-start.3) | async-done | bytes 262176 | tf_op jit(solution)/shard_map/all_to_all | solution.py:26
  96.2 0.1 fusion.35
  96.5 5.1 %fusion.15 = f32[128,8192]{1,0:T(8,128)S(1)} fusion(bf16[501,8192]{1,0:T(8,128)(2,1)} %param.6, f32[128,501]{0,1:T(8,128)S(1)} %get-tuple-element.16, f32[128]{0:T(128)S(1)} %get-tuple-element.9, s32[128]{0:T(128)S(1)} %fusion.34, s32[501]{0:T(512)S(1)} %iota_add_fusion.1, pred[128]{0:T(512)(128)(4,1)S(1)} %compare_reduce_fusion), kind=kOutput, calls=%fused_computation.28 | convolution fusion | flops 1051057920 | bytes 12662356 | tf_op jit(solution)/shard_map/dot_general | solution.py:75
  101.6 5.4 %fusion.1 = f16[128,8192]{1,0:T(8,128)(2,1)S(1)} fusion(f32[128,8192]{1,0:T(8,128)S(1)} %fusion.15, bf16[501,8192]{1,0:T(8,128)(2,1)} %collective-permute-done, f32[128,501]{0,1:T(8,128)S(1)} %get-tuple-element.18, f32[128]{0:T(128)S(1)} %get-tuple-element.9, s32[128]{0:T(128)S(1)} %fusion.34, s32[501]{0:T(512)S(1)} %iota_add_fusion, ...), kind=kOutput, calls=%fused_computation.2 | convolution fusion | flops 1054203648 | bytes 14759508 | tf_op jit(solution)/shard_map/dot_general | solution.py:75
  107.0 19.7 %all_to_all.37 = f16[4,32,8192]{2,1,0:T(8,128)(2,1)S(1)} all-to-all(f16[4,32,8192]{2,1,0:T(8,128)(2,1)S(1)} %bitcast.29), channel_id=1, replica_groups={{0,16,32,48},{1,17,33,49},{2,18,34,50},{3,19,35,51},{4,20,36,52},{5,21,..., dimensions={0} | all-to-all | bytes 4194304 | tf_op jit(solution)/shard_map/all_to_all | solution.py:26
  126.7 0.4 convert_reduce_fusion
  127.0 0.1 convert_bitcast_fusion
  127.1 10.9 %all_to_all.38 = f16[4,8,8192]{2,1,0:T(8,128)(2,1)S(1)} all-to-all(f16[4,8,8192]{2,1,0:T(8,128)(2,1)S(1)} %convert_bitcast_fusion), channel_id=1, replica_groups={{0,64,128,192},{1,65,129,193},{2,66,130,194},{3,67,131,195},{4,68,132,1..., dimensions={0} | all-to-all | bytes 1048576 | tf_op jit(solution)/shard_map/all_to_all | solution.py:26
  138.0 0.1 convert_reduce_fusion.1
  138.1 0.5 broadcast.124
  138.6 0.7 reduce.10
  139.3 0.7 reshape.153
  140.0 3.4 %all-to-all-start.6 = ((f16[8,2,4096]{2,1,0:T(2,128)(2,1)}), f16[8,2,4096]{2,1,0:T(2,128)(2,1)S(1)}, u32[]{:S(2)}, u32[]{:S(2)}) async-start(f16[8,2,4096]{2,1,0:T(2,128)(2,1)} %reshape.153), calls=%async_computation.6 | async-start | bytes 262144 | tf_op jit(solution)/shard_map/all_to_all | solution.py:26
  143.5 0.7 dynamic_slice.7
  144.2 1.2 broadcast_select_fusion.1
  145.4 7.1 %all-to-all-done.6 = f16[8,2,4096]{2,1,0:T(2,128)(2,1)S(1)} async-done(((f16[8,2,4096]{2,1,0:T(2,128)(2,1)}), f16[8,2,4096]{2,1,0:T(2,128)(2,1)S(1)}, u32[]{:S(2)}, u32[]{:S(2)}) %all-to-all-start.6) | async-done | bytes 131104 | tf_op jit(solution)/shard_map/all_to_all | solution.py:26
  152.4 0.1 reshape.154
  152.6 0.3 convert_reduce_fusion.2
  152.9 1.7 %select_convert_fusion = bf16[128,8192]{1,0:T(8,128)(2,1)} fusion(bf16[8192]{0:T(1024)(128)(2,1)S(1)} %broadcast_multiply_fusion, pred[128]{0:T(512)(128)(4,1)S(1)} %get-tuple-element.11), kind=kLoop, calls=%fused_computation.3 | loop fusion | flops 1048576 | bytes 2113664 | tf_op jit(solution)/shard_map/convert_element_type | solution.py:85
  (15 shorter events, 0.2 us)
Async XLA Ops:
  0.6 70.2 %collective-permute-start = (bf16[501,8192]{1,0:T(8,128)(2,1)}, bf16[501,8192]{1,0:T(8,128)(2,1)}, u32[]{:S(2)}, u32[]{:S(2)}) collective-permute-start(bf16[501,8192]{1,0:T(8,128)(2,1)} %param.6), channel_id=1, source_target_pairs={{0,8},{1,9},{2,10},{3,11},{4,12},{5,13},{6,14},{7,15},{8,0},{9,1},... | collective-permute-start | bytes 24625160 | tf_op jit(solution)/shard_map/ppermute | solution.py:38
  43.8 21.1 %all-to-all-start.2 = ((bf16[4,32,8320]{2,1,0:T(8,128)(2,1)}), bf16[4,32,8320]{2,1,0:T(8,128)(2,1)S(1)}, u32[]{:S(2)}, u32[]{:S(2)}) async-start(bf16[4,32,8320]{2,1,0:T(8,128)(2,1)} %broadcast_in_dim.133), calls=%async_computation.2 | async-start | bytes 4259840 | tf_op jit(solution)/shard_map/all_to_all | solution.py:26
  77.5 18.7 %all-to-all-start.3 = ((f32[128,4,128]{2,1,0:T(4,128)}), f32[128,4,128]{2,1,0:T(4,128)S(1)}, u32[]{:S(2)}, u32[]{:S(2)}) async-start(f32[128,4,128]{2,1,0:T(4,128)} %broadcast_in_dim.138), calls=%async_computation.3 | async-start | bytes 524288 | tf_op jit(solution)/shard_map/all_to_all | solution.py:26
  140.0 12.4 %all-to-all-start.6 = ((f16[8,2,4096]{2,1,0:T(2,128)(2,1)}), f16[8,2,4096]{2,1,0:T(2,128)(2,1)S(1)}, u32[]{:S(2)}, u32[]{:S(2)}) async-start(f16[8,2,4096]{2,1,0:T(2,128)(2,1)} %reshape.153), calls=%async_computation.6 | async-start | bytes 262144 | tf_op jit(solution)/shard_map/all_to_all | solution.py:26

commit v2 on v1

v2 whole, which is shorter than its diff:
```python
import functools

import jax
import jax.numpy as jnp
from jax import lax
from jax.experimental import pallas as pl
from jax.experimental.pallas import tpu as pltpu
from jax.sharding import Mesh, PartitionSpec as P

loss_scale = 128.0
send_scale = 32.0
send_type = jnp.float16
width = 8192
wide = width + 256
block = 1024
f32, bf16, i32 = jnp.float32, jnp.bfloat16, jnp.int32


def device(x, y, c, z):
    return ((x * 4 + y) * 2 + c) * 8 + z


R4, R8 = range(4), range(8)
places = [(x, y, c, z) for x in R4 for y in R4 for c in (0, 1) for z in R8]
along_z = [[device(x, y, c, z) for z in R8] for x in R4 for y in R4 for c in (0, 1)]
same_core = [[device(x, y, c, z) for x in R4 for y in R4 for z in R8] for c in (0, 1)]
partner = [(device(x, y, c, z), device(x, y, 1 - c, z)) for x, y, c, z in places]


def shift(value, outer, k):
    pairs = []
    for x, y, c, z in places:
        to = device(x, (y + k) % 4, c, z) if outer == (c == 0) else device((x + k) % 4, y, c, z)
        pairs.append((device(x, y, c, z), to))
    return lax.ppermute(value, "d", pairs)


def vmem(*args):
    return pl.BlockSpec(*args) if args else pl.BlockSpec(memory_space=pltpu.VMEM)


smem = pl.BlockSpec(memory_space=pltpu.SMEM)
anywhere = pl.BlockSpec(memory_space=pl.ANY)


def pack_kernel(count_ref, mask_ref, target_ref, hidden_ref, row_ref, kept_ref, slab, sem):
    lane = lax.broadcasted_iota(i32, (1, 128), 1)
    first = jnp.min(jnp.where(mask_ref[...] == 1, lane, 127).astype(f32)).astype(i32)
    copy = pltpu.make_async_copy(hidden_ref.at[pl.ds(pl.multiple_of(first // 8 * 8, 8), 8)], slab, sem)
    copy.start()
    kept = (lane == first) & (mask_ref[...] == 1) & (count_ref[0] > 0)
    kept_ref[...] = kept.astype(i32)
    code = jnp.sum(jnp.where(kept, target_ref[...] + 1, 0).astype(f32)).astype(i32)
    wide_lane = lax.broadcasted_iota(i32, (1, 256), 1)
    digits = jnp.where(wide_lane == 0, code % 256, 0) + jnp.where(wide_lane == 1, code // 256 % 256, 0)
    digits = digits + jnp.where(wide_lane == 2, code // 65536, 0)
    copy.wait()
    take = (lax.broadcasted_iota(i32, (8, width), 0) == first % 8) & (code > 0)
    row = jnp.sum(jnp.where(take, slab[...].astype(f32), 0.0), axis=0, keepdims=True)
    half = wide // 2
    low, high = row[:, :half], jnp.concatenate([row[:, half:], digits.astype(f32)], axis=1)
    both = jnp.where(lax.broadcasted_iota(i32, (2, half), 0) == 0, low, high).astype(bf16)
    row_ref[...] = jnp.broadcast_to(both[None], row_ref.shape)


def pack(count, mask, target, hidden):
    return pl.pallas_call(
        pack_kernel,
        in_specs=[smem, vmem(), vmem(), anywhere],
        out_specs=[vmem(), vmem()],
        out_shape=[jax.ShapeDtypeStruct((8, 2, wide // 2), bf16), jax.ShapeDtypeStruct((1, 128), i32)],
        scratch_shapes=[pltpu.VMEM((8, width), bf16), pltpu.SemaphoreType.DMA],
        name="pack",
    )(count, mask.reshape(1, 128), target.reshape(1, 128), hidden)


def by_rank(values, i, j):
    values = pltpu.roll(values, j * 32, 1)
    lane = lax.broadcasted_iota(i32, values.shape, 1)
    return jnp.where(lane % 32 >= i * 8, pltpu.roll(values, i * 8, 1), pltpu.roll(values, (i * 8 + 96) % 128, 1))


def by_arrival(values, i, j):
    lane = lax.broadcasted_iota(i32, values.shape, 1)
    back, around = pltpu.roll(values, (128 - i * 8) % 128, 1), pltpu.roll(values, 32 - i * 8, 1)
    return pltpu.roll(jnp.where(lane % 32 < 32 - i * 8, back, around), (128 - j * 32) % 128, 1)


def logits_kernel(vocab_rows, place_ref, r0, r1, r2, r3, digits_ref, w_ref, v_ref, own_ref, other_ref, stats_ref):
    step = pl.program_id(0)
    rows = jnp.concatenate([r0[...], r1[...], r2[...], r3[...]], axis=0)

    @pl.when(step == 0)
    def _():
        own_ref[...] = jnp.zeros_like(own_ref)
        other_ref[...] = jnp.zeros_like(other_ref)

    for out, weight in ((own_ref, w_ref), (other_ref, v_ref)):
        out[...] += lax.dot_general(weight[...], rows, (((1,), (1,)), ((), ())), preferred_element_type=f32)

    @pl.when(step == pl.num_programs(0) - 1)
    def _():
        i, j, me = place_ref[0], place_ref[1], place_ref[2]
        digits = digits_ref[...]
        target = digits[0:1] + 256 * digits[1:2] + 65536 * digits[2:3] - 1
        top = jnp.maximum(jnp.max(own_ref[...], axis=0, keepdims=True), jnp.max(other_ref[...], axis=0, keepdims=True))
        total, pick = 0.0, 0.0
        for out, base in ((own_ref, me), (other_ref, me ^ 8)):
            ids = lax.broadcasted_iota(i32, (vocab_rows, 128), 0) + base * vocab_rows
            total += jnp.sum(jnp.exp(out[...] - top), axis=0, keepdims=True)
            pick += jnp.sum(jnp.where(ids == target, out[...], 0.0), axis=0, keepdims=True)
        row = lax.broadcasted_iota(i32, (4, 128), 0)
        stats = jnp.where(row == 0, top, jnp.where(row == 1, total, jnp.where(row == 2, pick, target.astype(f32))))
        stats_ref[...] = jnp.broadcast_to(by_rank(stats, i, j)[None], stats_ref.shape)


def logits_call(place, rows, digits, own, other):
    vocab_rows = own.shape[0]
    part = pl.BlockSpec((32, block), lambda k: (0, k))
    weight = pl.BlockSpec((vocab_rows, block), lambda k: (0, k))
    logits = pl.BlockSpec((vocab_rows, 128), lambda k: (0, 0))
    return pl.pallas_call(
        functools.partial(logits_kernel, vocab_rows),
        grid=(width // block,),
        in_specs=[smem, part, part, part, part, pl.BlockSpec((4, 128), lambda k: (0, 0)), weight, weight],
        out_specs=[logits, logits, pl.BlockSpec((128, 4, 128), lambda k: (0, 0, 0))],
        out_shape=[jax.ShapeDtypeStruct((vocab_rows, 128), f32)] * 2 + [jax.ShapeDtypeStruct((128, 4, 128), f32)],
        name="logits",
    )(place, *rows, digits, own, other)


def grad_kernel(vocab_rows, place_ref, stats_ref, own_ref, other_ref, w_ref, v_ref, g0, g1, g2, g3, loss_ref, coefs):
    step = pl.program_id(0)

    @pl.when(step == 0)
    def _():
        i, j, me = place_ref[0], place_ref[1], place_ref[2]
        top = jnp.max(stats_ref[:, 0, :], axis=0, keepdims=True)
        total = jnp.sum(stats_ref[:, 1, :] * jnp.exp(stats_ref[:, 0, :] - top), axis=0, keepdims=True)
        picked = jnp.sum(stats_ref[:, 2, :], axis=0, keepdims=True)
        target = stats_ref[0, 3:4, :]
        log_total = top + jnp.log(total)
        loss_ref[...] = jnp.where(target >= 0, log_total - picked, 0.0)
        row = lax.broadcasted_iota(i32, (8, 128), 0)
        both = by_arrival(jnp.where(row == 0, log_total, target), i, j)
        log_total, target = both[0:1], both[1:2].astype(i32)
        for slot, (out, base) in enumerate(((own_ref, me), (other_ref, me ^ 8))):
            ids = lax.broadcasted_iota(i32, (vocab_rows, 128), 0) + base * vocab_rows
            hit = (ids == target).astype(f32)
            coefs[slot] = jnp.where(target >= 0, jnp.exp(out[...] - log_total) - hit, 0.0).T.astype(bf16)

    grad = jnp.dot(coefs[0], w_ref[...], preferred_element_type=f32)
    grad += jnp.dot(coefs[1], v_ref[...], preferred_element_type=f32)
    grad = grad * (loss_scale * send_scale)
    for k, out in enumerate((g0, g1, g2, g3)):
        out[...] = grad[k * 32:(k + 1) * 32].astype(out.dtype)


def grad_call(place, stats, logits, own, other, out_type):
    vocab_rows = own.shape[0]
    part = pl.BlockSpec((32, block), lambda k: (0, k))
    weight = pl.BlockSpec((vocab_rows, block), lambda k: (0, k))
    held = pl.BlockSpec((vocab_rows, 128), lambda k: (0, 0))
    return pl.pallas_call(
        functools.partial(grad_kernel, vocab_rows),
        grid=(width // block,),
        in_specs=[smem, pl.BlockSpec((128, 4, 128), lambda k: (0, 0, 0)), held, held, weight, weight],
        out_specs=[part] * 4 + [pl.BlockSpec((1, 128), lambda k: (0, 0))],
        out_shape=[jax.ShapeDtypeStruct((32, width), out_type)] * 4 + [jax.ShapeDtypeStruct((1, 128), f32)],
        scratch_shapes=[pltpu.VMEM((2, 128, vocab_rows), bf16)],
        name="grad",
    )(place, stats, *logits, own, other)


def exchange(value, groups):
    return lax.all_to_all(value, "d", 0, 0, axis_index_groups=groups)


def gather4(value, outer):
    far, back, on = shift(value, outer, 2), shift(value, outer, 1), shift(value, outer, 3)
    return [value, on, far, back]


def reduce4(blocks, outer):
    far, on, back = shift(blocks[2], outer, 2), shift(blocks[1], outer, 1), shift(blocks[3], outer, 3)
    return (blocks[0].astype(f32) + on.astype(f32)) + (far.astype(f32) + back.astype(f32))


def shards(hidden, out_weight, loss_mask, targets, kept_count):
    me = lax.axis_index("d")
    z, c, y, x = me % 8, (me // 8) % 2, (me // 16) % 4, me // 64
    i, j = jnp.where(c == 0, x, y), jnp.where(c == 0, y, x)
    place = jnp.stack([i, j, me])
    other_weight = lax.ppermute(out_weight, "d", partner)

    packed, kept = pack(kept_count, loss_mask, targets, hidden)
    rows = exchange(packed, along_z).reshape(8, wide)
    rows = jnp.concatenate(gather4(rows, False), axis=0)
    rows = gather4(rows, True)
    digits = jnp.concatenate([r[:, width:width + 4] for r in rows], axis=0).T.astype(i32)
    *logits, stats = logits_call(place, rows, digits, out_weight, other_weight)
    stats = exchange(stats, same_core)
    *parts, loss = grad_call(place, stats, logits, out_weight, other_weight, OUT)
    part = reduce4([p.astype(send_type) for p in parts], True)
    part = part.astype(send_type)
    part = reduce4([part[k * 8:(k + 1) * 8] for k in R4], False)
    part = exchange(part.astype(send_type).reshape(8, 1, width), along_z)
    own_grad = jnp.sum(part.astype(f32), axis=0) * (1.0 / send_scale)

    own_loss = lax.dynamic_slice_in_dim(loss[0], (j * 4 + i) * 8 + z, 1, 0)
    kept_row = kept[0] > 0
    hidden_grad = jnp.where(kept_row[:, None], own_grad, 0.0).astype(bf16)
    row_loss = jnp.where(kept_row, own_loss, 0.0)
    return hidden_grad, row_loss


OUT = jnp.float32


def solution(mesh):
    flat = Mesh(mesh.devices.reshape(-1), ("d",))
    rows = P("d", None)
    vector = P("d")
    return jax.shard_map(
        shards, mesh=flat, in_specs=(rows, rows, vector, vector, vector), out_specs=(rows, vector), check_vma=False
    )
```

time: 155 us -> 143 us (0.923)
  Pallas kernels: 0 us -> 25.9 us
  matrix products: 21.8 us -> 0 us
  blocking collectives: 60 us -> 38.2 us
  waiting for transfers between devices: 35.4 us -> 45.7 us
  starting transfers between devices: 14.8 us -> 20.1 us
  between operations: 6.35 us -> 1.52 us
  local copies, waits for them, and re-layouts: 5.45 us -> 2.65 us
  other arithmetic: 10.8 us -> 8.29 us
    ppermute x0 -> x12, waiting for transfers between devices: none -> 38.5 us  [shift(): return lax.ppermute(value, 'd', pairs)]
    all_to_all x3 -> x1, waiting for transfers between devices: 35.4 us -> 7.2 us  [exchange(): return lax.all_to_all(value, 'd', 0, 0, axis_index_groups=groups)]
    pallas_call x0 -> x3, Pallas kernels: none -> 25.9 us  [the longest x1 12.1 us: logits_call(): pl.pallas_call(functools.partial(logits_kernel, vocab_rows), grid=(width...]
    dot_general x4 -> x0, matrix products: 21.8 us -> none  [the longest x2 11.3 us: shards(): jnp.einsum('rd,vd->rv', gathered, w, preferred_element_type=jnp.float32)]
    all_to_all x4 -> x2, blocking collectives: 60 us -> 38.2 us  [exchange(): return lax.all_to_all(value, 'd', 0, 0, axis_index_groups=groups)]
    ppermute x0 -> x12, starting transfers between devices: none -> 16.6 us  [shift(): return lax.ppermute(value, 'd', pairs)]
    all_to_all x3 -> x1, starting transfers between devices: 14.7 us -> 3.37 us  [exchange(): return lax.all_to_all(value, 'd', 0, 0, axis_index_groups=groups)]
    convert_element_type x6, other arithmetic: 2.43 us -> 5.4 us  [the longest x3 2.76 us: shards(): part = reduce4([p.astype(send_type) for p in parts], True)]
  transfers between devices with their start and end apart: 4 -> 14, of which waited for: 3 -> 9; matrix products, arithmetic and copies ran while one was open for 10% -> 2% of each run, Pallas kernels for 0% -> 2%
where the time goes in v2:
time: 143 us; the launch traced here: 142 us
  waiting for transfers between devices  45.7 us (32%)
  blocking collectives  38.2 us (27%)
  Pallas kernels  25.9 us (18%)
  starting transfers between devices  20.1 us (14%)
  other arithmetic  8.29 us (6%)
  local copies, waits for them, and re-layouts  2.65 us (2%)
  between operations  1.52 us (1%)
    ppermute x12, waiting for transfers between devices, shift(): return lax.ppermute(value, 'd', pairs)  38.5 us
    all_to_all x2, blocking collectives, exchange(): return lax.all_to_all(value, 'd', 0, 0, axis_index_groups=groups)  38.2 us
    ppermute x12, starting transfers between devices, shift(): return lax.ppermute(value, 'd', pairs)  16.6 us
    pallas_call x1, Pallas kernels, logits_call(): pl.pallas_call(functools.partial(logits_kernel, vocab_rows), grid=(width...  12.1 us
    pallas_call x1, Pallas kernels, grad_call(): pl.pallas_call(functools.partial(grad_kernel, vocab_rows), grid=(width //...  11.3 us
    all_to_all x1, waiting for transfers between devices, exchange(): return lax.all_to_all(value, 'd', 0, 0, axis_index_groups=groups)  7.2 us
    all_to_all x1, starting transfers between devices, exchange(): return lax.all_to_all(value, 'd', 0, 0, axis_index_groups=groups)  3.37 us
  transfers between devices with their start and end apart: 14, of which 9 were waited for; matrix products, arithmetic and copies ran while one was open for 2% of the time, Pallas kernels for 2%

profile of v2, /device:TPU:2, one launch (start us, length us, event | category | flops | bytes accessed | tf_op | source)
XLA Modules:
  0.0 142.3 jit_solution(8157902197225868270)
XLA Ops:
  0.6 0.1 collective-permute-start.6
  1.4 2.5 %pack.1 = (bf16[8,2,4224]{2,1,0:T(2,128)(2,1)}, s32[1,128]{1,0:T(1,128)}) custom-call(s32[1]{0:T(128)S(6)} %copy.26.count_ref, s32[1,128]{1,0:T(1,128)} %bitcast.21, s32[1,128]{1,0:T(1,128)} %bitcast.22, bf16[128,8192]{1,0:T(8,128)(2,1)} %hidden_ref.1), custom_call_target="tpu_custom_call" | custom-call | tf_op jit(solution)/shard_map/pack/pallas_call | solution.py:67
  3.9 18.3 %all_to_all.15 = bf16[8,2,4224]{2,1,0:T(2,128)(2,1)S(1)} all-to-all(bf16[8,2,4224]{2,1,0:T(2,128)(2,1)} %get-tuple-element.13), channel_id=1, replica_groups={{0,1,2,3,4,5,6,7},{8,9,10,11,12,13,14,15},{16,17,18,19,20,21,22,23},{24..., dimensions={0} | all-to-all | bytes 270336 | tf_op jit(solution)/shard_map/all_to_all | solution.py:176
  22.2 1.6 %collective-permute-start.2 = (bf16[8,8448]{1,0:T(8,128)(2,1)S(1)}, bf16[8,8448]{1,0:T(8,128)(2,1)S(1)}, u32[]{:S(2)}, u32[]{:S(2)}) collective-permute-start(bf16[8,8448]{1,0:T(8,128)(2,1)S(1)} %bitcast.16), channel_id=1, source_target_pairs={{0,64},{1,65},{2,66},{3,67},{4,68},{5,69},{6,70},{7,71},{8,24},{9,... | collective-permute-start | bytes 405512 | tf_op jit(solution)/shard_map/ppermute | solution.py:35
  23.7 1.1 collective-permute-start.1
  24.8 2.2 %collective-permute-start = (bf16[8,8448]{1,0:T(8,128)(2,1)S(1)}, bf16[8,8448]{1,0:T(8,128)(2,1)S(1)}, u32[]{:S(2)}, u32[]{:S(2)}) collective-permute-start(bf16[8,8448]{1,0:T(8,128)(2,1)S(1)} %bitcast.18), channel_id=1, source_target_pairs={{0,192},{1,193},{2,194},{3,195},{4,196},{5,197},{6,198},{7,199},{8... | collective-permute-start | bytes 405512 | tf_op jit(solution)/shard_map/ppermute | solution.py:35
  27.0 4.3 %collective-permute-done = bf16[8,8448]{1,0:T(8,128)(2,1)S(1)} collective-permute-done((bf16[8,8448]{1,0:T(8,128)(2,1)S(1)}, bf16[8,8448]{1,0:T(8,128)(2,1)S(1)}, u32[]{:S(2)}, u32[]{:S(2)}) %collective-permute-start) | collective-permute-done | bytes 135200 | tf_op jit(solution)/shard_map/ppermute | solution.py:35
  31.3 0.0 collective-permute-done.1
  31.4 0.0 collective-permute-done.2
  31.4 0.0 copy-start.2
  31.4 1.7 %collective-permute-start.5 = (bf16[32,8448]{1,0:T(8,128)(2,1)S(1)}, bf16[32,8448]{1,0:T(8,128)(2,1)S(1)}, u32[]{:S(2)}, u32[]{:S(2)}) collective-permute-start(bf16[32,8448]{1,0:T(8,128)(2,1)S(1)} %constant_dynamic-update-slice_fusion.r0), channel_id=1, source_target_pairs={{0,16},{1,17},{2,18},{3,19},{4,20},{5,21},{6,22},{7,23},{8,72},{9,... | collective-permute-start | bytes 1622024 | tf_op jit(solution)/shard_map/ppermute | solution.py:35
  33.0 2.9 %collective-permute-start.4 = (bf16[32,8448]{1,0:T(8,128)(2,1)S(1)}, bf16[32,8448]{1,0:T(8,128)(2,1)S(1)}, u32[]{:S(2)}, u32[]{:S(2)}) collective-permute-start(bf16[32,8448]{1,0:T(8,128)(2,1)S(1)} %constant_dynamic-update-slice_fusion.r0), channel_id=1, source_target_pairs={{0,32},{1,33},{2,34},{3,35},{4,36},{5,37},{6,38},{7,39},{8,136},{9... | collective-permute-start | bytes 1622024 | tf_op jit(solution)/shard_map/ppermute | solution.py:35
  35.9 1.3 collective-permute-start.3
  37.3 0.7 pad_add_fusion.place_ref
  38.0 0.1 copy.17
  38.0 4.0 %collective-permute-done.5.r3 = bf16[32,8448]{1,0:T(8,128)(2,1)S(1)} collective-permute-done((bf16[32,8448]{1,0:T(8,128)(2,1)S(1)}, bf16[32,8448]{1,0:T(8,128)(2,1)S(1)}, u32[]{:S(2)}, u32[]{:S(2)}) %collective-permute-start.5) | collective-permute-done | bytes 540704 | tf_op jit(solution)/shard_map/ppermute | solution.py:35
  42.0 0.0 copy-start.3
  42.0 0.1 copy.20
  42.1 6.9 %collective-permute-done.4.r2 = bf16[32,8448]{1,0:T(8,128)(2,1)S(1)} collective-permute-done((bf16[32,8448]{1,0:T(8,128)(2,1)S(1)}, bf16[32,8448]{1,0:T(8,128)(2,1)S(1)}, u32[]{:S(2)}, u32[]{:S(2)}) %collective-permute-start.4) | collective-permute-done | bytes 540704 | tf_op jit(solution)/shard_map/ppermute | solution.py:35
  49.1 0.1 copy.19
  49.2 0.0 collective-permute-done.3.r1
  49.2 0.1 copy.18
  49.3 0.7 convert_bitcast_fusion.digits_ref
  50.0 0.0 collective-permute-done.6.v_ref
  50.0 0.0 copy-done.2
  50.0 0.0 copy-done.3
  50.0 0.0 copy-done.4
  50.0 0.1 copy-done.5
  50.1 12.1 %logits.1 = (f32[501,128]{1,0:T(8,128)}, f32[501,128]{1,0:T(8,128)}, f32[128,4,128]{2,1,0:T(4,128)}) custom-call(s32[3]{0:T(128)} %pad_add_fusion.place_ref, bf16[32,8448]{1,0:T(8,128)(2,1)} %copy-done.2, bf16[32,8448]{1,0:T(8,128)(2,1)} %copy-done.5, bf16[32,8448]{1,0:T(8,128)(2,1)} %copy-done.4, bf16[32,8448]{1,0:T(8,128)(2,1)} %copy-done.3, ...), custom_call_target="tpu_custom_call" | custom-call | tf_op jit(solution)/shard_map/logits/pallas_call | solution.py:122
  62.2 19.9 %all_to_all.16.stats_ref = f32[128,4,128]{2,1,0:T(4,128)} all-to-all(f32[128,4,128]{2,1,0:T(4,128)} %get-tuple-element.14), channel_id=1, replica_groups={{0,1,2,3,4,5,6,7,16,17,18,19,20,21,22,23,32,33,34,35,36,37,38,39,48,49,..., dimensions={0} | all-to-all | bytes 524288 | tf_op jit(solution)/shard_map/all_to_all | solution.py:176
  82.2 11.3 %grad.1 = (f32[32,8192]{1,0:T(8,128)}, f32[32,8192]{1,0:T(8,128)}, f32[32,8192]{1,0:T(8,128)}, f32[32,8192]{1,0:T(8,128)}, f32[1,128]{1,0:T(1,128)}) custom-call(s32[3]{0:T(128)} %pad_add_fusion.place_ref, f32[128,4,128]{2,1,0:T(4,128)} %all_to_all.16.stats_ref, f32[501,128]{1,0:T(8,128)} %get-tuple-element.15.own_ref, ...), custom_call_target="tpu_custom_call" | custom-call | tf_op jit(solution)/shard_map/grad/pallas_call | solution.py:164
  93.5 0.0 copy-start
  93.5 1.4 %convert_element_type.57 = f16[32,8192]{1,0:T(8,128)(2,1)S(1)} convert(f32[32,8192]{1,0:T(8,128)} %get-tuple-element.18) | non-fusion elementwise | flops 262144 | bytes 1572864 | tf_op jit(solution)/shard_map/convert_element_type | solution.py:204
  94.9 1.3 convert_element_type.59
  96.2 0.0 copy-done.1
  96.2 0.1 convert_element_type.61
  96.3 2.0 %collective-permute-start.9 = (f16[32,8192]{1,0:T(8,128)(2,1)S(1)}, f16[32,8192]{1,0:T(8,128)(2,1)S(1)}, u32[]{:S(2)}, u32[]{:S(2)}) collective-permute-start(f16[32,8192]{1,0:T(8,128)(2,1)S(1)} %convert_element_type.61), channel_id=1, source_target_pairs={{0,48},{1,49},{2,50},{3,51},{4,52},{5,53},{6,54},{7,55},{8,200},{9... | collective-permute-start | bytes 1572872 | tf_op jit(solution)/shard_map/ppermute | solution.py:35
  98.2 1.0 collective-permute-start.8
  99.3 0.6 collective-permute-start.7
  99.9 10.7 %collective-permute-done.9 = f16[32,8192]{1,0:T(8,128)(2,1)S(1)} collective-permute-done((f16[32,8192]{1,0:T(8,128)(2,1)S(1)}, f16[32,8192]{1,0:T(8,128)(2,1)S(1)}, u32[]{:S(2)}, u32[]{:S(2)}) %collective-permute-start.9) | collective-permute-done | bytes 524320 | tf_op jit(solution)/shard_map/ppermute | solution.py:35
  110.6 0.0 collective-permute-done.8
  110.6 6.1 %collective-permute-done.7 = f16[32,8192]{1,0:T(8,128)(2,1)S(1)} collective-permute-done((f16[32,8192]{1,0:T(8,128)(2,1)S(1)}, f16[32,8192]{1,0:T(8,128)(2,1)S(1)}, u32[]{:S(2)}, u32[]{:S(2)}) %collective-permute-start.7) | collective-permute-done | bytes 524320 | tf_op jit(solution)/shard_map/ppermute | solution.py:35
  116.7 0.0 copy-done
  116.7 0.3 add_convert_fusion
  116.9 0.1 fusion.1
  117.0 0.3 collective-permute-start.10
  117.3 2.0 %collective-permute-start.12 = (f16[8,8192]{1,0:T(8,128)(2,1)S(1)}, f16[8,8192]{1,0:T(8,128)(2,1)S(1)}, u32[]{:S(2)}, u32[]{:S(2)}) collective-permute-start(f16[8,8192]{1,0:T(8,128)(2,1)S(1)} %get-tuple-element.23), channel_id=1, source_target_pairs={{0,192},{1,193},{2,194},{3,195},{4,196},{5,197},{6,198},{7,199},{8... | collective-permute-start | bytes 393224 | tf_op jit(solution)/shard_map/ppermute | solution.py:35
  119.3 0.0 collective-permute-start.11
  119.3 2.9 %collective-permute-done.10 = f16[8,8192]{1,0:T(8,128)(2,1)S(1)} collective-permute-done((f16[8,8192]{1,0:T(8,128)(2,1)S(1)}, f16[8,8192]{1,0:T(8,128)(2,1)S(1)}, u32[]{:S(2)}, u32[]{:S(2)}) %collective-permute-start.10) | collective-permute-done | bytes 131104 | tf_op jit(solution)/shard_map/ppermute | solution.py:35
  122.2 0.1 collective-permute-done.12
  122.3 3.4 %collective-permute-done.11 = f16[8,8192]{1,0:T(8,128)(2,1)S(1)} collective-permute-done((f16[8,8192]{1,0:T(8,128)(2,1)S(1)}, f16[8,8192]{1,0:T(8,128)(2,1)S(1)}, u32[]{:S(2)}, u32[]{:S(2)}) %collective-permute-start.11) | collective-permute-done | bytes 131104 | tf_op jit(solution)/shard_map/ppermute | solution.py:35
  125.8 0.1 fusion
  125.8 0.5 broadcast.17
  126.4 0.7 reduce.1
  127.1 0.7 reshape.34
  127.8 3.4 %all-to-all-start.2 = ((f16[8,2,4096]{2,1,0:T(2,128)(2,1)}), f16[8,2,4096]{2,1,0:T(2,128)(2,1)S(1)}, u32[]{:S(2)}, u32[]{:S(2)}) async-start(f16[8,2,4096]{2,1,0:T(2,128)(2,1)} %reshape.34), calls=%async_computation.2 | async-start | bytes 262144 | tf_op jit(solution)/shard_map/all_to_all | solution.py:176
  131.2 0.0 copy-done.6
  131.2 0.0 copy-done.7
  131.2 0.6 constant_dynamic-slice_fusion
  131.8 1.1 broadcast_select_fusion
  133.0 7.2 %all-to-all-done.2 = f16[8,2,4096]{2,1,0:T(2,128)(2,1)S(1)} async-done(((f16[8,2,4096]{2,1,0:T(2,128)(2,1)}), f16[8,2,4096]{2,1,0:T(2,128)(2,1)S(1)}, u32[]{:S(2)}, u32[]{:S(2)}) %all-to-all-start.2) | async-done | bytes 131104 | tf_op jit(solution)/shard_map/all_to_all | solution.py:176
  140.2 0.1 reshape.35
  140.3 0.3 convert_reduce_fusion
  140.7 1.7 %select_convert_fusion = bf16[128,8192]{1,0:T(8,128)(2,1)} fusion(bf16[8192]{0:T(1024)(128)(2,1)S(1)} %broadcast_multiply_fusion, pred[128]{0:T(512)(128)(4,1)S(1)} %compare_bitcast_fusion), kind=kLoop, calls=%fused_computation | loop fusion | flops 1048576 | bytes 2113664 | tf_op jit(solution)/shard_map/convert_element_type | solution.py:212
  (16 shorter events, 0.1 us)
Async XLA Ops:
  0.6 49.4 %collective-permute-start.6 = (bf16[501,8192]{1,0:T(8,128)(2,1)}, bf16[501,8192]{1,0:T(8,128)(2,1)}, u32[]{:S(2)}, u32[]{:S(2)}) collective-permute-start(bf16[501,8192]{1,0:T(8,128)(2,1)} %w_ref.3), channel_id=1, source_target_pairs={{0,8},{1,9},{2,10},{3,11},{4,12},{5,13},{6,14},{7,15},{8,0},{9,1},... | collective-permute-start | bytes 24625160 | tf_op jit(solution)/shard_map/ppermute | solution.py:194
  22.2 9.2 %collective-permute-start.2 = (bf16[8,8448]{1,0:T(8,128)(2,1)S(1)}, bf16[8,8448]{1,0:T(8,128)(2,1)S(1)}, u32[]{:S(2)}, u32[]{:S(2)}) collective-permute-start(bf16[8,8448]{1,0:T(8,128)(2,1)S(1)} %bitcast.16), channel_id=1, source_target_pairs={{0,64},{1,65},{2,66},{3,67},{4,68},{5,69},{6,70},{7,71},{8,24},{9,... | collective-permute-start | bytes 405512 | tf_op jit(solution)/shard_map/ppermute | solution.py:35
  23.7 7.6 %collective-permute-start.1 = (bf16[8,8448]{1,0:T(8,128)(2,1)S(1)}, bf16[8,8448]{1,0:T(8,128)(2,1)S(1)}, u32[]{:S(2)}, u32[]{:S(2)}) collective-permute-start(bf16[8,8448]{1,0:T(8,128)(2,1)S(1)} %bitcast.17), channel_id=1, source_target_pairs={{0,128},{1,129},{2,130},{3,131},{4,132},{5,133},{6,134},{7,135},{8... | collective-permute-start | bytes 405512 | tf_op jit(solution)/shard_map/ppermute | solution.py:35
  24.8 6.5 %collective-permute-start = (bf16[8,8448]{1,0:T(8,128)(2,1)S(1)}, bf16[8,8448]{1,0:T(8,128)(2,1)S(1)}, u32[]{:S(2)}, u32[]{:S(2)}) collective-permute-start(bf16[8,8448]{1,0:T(8,128)(2,1)S(1)} %bitcast.18), channel_id=1, source_target_pairs={{0,192},{1,193},{2,194},{3,195},{4,196},{5,197},{6,198},{7,199},{8... | collective-permute-start | bytes 405512 | tf_op jit(solution)/shard_map/ppermute | solution.py:35
  31.4 18.6 %copy-start.2 = (bf16[32,8448]{1,0:T(8,128)(2,1)}, bf16[32,8448]{1,0:T(8,128)(2,1)S(1)}, u32[]{:S(2)}) copy-start(bf16[32,8448]{1,0:T(8,128)(2,1)S(1)} %constant_dynamic-update-slice_fusion.r0) | copy-start | bytes 1622020
  31.4 10.6 %collective-permute-start.5 = (bf16[32,8448]{1,0:T(8,128)(2,1)S(1)}, bf16[32,8448]{1,0:T(8,128)(2,1)S(1)}, u32[]{:S(2)}, u32[]{:S(2)}) collective-permute-start(bf16[32,8448]{1,0:T(8,128)(2,1)S(1)} %constant_dynamic-update-slice_fusion.r0), channel_id=1, source_target_pairs={{0,16},{1,17},{2,18},{3,19},{4,20},{5,21},{6,22},{7,23},{8,72},{9,... | collective-permute-start | bytes 1622024 | tf_op jit(solution)/shard_map/ppermute | solution.py:35
  33.0 16.0 %collective-permute-start.4 = (bf16[32,8448]{1,0:T(8,128)(2,1)S(1)}, bf16[32,8448]{1,0:T(8,128)(2,1)S(1)}, u32[]{:S(2)}, u32[]{:S(2)}) collective-permute-start(bf16[32,8448]{1,0:T(8,128)(2,1)S(1)} %constant_dynamic-update-slice_fusion.r0), channel_id=1, source_target_pairs={{0,32},{1,33},{2,34},{3,35},{4,36},{5,37},{6,38},{7,39},{8,136},{9... | collective-permute-start | bytes 1622024 | tf_op jit(solution)/shard_map/ppermute | solution.py:35
  35.9 13.2 %collective-permute-start.3 = (bf16[32,8448]{1,0:T(8,128)(2,1)S(1)}, bf16[32,8448]{1,0:T(8,128)(2,1)S(1)}, u32[]{:S(2)}, u32[]{:S(2)}) collective-permute-start(bf16[32,8448]{1,0:T(8,128)(2,1)S(1)} %constant_dynamic-update-slice_fusion.r0), channel_id=1, source_target_pairs={{0,48},{1,49},{2,50},{3,51},{4,52},{5,53},{6,54},{7,55},{8,200},{9... | collective-permute-start | bytes 1622024 | tf_op jit(solution)/shard_map/ppermute | solution.py:35
  42.0 8.0 %copy-start.3 = (bf16[32,8448]{1,0:T(8,128)(2,1)}, bf16[32,8448]{1,0:T(8,128)(2,1)S(1)}, u32[]{:S(2)}) copy-start(bf16[32,8448]{1,0:T(8,128)(2,1)S(1)} %collective-permute-done.5.r3) | copy-start | bytes 1622020
  49.1 0.9 copy-start.4
  49.2 0.9 copy-start.5
  93.5 2.7 %copy-start.1 = (f32[32,8192]{1,0:T(8,128)S(1)}, f32[32,8192]{1,0:T(8,128)}, u32[]{:S(2)}) copy-start(f32[32,8192]{1,0:T(8,128)} %get-tuple-element.20) | copy-start | bytes 3145732
  93.5 23.2 %copy-start = (f32[32,8192]{1,0:T(8,128)S(1)}, f32[32,8192]{1,0:T(8,128)}, u32[]{:S(2)}) copy-start(f32[32,8192]{1,0:T(8,128)} %get-tuple-element.17) | copy-start | bytes 3145732
  96.3 14.3 %collective-permute-start.9 = (f16[32,8192]{1,0:T(8,128)(2,1)S(1)}, f16[32,8192]{1,0:T(8,128)(2,1)S(1)}, u32[]{:S(2)}, u32[]{:S(2)}) collective-permute-start(f16[32,8192]{1,0:T(8,128)(2,1)S(1)} %convert_element_type.61), channel_id=1, source_target_pairs={{0,48},{1,49},{2,50},{3,51},{4,52},{5,53},{6,54},{7,55},{8,200},{9... | collective-permute-start | bytes 1572872 | tf_op jit(solution)/shard_map/ppermute | solution.py:35
  98.2 12.4 %collective-permute-start.8 = (f16[32,8192]{1,0:T(8,128)(2,1)S(1)}, f16[32,8192]{1,0:T(8,128)(2,1)S(1)}, u32[]{:S(2)}, u32[]{:S(2)}) collective-permute-start(f16[32,8192]{1,0:T(8,128)(2,1)S(1)} %convert_element_type.59), channel_id=1, source_target_pairs={{0,32},{1,33},{2,34},{3,35},{4,36},{5,37},{6,38},{7,39},{8,136},{9... | collective-permute-start | bytes 1572872 | tf_op jit(solution)/shard_map/ppermute | solution.py:35
  99.3 17.4 %collective-permute-start.7 = (f16[32,8192]{1,0:T(8,128)(2,1)S(1)}, f16[32,8192]{1,0:T(8,128)(2,1)S(1)}, u32[]{:S(2)}, u32[]{:S(2)}) collective-permute-start(f16[32,8192]{1,0:T(8,128)(2,1)S(1)} %convert_element_type.57), channel_id=1, source_target_pairs={{0,16},{1,17},{2,18},{3,19},{4,20},{5,21},{6,22},{7,23},{8,72},{9,... | collective-permute-start | bytes 1572872 | tf_op jit(solution)/shard_map/ppermute | solution.py:35
  116.7 14.5 %copy-start.6 = (s32[1,128]{1,0:T(1,128)S(1)}, s32[1,128]{1,0:T(1,128)}, u32[]{:S(2)}) copy-start(s32[1,128]{1,0:T(1,128)} %get-tuple-element.12) | copy-start | bytes 1540
  116.7 14.6 %copy-start.7 = (f32[1,128]{1,0:T(1,128)S(1)}, f32[1,128]{1,0:T(1,128)}, u32[]{:S(2)}) copy-start(f32[1,128]{1,0:T(1,128)} %get-tuple-element.21) | copy-start | bytes 1540
  117.0 5.2 %collective-permute-start.10 = (f16[8,8192]{1,0:T(8,128)(2,1)S(1)}, f16[8,8192]{1,0:T(8,128)(2,1)S(1)}, u32[]{:S(2)}, u32[]{:S(2)}) collective-permute-start(f16[8,8192]{1,0:T(8,128)(2,1)S(1)} %get-tuple-element.22), channel_id=1, source_target_pairs={{0,64},{1,65},{2,66},{3,67},{4,68},{5,69},{6,70},{7,71},{8,24},{9,... | collective-permute-start | bytes 393224 | tf_op jit(solution)/shard_map/ppermute | solution.py:35
  117.3 5.0 %collective-permute-start.12 = (f16[8,8192]{1,0:T(8,128)(2,1)S(1)}, f16[8,8192]{1,0:T(8,128)(2,1)S(1)}, u32[]{:S(2)}, u32[]{:S(2)}) collective-permute-start(f16[8,8192]{1,0:T(8,128)(2,1)S(1)} %get-tuple-element.23), channel_id=1, source_target_pairs={{0,192},{1,193},{2,194},{3,195},{4,196},{5,197},{6,198},{7,199},{8... | collective-permute-start | bytes 393224 | tf_op jit(solution)/shard_map/ppermute | solution.py:35
  119.3 6.5 %collective-permute-start.11 = (f16[8,8192]{1,0:T(8,128)(2,1)S(1)}, f16[8,8192]{1,0:T(8,128)(2,1)S(1)}, u32[]{:S(2)}, u32[]{:S(2)}) collective-permute-start(f16[8,8192]{1,0:T(8,128)(2,1)S(1)} %get-tuple-element.24), channel_id=1, source_target_pairs={{0,128},{1,129},{2,130},{3,131},{4,132},{5,133},{6,134},{7,135},{8... | collective-permute-start | bytes 393224 | tf_op jit(solution)/shard_map/ppermute | solution.py:35
  127.8 12.4 %all-to-all-start.2 = ((f16[8,2,4096]{2,1,0:T(2,128)(2,1)}), f16[8,2,4096]{2,1,0:T(2,128)(2,1)S(1)}, u32[]{:S(2)}, u32[]{:S(2)}) async-start(f16[8,2,4096]{2,1,0:T(2,128)(2,1)} %reshape.34), calls=%async_computation.2 | async-start | bytes 262144 | tf_op jit(solution)/shard_map/all_to_all | solution.py:176

commit v3 on v2

v3 whole, which is shorter than its diff:
```python
import functools

import jax
import jax.numpy as jnp
from jax import lax
from jax.experimental import pallas as pl
from jax.experimental.pallas import tpu as pltpu
from jax.sharding import Mesh, PartitionSpec as P

loss_scale = 128.0
send_scale = 32.0
send_type = jnp.float16
width = 8192
wide = width + 256


def spans(sizes):
    return [(sum(sizes[:k]), size) for k, size in enumerate(sizes)]


logit_chunks = spans([1024, 1024, 2048, 2048, 2048])
grad_chunks = spans([1024, 2048, 2048, 2048, 1024])
f32, bf16, i32 = jnp.float32, jnp.bfloat16, jnp.int32


def device(x, y, c, z):
    return ((x * 4 + y) * 2 + c) * 8 + z


R4, R8 = range(4), range(8)
places = [(x, y, c, z) for x in R4 for y in R4 for c in (0, 1) for z in R8]
along_z = [[device(x, y, c, z) for z in R8] for x in R4 for y in R4 for c in (0, 1)]
same_core = [[device(x, y, c, z) for x in R4 for y in R4 for z in R8] for c in (0, 1)]
partner = [(device(x, y, c, z), device(x, y, 1 - c, z)) for x, y, c, z in places]


def shift(value, outer, k):
    pairs = []
    for x, y, c, z in places:
        to = device(x, (y + k) % 4, c, z) if outer == (c == 0) else device((x + k) % 4, y, c, z)
        pairs.append((device(x, y, c, z), to))
    return lax.ppermute(value, "d", pairs)


def vmem(*args):
    return pl.BlockSpec(*args) if args else pl.BlockSpec(memory_space=pltpu.VMEM)


smem = pl.BlockSpec(memory_space=pltpu.SMEM)
anywhere = pl.BlockSpec(memory_space=pl.ANY)


def pack_kernel(count_ref, mask_ref, target_ref, hidden_ref, row_ref, kept_ref, slab, sem):
    lane = lax.broadcasted_iota(i32, (1, 128), 1)
    first = jnp.min(jnp.where(mask_ref[...] == 1, lane, 127).astype(f32)).astype(i32)
    copy = pltpu.make_async_copy(hidden_ref.at[pl.ds(pl.multiple_of(first // 8 * 8, 8), 8)], slab, sem)
    copy.start()
    kept = (lane == first) & (mask_ref[...] == 1) & (count_ref[0] > 0)
    kept_ref[...] = kept.astype(i32)
    code = jnp.sum(jnp.where(kept, target_ref[...] + 1, 0).astype(f32)).astype(i32)
    wide_lane = lax.broadcasted_iota(i32, (1, 256), 1)
    digits = jnp.where(wide_lane == 0, code % 256, 0) + jnp.where(wide_lane == 1, code // 256 % 256, 0)
    digits = digits + jnp.where(wide_lane == 2, code // 65536, 0)
    copy.wait()
    take = (lax.broadcasted_iota(i32, (8, width), 0) == first % 8) & (code > 0)
    row = jnp.sum(jnp.where(take, slab[...].astype(f32), 0.0), axis=0, keepdims=True)
    half = wide // 2
    low, high = row[:, :half], jnp.concatenate([row[:, half:], digits.astype(f32)], axis=1)
    both = jnp.where(lax.broadcasted_iota(i32, (2, half), 0) == 0, low, high).astype(bf16)
    row_ref[...] = jnp.broadcast_to(both[None], row_ref.shape)


def pack(count, mask, target, hidden):
    return pl.pallas_call(
        pack_kernel,
        in_specs=[smem, vmem(), vmem(), anywhere],
        out_specs=[vmem(), vmem()],
        out_shape=[jax.ShapeDtypeStruct((8, 2, wide // 2), bf16), jax.ShapeDtypeStruct((1, 128), i32)],
        scratch_shapes=[pltpu.VMEM((8, width), bf16), pltpu.SemaphoreType.DMA],
        name="pack",
    )(count, mask.reshape(1, 128), target.reshape(1, 128), hidden)


def by_rank(values, i, j):
    values = pltpu.roll(values, j * 32, 1)
    lane = lax.broadcasted_iota(i32, values.shape, 1)
    return jnp.where(lane % 32 >= i * 8, pltpu.roll(values, i * 8, 1), pltpu.roll(values, (i * 8 + 96) % 128, 1))


def by_arrival(values, i, j):
    lane = lax.broadcasted_iota(i32, values.shape, 1)
    back, around = pltpu.roll(values, (128 - i * 8) % 128, 1), pltpu.roll(values, 32 - i * 8, 1)
    return pltpu.roll(jnp.where(lane % 32 < 32 - i * 8, back, around), (128 - j * 32) % 128, 1)


def fetch(pairs, sems):
    copies = [[pltpu.make_async_copy(a, b, sems.at[k, n]) for n, (a, b) in enumerate(p)] for k, p in enumerate(pairs)]
    for chunk in copies:
        for copy in chunk:
            copy.start()
    return copies


def logits_kernel(vocab_rows, place_ref, digits_ref, r0, r1, r2, r3, w_ref, v_ref, own_ref, other_ref, stats_ref, rows, weights, sems):
    pairs = []
    for start, size in logit_chunks:
        cols = pl.ds(start, size)
        pair = [(w_ref.at[:, cols], weights.at[0, :, cols]), (v_ref.at[:, cols], weights.at[1, :, cols])]
        pair += [(r.at[:, cols], rows.at[pl.ds(k * 32, 32), cols]) for k, r in enumerate((r0, r1, r2, r3))]
        pairs.append(pair)
    copies = fetch(pairs, sems)
    for k, (start, size) in enumerate(logit_chunks):
        for copy in copies[k]:
            copy.wait()
        cols = pl.ds(start, size)
        for slot, out in enumerate((own_ref, other_ref)):
            part = lax.dot_general(
                weights[slot, :, cols], rows[:, cols], (((1,), (1,)), ((), ())), preferred_element_type=f32
            )
            out[...] = part if k == 0 else out[...] + part

    i, j, me = place_ref[0], place_ref[1], place_ref[2]
    target = digits_ref[0:1] + 256 * digits_ref[1:2] + 65536 * digits_ref[2:3] - 1
    top = jnp.maximum(jnp.max(own_ref[...], axis=0, keepdims=True), jnp.max(other_ref[...], axis=0, keepdims=True))
    total, pick = 0.0, 0.0
    for out, base in ((own_ref, me), (other_ref, me ^ 8)):
        ids = lax.broadcasted_iota(i32, (vocab_rows, 128), 0) + base * vocab_rows
        total += jnp.sum(jnp.exp(out[...] - top), axis=0, keepdims=True)
        pick += jnp.sum(jnp.where(ids == target, out[...], 0.0), axis=0, keepdims=True)
    row = lax.broadcasted_iota(i32, (8, 128), 0)
    stats = jnp.where(row == 0, top + jnp.log(total), pick)
    stats_ref[...] = jnp.broadcast_to(by_rank(stats, i, j)[None, :2], stats_ref.shape)


def logits_call(place, digits, rows, own, other):
    vocab_rows = own.shape[0]
    return pl.pallas_call(
        functools.partial(logits_kernel, vocab_rows),
        in_specs=[smem, vmem()] + [anywhere] * 6,
        out_specs=[vmem()] * 3,
        out_shape=[jax.ShapeDtypeStruct((vocab_rows, 128), f32)] * 2 + [jax.ShapeDtypeStruct((128, 2, 128), f32)],
        scratch_shapes=[
            pltpu.VMEM((128, width), bf16),
            pltpu.VMEM((2, vocab_rows, width), bf16),
            pltpu.SemaphoreType.DMA((len(logit_chunks), 6)),
        ],
        name="logits",
    )(place, digits, *rows, own, other)


def grad_kernel(
    vocab_rows, place_ref, digits_ref, stats_ref, own_ref, other_ref, w_ref, v_ref, g0, g1, g2, g3, loss_ref, coefs, weights, grads, sems, sent
):
    pairs = []
    for start, size in grad_chunks:
        cols = pl.ds(start, size)
        pairs.append([(w_ref.at[:, cols], weights.at[0, :, cols]), (v_ref.at[:, cols], weights.at[1, :, cols])])
    copies = fetch(pairs, sems)

    i, j, me = place_ref[0], place_ref[1], place_ref[2]
    lse = stats_ref[:, 0, :]
    top = jnp.max(lse, axis=0, keepdims=True)
    log_total = top + jnp.log(jnp.sum(jnp.exp(lse - top), axis=0, keepdims=True))
    picked = jnp.sum(stats_ref[:, 1, :], axis=0, keepdims=True)
    target = digits_ref[0:1] + 256 * digits_ref[1:2] + 65536 * digits_ref[2:3] - 1
    loss_ref[...] = log_total - picked
    log_total = by_arrival(jnp.broadcast_to(log_total, (8, 128)), i, j)[0:1]
    for slot, (out, base) in enumerate(((own_ref, me), (other_ref, me ^ 8))):
        ids = lax.broadcasted_iota(i32, (vocab_rows, 128), 0) + base * vocab_rows
        hit = (ids == target).astype(f32)
        coefs[slot] = jnp.where(target >= 0, jnp.exp(out[...] - log_total) - hit, 0.0).T.astype(bf16)

    out_copies = []
    for k, (start, size) in enumerate(grad_chunks):
        for copy in copies[k]:
            copy.wait()
        cols = pl.ds(start, size)
        grad = jnp.dot(coefs[0], weights[0, :, cols], preferred_element_type=f32)
        grad += jnp.dot(coefs[1], weights[1, :, cols], preferred_element_type=f32)
        grads[:, cols] = grad * (loss_scale * send_scale)
        for n, out in enumerate((g0, g1, g2, g3)):
            copy = pltpu.make_async_copy(grads.at[pl.ds(n * 32, 32), cols], out.at[:, cols], sent.at[k, n])
            copy.start()
            out_copies.append(copy)
    for copy in out_copies:
        copy.wait()


def grad_call(place, digits, stats, logits, own, other):
    vocab_rows = own.shape[0]
    return pl.pallas_call(
        functools.partial(grad_kernel, vocab_rows),
        in_specs=[smem] + [vmem()] * 4 + [anywhere] * 2,
        out_specs=[anywhere] * 4 + [vmem()],
        out_shape=[jax.ShapeDtypeStruct((32, width), f32)] * 4 + [jax.ShapeDtypeStruct((1, 128), f32)],
        scratch_shapes=[
            pltpu.VMEM((2, 128, vocab_rows), bf16),
            pltpu.VMEM((2, vocab_rows, width), bf16),
            pltpu.VMEM((128, width), f32),
            pltpu.SemaphoreType.DMA((len(grad_chunks), 2)),
            pltpu.SemaphoreType.DMA((len(grad_chunks), 4)),
        ],
        name="grad",
    )(place, digits, stats, *logits, own, other)


def exchange(value, groups):
    return lax.all_to_all(value, "d", 0, 0, axis_index_groups=groups)


def gather4(value, outer):
    far, back, on = shift(value, outer, 2), shift(value, outer, 1), shift(value, outer, 3)
    return [value, on, far, back]


def reduce4(blocks, outer):
    far, on, back = shift(blocks[2], outer, 2), shift(blocks[1], outer, 1), shift(blocks[3], outer, 3)
    return (blocks[0].astype(f32) + on.astype(f32)) + (far.astype(f32) + back.astype(f32))


def shards(hidden, out_weight, loss_mask, targets, kept_count):
    me = lax.axis_index("d")
    z, c, y, x = me % 8, (me // 8) % 2, (me // 16) % 4, me // 64
    i, j = jnp.where(c == 0, x, y), jnp.where(c == 0, y, x)
    place = jnp.stack([i, j, me])
    other_weight = lax.ppermute(out_weight, "d", partner)

    packed, kept = pack(kept_count, loss_mask, targets, hidden)
    rows = exchange(packed, along_z).reshape(8, wide)
    rows = jnp.concatenate(gather4(rows, False), axis=0)
    rows = gather4(rows, True)
    digits = jnp.concatenate([r[:, width:width + 4] for r in rows], axis=0).T.astype(i32)
    *logits, stats = logits_call(place, digits, rows, out_weight, other_weight)
    stats = exchange(stats, same_core)
    *parts, loss = grad_call(place, digits, stats, logits, out_weight, other_weight)
    part = reduce4([p.astype(send_type) for p in parts], True)
    part = part.astype(send_type)
    part = reduce4([part[k * 8:(k + 1) * 8] for k in R4], False)
    part = exchange(part.astype(send_type).reshape(8, width // 128, 128), along_z)
    own_grad = (jnp.sum(part.astype(f32), axis=0) * (1.0 / send_scale)).reshape(1, width)

    own_loss = lax.dynamic_slice_in_dim(loss[0], (j * 4 + i) * 8 + z, 1, 0)
    kept_row = kept[0] > 0
    hidden_grad = jnp.where(kept_row[:, None], own_grad, 0.0).astype(bf16)
    row_loss = jnp.where(kept_row, own_loss, 0.0)
    return hidden_grad, row_loss


def solution(mesh):
    flat = Mesh(mesh.devices.reshape(-1), ("d",))
    rows = P("d", None)
    vector = P("d")
    return jax.shard_map(
        shards, mesh=flat, in_specs=(rows, rows, vector, vector, vector), out_specs=(rows, vector), check_vma=False
    )
```

time: 143 us -> 136 us (0.951)
  Pallas kernels: 25.9 us -> 21.8 us
    pallas_call x2, Pallas kernels: 23.4 us -> 19.4 us  [the longest x1 9.92 us: grad_call(): pl.pallas_call(functools.partial(grad_kernel, vocab_rows), in_specs=[smem...]
  transfers between devices with their start and end apart: 14 -> 14, of which waited for: 9 -> 10; matrix products, arithmetic and copies ran while one was open for 2% -> 3% of each run, Pallas kernels for 2% -> 2%
where the time goes in v3:
time: 136 us; the launch traced here: 135 us
  waiting for transfers between devices  44.8 us (33%)
  blocking collectives  37.6 us (28%)
  Pallas kernels  21.8 us (16%)
  starting transfers between devices  20.4 us (15%)
  other arithmetic  7.25 us (5%)
  local copies, waits for them, and re-layouts  1.93 us (1%)
  between operations  1.52 us (1%)
    ppermute x12, waiting for transfers between devices, shift(): return lax.ppermute(value, 'd', pairs)  37.6 us
    all_to_all x2, blocking collectives, exchange(): return lax.all_to_all(value, 'd', 0, 0, axis_index_groups=groups)  37.6 us
    ppermute x12, starting transfers between devices, shift(): return lax.ppermute(value, 'd', pairs)  16.9 us
    pallas_call x1, Pallas kernels, grad_call(): pl.pallas_call(functools.partial(grad_kernel, vocab_rows), in_specs=[smem...  9.92 us
    pallas_call x1, Pallas kernels, logits_call(): pl.pallas_call(functools.partial(logits_kernel, vocab_rows), in_specs=[sm...  9.44 us
    all_to_all x1, waiting for transfers between devices, exchange(): return lax.all_to_all(value, 'd', 0, 0, axis_index_groups=groups)  7.21 us
    all_to_all x1, starting transfers between devices, exchange(): return lax.all_to_all(value, 'd', 0, 0, axis_index_groups=groups)  3.37 us
    convert_element_type x3, other arithmetic, shards(): part = reduce4([p.astype(send_type) for p in parts], True)  2.76 us
  transfers between devices with their start and end apart: 14, of which 10 were waited for; matrix products, arithmetic and copies ran while one was open for 3% of the time, Pallas kernels for 2%

profile of v3, /device:TPU:2, one launch (start us, length us, event | category | flops | bytes accessed | tf_op | source)
XLA Modules:
  0.0 135.3 jit_solution(10450540900840850216)
XLA Ops:
  0.6 0.1 collective-permute-start.6
  1.4 2.5 %pack.1 = (bf16[8,2,4224]{2,1,0:T(2,128)(2,1)}, s32[1,128]{1,0:T(1,128)}) custom-call(s32[1]{0:T(128)S(6)} %copy.25.count_ref, s32[1,128]{1,0:T(1,128)} %bitcast.23, s32[1,128]{1,0:T(1,128)} %bitcast.24, bf16[128,8192]{1,0:T(8,128)(2,1)} %hidden_ref.1), custom_call_target="tpu_custom_call" | custom-call | tf_op jit(solution)/shard_map/pack/pallas_call | solution.py:74
  3.9 18.3 %all_to_all.15 = bf16[8,2,4224]{2,1,0:T(2,128)(2,1)S(1)} all-to-all(bf16[8,2,4224]{2,1,0:T(2,128)(2,1)} %get-tuple-element.13), channel_id=1, replica_groups={{0,1,2,3,4,5,6,7},{8,9,10,11,12,13,14,15},{16,17,18,19,20,21,22,23},{24..., dimensions={0} | all-to-all | bytes 270336 | tf_op jit(solution)/shard_map/all_to_all | solution.py:208
  22.2 1.6 %collective-permute-start.2 = (bf16[8,8448]{1,0:T(8,128)(2,1)S(1)}, bf16[8,8448]{1,0:T(8,128)(2,1)S(1)}, u32[]{:S(2)}, u32[]{:S(2)}) collective-permute-start(bf16[8,8448]{1,0:T(8,128)(2,1)S(1)} %bitcast.18), channel_id=1, source_target_pairs={{0,64},{1,65},{2,66},{3,67},{4,68},{5,69},{6,70},{7,71},{8,24},{9,... | collective-permute-start | bytes 405512 | tf_op jit(solution)/shard_map/ppermute | solution.py:42
  23.7 1.1 collective-permute-start.1
  24.8 2.2 %collective-permute-start = (bf16[8,8448]{1,0:T(8,128)(2,1)S(1)}, bf16[8,8448]{1,0:T(8,128)(2,1)S(1)}, u32[]{:S(2)}, u32[]{:S(2)}) collective-permute-start(bf16[8,8448]{1,0:T(8,128)(2,1)S(1)} %bitcast.20), channel_id=1, source_target_pairs={{0,192},{1,193},{2,194},{3,195},{4,196},{5,197},{6,198},{7,199},{8... | collective-permute-start | bytes 405512 | tf_op jit(solution)/shard_map/ppermute | solution.py:42
  27.0 4.3 %collective-permute-done = bf16[8,8448]{1,0:T(8,128)(2,1)S(1)} collective-permute-done((bf16[8,8448]{1,0:T(8,128)(2,1)S(1)}, bf16[8,8448]{1,0:T(8,128)(2,1)S(1)}, u32[]{:S(2)}, u32[]{:S(2)}) %collective-permute-start) | collective-permute-done | bytes 135200 | tf_op jit(solution)/shard_map/ppermute | solution.py:42
  31.3 0.0 collective-permute-done.1
  31.4 0.0 collective-permute-done.2
  31.4 0.0 copy-start.2
  31.4 1.7 %collective-permute-start.5 = (bf16[32,8448]{1,0:T(8,128)(2,1)S(1)}, bf16[32,8448]{1,0:T(8,128)(2,1)S(1)}, u32[]{:S(2)}, u32[]{:S(2)}) collective-permute-start(bf16[32,8448]{1,0:T(8,128)(2,1)S(1)} %constant_dynamic-update-slice_fusion.r0), channel_id=1, source_target_pairs={{0,16},{1,17},{2,18},{3,19},{4,20},{5,21},{6,22},{7,23},{8,72},{9,... | collective-permute-start | bytes 1622024 | tf_op jit(solution)/shard_map/ppermute | solution.py:42
  33.0 2.9 %collective-permute-start.4 = (bf16[32,8448]{1,0:T(8,128)(2,1)S(1)}, bf16[32,8448]{1,0:T(8,128)(2,1)S(1)}, u32[]{:S(2)}, u32[]{:S(2)}) collective-permute-start(bf16[32,8448]{1,0:T(8,128)(2,1)S(1)} %constant_dynamic-update-slice_fusion.r0), channel_id=1, source_target_pairs={{0,32},{1,33},{2,34},{3,35},{4,36},{5,37},{6,38},{7,39},{8,136},{9... | collective-permute-start | bytes 1622024 | tf_op jit(solution)/shard_map/ppermute | solution.py:42
  35.9 1.3 collective-permute-start.3
  37.3 0.6 pad_add_fusion.place_ref
  37.9 0.1 copy.17
  38.0 4.1 %collective-permute-done.5.r3 = bf16[32,8448]{1,0:T(8,128)(2,1)S(1)} collective-permute-done((bf16[32,8448]{1,0:T(8,128)(2,1)S(1)}, bf16[32,8448]{1,0:T(8,128)(2,1)S(1)}, u32[]{:S(2)}, u32[]{:S(2)}) %collective-permute-start.5) | collective-permute-done | bytes 540704 | tf_op jit(solution)/shard_map/ppermute | solution.py:42
  42.0 0.0 copy-start.3
  42.0 0.1 copy.20
  42.1 6.9 %collective-permute-done.4.r2 = bf16[32,8448]{1,0:T(8,128)(2,1)S(1)} collective-permute-done((bf16[32,8448]{1,0:T(8,128)(2,1)S(1)}, bf16[32,8448]{1,0:T(8,128)(2,1)S(1)}, u32[]{:S(2)}, u32[]{:S(2)}) %collective-permute-start.4) | collective-permute-done | bytes 540704 | tf_op jit(solution)/shard_map/ppermute | solution.py:42
  49.1 0.0 copy-start.4
  49.1 0.1 copy.19
  49.2 0.0 collective-permute-done.3.r1
  49.2 0.0 copy-start.5
  49.2 0.1 copy.18
  49.3 0.7 convert_bitcast_fusion.digits_ref
  50.0 0.0 collective-permute-done.6.v_ref
  50.0 0.0 copy-done.2
  50.0 0.0 copy-done.3
  50.0 0.0 copy-done.4
  50.0 0.1 copy-done.5
  50.1 9.4 %logits.1 = (f32[501,128]{1,0:T(8,128)}, f32[501,128]{1,0:T(8,128)}, f32[128,2,128]{2,1,0:T(2,128)}) custom-call(s32[3]{0:T(128)} %pad_add_fusion.place_ref, s32[4,128]{1,0:T(4,128)} %convert_bitcast_fusion.digits_ref, bf16[32,8448]{1,0:T(8,128)(2,1)} %copy-done.2, bf16[32,8448]{1,0:T(8,128)(2,1)} %copy-done.5, bf16[32,8448]{1,0:T(8,128)(2,1)} %copy-done.4, ...), custom_call_target="tpu_custom_call" | custom-call | tf_op jit(solution)/shard_map/logits/pallas_call | solution.py:137
  59.6 19.3 %all_to_all.16.stats_ref = f32[128,2,128]{2,1,0:T(2,128)} all-to-all(f32[128,2,128]{2,1,0:T(2,128)} %get-tuple-element.14), channel_id=1, replica_groups={{0,1,2,3,4,5,6,7,16,17,18,19,20,21,22,23,32,33,34,35,36,37,38,39,48,49,..., dimensions={0} | all-to-all | bytes 262144 | tf_op jit(solution)/shard_map/all_to_all | solution.py:208
  78.8 9.9 %grad.1 = (f32[32,8192]{1,0:T(8,128)}, f32[32,8192]{1,0:T(8,128)}, f32[32,8192]{1,0:T(8,128)}, f32[32,8192]{1,0:T(8,128)}, f32[1,128]{1,0:T(1,128)}) custom-call(s32[3]{0:T(128)} %pad_add_fusion.place_ref, s32[4,128]{1,0:T(4,128)} %convert_bitcast_fusion.digits_ref, f32[128,2,128]{2,1,0:T(2,128)} %all_to_all.16.stats_ref, ...), custom_call_target="tpu_custom_call" | custom-call | tf_op jit(solution)/shard_map/grad/pallas_call | solution.py:191
  88.8 0.0 copy-start.1
  88.8 0.0 copy-start
  88.8 1.4 %convert_element_type.57 = f16[32,8192]{1,0:T(8,128)(2,1)S(1)} convert(f32[32,8192]{1,0:T(8,128)} %get-tuple-element.18) | non-fusion elementwise | flops 262144 | bytes 1572864 | tf_op jit(solution)/shard_map/convert_element_type | solution.py:236
  90.2 1.3 convert_element_type.59
  91.5 0.0 copy-done.1
  91.5 0.1 convert_element_type.61
  91.6 1.7 %collective-permute-start.9 = (f16[32,8192]{1,0:T(8,128)(2,1)S(1)}, f16[32,8192]{1,0:T(8,128)(2,1)S(1)}, u32[]{:S(2)}, u32[]{:S(2)}) collective-permute-start(f16[32,8192]{1,0:T(8,128)(2,1)S(1)} %convert_element_type.61), channel_id=1, source_target_pairs={{0,48},{1,49},{2,50},{3,51},{4,52},{5,53},{6,54},{7,55},{8,200},{9... | collective-permute-start | bytes 1572872 | tf_op jit(solution)/shard_map/ppermute | solution.py:42
  93.2 1.2 collective-permute-start.8
  94.5 0.5 collective-permute-start.7
  94.9 5.9 %collective-permute-done.9 = f16[32,8192]{1,0:T(8,128)(2,1)S(1)} collective-permute-done((f16[32,8192]{1,0:T(8,128)(2,1)S(1)}, f16[32,8192]{1,0:T(8,128)(2,1)S(1)}, u32[]{:S(2)}, u32[]{:S(2)}) %collective-permute-start.9) | collective-permute-done | bytes 524320 | tf_op jit(solution)/shard_map/ppermute | solution.py:42
  100.8 3.2 %collective-permute-done.8 = f16[32,8192]{1,0:T(8,128)(2,1)S(1)} collective-permute-done((f16[32,8192]{1,0:T(8,128)(2,1)S(1)}, f16[32,8192]{1,0:T(8,128)(2,1)S(1)}, u32[]{:S(2)}, u32[]{:S(2)}) %collective-permute-start.8) | collective-permute-done | bytes 524320 | tf_op jit(solution)/shard_map/ppermute | solution.py:42
  104.0 7.5 %collective-permute-done.7 = f16[32,8192]{1,0:T(8,128)(2,1)S(1)} collective-permute-done((f16[32,8192]{1,0:T(8,128)(2,1)S(1)}, f16[32,8192]{1,0:T(8,128)(2,1)S(1)}, u32[]{:S(2)}, u32[]{:S(2)}) %collective-permute-start.7) | collective-permute-done | bytes 524320 | tf_op jit(solution)/shard_map/ppermute | solution.py:42
  111.5 0.0 copy-done
  111.5 0.0 copy-start.6
  111.5 0.3 add_convert_fusion
  111.8 0.1 fusion.1
  111.8 0.1 collective-permute-start.10
  111.9 2.0 %collective-permute-start.12 = (f16[8,8192]{1,0:T(8,128)(2,1)S(1)}, f16[8,8192]{1,0:T(8,128)(2,1)S(1)}, u32[]{:S(2)}, u32[]{:S(2)}) collective-permute-start(f16[8,8192]{1,0:T(8,128)(2,1)S(1)} %get-tuple-element.23), channel_id=1, source_target_pairs={{0,192},{1,193},{2,194},{3,195},{4,196},{5,197},{6,198},{7,199},{8... | collective-permute-start | bytes 393224 | tf_op jit(solution)/shard_map/ppermute | solution.py:42
  114.0 0.7 collective-permute-start.11
  114.7 2.2 %collective-permute-done.10 = f16[8,8192]{1,0:T(8,128)(2,1)S(1)} collective-permute-done((f16[8,8192]{1,0:T(8,128)(2,1)S(1)}, f16[8,8192]{1,0:T(8,128)(2,1)S(1)}, u32[]{:S(2)}, u32[]{:S(2)}) %collective-permute-start.10) | collective-permute-done | bytes 131104 | tf_op jit(solution)/shard_map/ppermute | solution.py:42
  116.9 0.1 collective-permute-done.12
  117.0 3.4 %collective-permute-done.11 = f16[8,8192]{1,0:T(8,128)(2,1)S(1)} collective-permute-done((f16[8,8192]{1,0:T(8,128)(2,1)S(1)}, f16[8,8192]{1,0:T(8,128)(2,1)S(1)}, u32[]{:S(2)}, u32[]{:S(2)}) %collective-permute-start.11) | collective-permute-done | bytes 131104 | tf_op jit(solution)/shard_map/ppermute | solution.py:42
  120.4 0.1 fusion
  120.5 0.7 copy.16
  121.2 3.4 %all-to-all-start.2 = ((f16[8,64,128]{2,1,0:T(8,128)(2,1)}), f16[8,64,128]{2,1,0:T(8,128)(2,1)S(1)}, u32[]{:S(2)}, u32[]{:S(2)}) async-start(f16[8,64,128]{2,1,0:T(8,128)(2,1)} %copy.16), calls=%async_computation.2 | async-start | bytes 262144 | tf_op jit(solution)/shard_map/all_to_all | solution.py:208
  124.6 0.0 copy-done.6
  124.6 0.0 copy-done.7
  124.6 0.6 constant_dynamic-slice_fusion
  125.2 1.1 broadcast_select_fusion
  126.4 7.2 %all-to-all-done.2 = f16[8,64,128]{2,1,0:T(8,128)(2,1)S(1)} async-done(((f16[8,64,128]{2,1,0:T(8,128)(2,1)}), f16[8,64,128]{2,1,0:T(8,128)(2,1)S(1)}, u32[]{:S(2)}, u32[]{:S(2)}) %all-to-all-start.2) | async-done | bytes 131104 | tf_op jit(solution)/shard_map/all_to_all | solution.py:208
  133.6 1.7 %select_convert_fusion = bf16[128,8192]{1,0:T(8,128)(2,1)} fusion(bf16[8192]{0:T(1024)(128)(2,1)S(1)} %multiply_bitcast_fusion, pred[128]{0:T(512)(128)(4,1)S(1)} %compare_bitcast_fusion), kind=kLoop, calls=%fused_computation | loop fusion | flops 1048576 | bytes 2113664 | tf_op jit(solution)/shard_map/convert_element_type | solution.py:244
  (13 shorter events, 0.1 us)
Async XLA Ops:
  0.6 49.4 %collective-permute-start.6 = (bf16[501,8192]{1,0:T(8,128)(2,1)}, bf16[501,8192]{1,0:T(8,128)(2,1)}, u32[]{:S(2)}, u32[]{:S(2)}) collective-permute-start(bf16[501,8192]{1,0:T(8,128)(2,1)} %w_ref.3), channel_id=1, source_target_pairs={{0,8},{1,9},{2,10},{3,11},{4,12},{5,13},{6,14},{7,15},{8,0},{9,1},... | collective-permute-start | bytes 24625160 | tf_op jit(solution)/shard_map/ppermute | solution.py:226
  22.2 9.2 %collective-permute-start.2 = (bf16[8,8448]{1,0:T(8,128)(2,1)S(1)}, bf16[8,8448]{1,0:T(8,128)(2,1)S(1)}, u32[]{:S(2)}, u32[]{:S(2)}) collective-permute-start(bf16[8,8448]{1,0:T(8,128)(2,1)S(1)} %bitcast.18), channel_id=1, source_target_pairs={{0,64},{1,65},{2,66},{3,67},{4,68},{5,69},{6,70},{7,71},{8,24},{9,... | collective-permute-start | bytes 405512 | tf_op jit(solution)/shard_map/ppermute | solution.py:42
  23.7 7.6 %collective-permute-start.1 = (bf16[8,8448]{1,0:T(8,128)(2,1)S(1)}, bf16[8,8448]{1,0:T(8,128)(2,1)S(1)}, u32[]{:S(2)}, u32[]{:S(2)}) collective-permute-start(bf16[8,8448]{1,0:T(8,128)(2,1)S(1)} %bitcast.19), channel_id=1, source_target_pairs={{0,128},{1,129},{2,130},{3,131},{4,132},{5,133},{6,134},{7,135},{8... | collective-permute-start | bytes 405512 | tf_op jit(solution)/shard_map/ppermute | solution.py:42
  24.8 6.5 %collective-permute-start = (bf16[8,8448]{1,0:T(8,128)(2,1)S(1)}, bf16[8,8448]{1,0:T(8,128)(2,1)S(1)}, u32[]{:S(2)}, u32[]{:S(2)}) collective-permute-start(bf16[8,8448]{1,0:T(8,128)(2,1)S(1)} %bitcast.20), channel_id=1, source_target_pairs={{0,192},{1,193},{2,194},{3,195},{4,196},{5,197},{6,198},{7,199},{8... | collective-permute-start | bytes 405512 | tf_op jit(solution)/shard_map/ppermute | solution.py:42
  31.4 18.6 %copy-start.2 = (bf16[32,8448]{1,0:T(8,128)(2,1)}, bf16[32,8448]{1,0:T(8,128)(2,1)S(1)}, u32[]{:S(2)}) copy-start(bf16[32,8448]{1,0:T(8,128)(2,1)S(1)} %constant_dynamic-update-slice_fusion.r0) | copy-start | bytes 1622020
  31.4 10.6 %collective-permute-start.5 = (bf16[32,8448]{1,0:T(8,128)(2,1)S(1)}, bf16[32,8448]{1,0:T(8,128)(2,1)S(1)}, u32[]{:S(2)}, u32[]{:S(2)}) collective-permute-start(bf16[32,8448]{1,0:T(8,128)(2,1)S(1)} %constant_dynamic-update-slice_fusion.r0), channel_id=1, source_target_pairs={{0,16},{1,17},{2,18},{3,19},{4,20},{5,21},{6,22},{7,23},{8,72},{9,... | collective-permute-start | bytes 1622024 | tf_op jit(solution)/shard_map/ppermute | solution.py:42
  33.0 16.0 %collective-permute-start.4 = (bf16[32,8448]{1,0:T(8,128)(2,1)S(1)}, bf16[32,8448]{1,0:T(8,128)(2,1)S(1)}, u32[]{:S(2)}, u32[]{:S(2)}) collective-permute-start(bf16[32,8448]{1,0:T(8,128)(2,1)S(1)} %constant_dynamic-update-slice_fusion.r0), channel_id=1, source_target_pairs={{0,32},{1,33},{2,34},{3,35},{4,36},{5,37},{6,38},{7,39},{8,136},{9... | collective-permute-start | bytes 1622024 | tf_op jit(solution)/shard_map/ppermute | solution.py:42
  35.9 13.2 %collective-permute-start.3 = (bf16[32,8448]{1,0:T(8,128)(2,1)S(1)}, bf16[32,8448]{1,0:T(8,128)(2,1)S(1)}, u32[]{:S(2)}, u32[]{:S(2)}) collective-permute-start(bf16[32,8448]{1,0:T(8,128)(2,1)S(1)} %constant_dynamic-update-slice_fusion.r0), channel_id=1, source_target_pairs={{0,48},{1,49},{2,50},{3,51},{4,52},{5,53},{6,54},{7,55},{8,200},{9... | collective-permute-start | bytes 1622024 | tf_op jit(solution)/shard_map/ppermute | solution.py:42
  42.0 8.0 %copy-start.3 = (bf16[32,8448]{1,0:T(8,128)(2,1)}, bf16[32,8448]{1,0:T(8,128)(2,1)S(1)}, u32[]{:S(2)}) copy-start(bf16[32,8448]{1,0:T(8,128)(2,1)S(1)} %collective-permute-done.5.r3) | copy-start | bytes 1622020
  49.1 0.9 copy-start.4
  49.2 1.0 copy-start.5
  88.8 2.7 %copy-start.1 = (f32[32,8192]{1,0:T(8,128)S(1)}, f32[32,8192]{1,0:T(8,128)}, u32[]{:S(2)}) copy-start(f32[32,8192]{1,0:T(8,128)} %get-tuple-element.20) | copy-start | bytes 3145732
  88.8 22.7 %copy-start = (f32[32,8192]{1,0:T(8,128)S(1)}, f32[32,8192]{1,0:T(8,128)}, u32[]{:S(2)}) copy-start(f32[32,8192]{1,0:T(8,128)} %get-tuple-element.17) | copy-start | bytes 3145732
  91.6 9.3 %collective-permute-start.9 = (f16[32,8192]{1,0:T(8,128)(2,1)S(1)}, f16[32,8192]{1,0:T(8,128)(2,1)S(1)}, u32[]{:S(2)}, u32[]{:S(2)}) collective-permute-start(f16[32,8192]{1,0:T(8,128)(2,1)S(1)} %convert_element_type.61), channel_id=1, source_target_pairs={{0,48},{1,49},{2,50},{3,51},{4,52},{5,53},{6,54},{7,55},{8,200},{9... | collective-permute-start | bytes 1572872 | tf_op jit(solution)/shard_map/ppermute | solution.py:42
  93.2 10.8 %collective-permute-start.8 = (f16[32,8192]{1,0:T(8,128)(2,1)S(1)}, f16[32,8192]{1,0:T(8,128)(2,1)S(1)}, u32[]{:S(2)}, u32[]{:S(2)}) collective-permute-start(f16[32,8192]{1,0:T(8,128)(2,1)S(1)} %convert_element_type.59), channel_id=1, source_target_pairs={{0,32},{1,33},{2,34},{3,35},{4,36},{5,37},{6,38},{7,39},{8,136},{9... | collective-permute-start | bytes 1572872 | tf_op jit(solution)/shard_map/ppermute | solution.py:42
  94.5 17.0 %collective-permute-start.7 = (f16[32,8192]{1,0:T(8,128)(2,1)S(1)}, f16[32,8192]{1,0:T(8,128)(2,1)S(1)}, u32[]{:S(2)}, u32[]{:S(2)}) collective-permute-start(f16[32,8192]{1,0:T(8,128)(2,1)S(1)} %convert_element_type.57), channel_id=1, source_target_pairs={{0,16},{1,17},{2,18},{3,19},{4,20},{5,21},{6,22},{7,23},{8,72},{9,... | collective-permute-start | bytes 1572872 | tf_op jit(solution)/shard_map/ppermute | solution.py:42
  111.5 13.1 %copy-start.6 = (s32[1,128]{1,0:T(1,128)S(1)}, s32[1,128]{1,0:T(1,128)}, u32[]{:S(2)}) copy-start(s32[1,128]{1,0:T(1,128)} %get-tuple-element.12) | copy-start | bytes 1540
  111.5 13.1 %copy-start.7 = (f32[1,128]{1,0:T(1,128)S(1)}, f32[1,128]{1,0:T(1,128)}, u32[]{:S(2)}) copy-start(f32[1,128]{1,0:T(1,128)} %get-tuple-element.21) | copy-start | bytes 1540
  111.8 5.0 %collective-permute-start.10 = (f16[8,8192]{1,0:T(8,128)(2,1)S(1)}, f16[8,8192]{1,0:T(8,128)(2,1)S(1)}, u32[]{:S(2)}, u32[]{:S(2)}) collective-permute-start(f16[8,8192]{1,0:T(8,128)(2,1)S(1)} %get-tuple-element.22), channel_id=1, source_target_pairs={{0,64},{1,65},{2,66},{3,67},{4,68},{5,69},{6,70},{7,71},{8,24},{9,... | collective-permute-start | bytes 393224 | tf_op jit(solution)/shard_map/ppermute | solution.py:42
  111.9 5.0 %collective-permute-start.12 = (f16[8,8192]{1,0:T(8,128)(2,1)S(1)}, f16[8,8192]{1,0:T(8,128)(2,1)S(1)}, u32[]{:S(2)}, u32[]{:S(2)}) collective-permute-start(f16[8,8192]{1,0:T(8,128)(2,1)S(1)} %get-tuple-element.23), channel_id=1, source_target_pairs={{0,192},{1,193},{2,194},{3,195},{4,196},{5,197},{6,198},{7,199},{8... | collective-permute-start | bytes 393224 | tf_op jit(solution)/shard_map/ppermute | solution.py:42
  114.0 6.5 %collective-permute-start.11 = (f16[8,8192]{1,0:T(8,128)(2,1)S(1)}, f16[8,8192]{1,0:T(8,128)(2,1)S(1)}, u32[]{:S(2)}, u32[]{:S(2)}) collective-permute-start(f16[8,8192]{1,0:T(8,128)(2,1)S(1)} %get-tuple-element.24), channel_id=1, source_target_pairs={{0,128},{1,129},{2,130},{3,131},{4,132},{5,133},{6,134},{7,135},{8... | collective-permute-start | bytes 393224 | tf_op jit(solution)/shard_map/ppermute | solution.py:42
  121.2 12.4 %all-to-all-start.2 = ((f16[8,64,128]{2,1,0:T(8,128)(2,1)}), f16[8,64,128]{2,1,0:T(8,128)(2,1)S(1)}, u32[]{:S(2)}, u32[]{:S(2)}) async-start(f16[8,64,128]{2,1,0:T(8,128)(2,1)} %copy.16), calls=%async_computation.2 | async-start | bytes 262144 | tf_op jit(solution)/shard_map/all_to_all | solution.py:208

commit v4 on v3

--- a/solution.py
+++ b/solution.py
@@ -7,6 +7,7 @@
 from jax.experimental.pallas import tpu as pltpu
 from jax.sharding import Mesh, PartitionSpec as P
 
+
 loss_scale = 128.0
 send_scale = 32.0
 send_type = jnp.float16
@@ -18,8 +19,7 @@
     return [(sum(sizes[:k]), size) for k, size in enumerate(sizes)]
 
 
-logit_chunks = spans([1024, 1024, 2048, 2048, 2048])
-grad_chunks = spans([1024, 2048, 2048, 2048, 1024])
+middle = width // 2
 f32, bf16, i32 = jnp.float32, jnp.bfloat16, jnp.int32
 
 
@@ -101,26 +101,47 @@
     return copies
 
 
-def logits_kernel(vocab_rows, place_ref, digits_ref, r0, r1, r2, r3, w_ref, v_ref, own_ref, other_ref, stats_ref, rows, weights, sems):
+def weight_copies(chunks, start, w_ref, v_ref, weights):
     pairs = []
-    for start, size in logit_chunks:
-        cols = pl.ds(start, size)
-        pair = [(w_ref.at[:, cols], weights.at[0, :, cols]), (v_ref.at[:, cols], weights.at[1, :, cols])]
+    for at, size in chunks:
+        source, held = pl.ds(start + at, size), pl.ds(at, size)
+        pairs.append([(w_ref.at[:, source], weights.at[0, :, held]), (v_ref.at[:, source], weights.at[1, :, held])])
+    return pairs
+
+
+def logits_kernel(half, vocab_rows, *refs):
+    if half == 0:
+        r0, r1, r2, r3, w_ref, v_ref, own_ref, other_ref, rows, weights, sems = refs
+        chunks = spans([1024, 1024, 2048])
+    else:
+        place_ref, own_in, other_in, r0, r1, r2, r3, w_ref, v_ref = refs[:9]
+        own_ref, other_ref, stats_ref, target_ref, rows, weights, sems = refs[9:]
+        chunks = spans([2048, 1024, 1024])
+    pairs = weight_copies(chunks, half * middle, w_ref, v_ref, weights)
+    for pair, (at, size) in zip(pairs, chunks):
+        size += (wide - width) * (half == 1 and at + size == middle)
+        cols = pl.ds(at, size)
         pair += [(r.at[:, cols], rows.at[pl.ds(k * 32, 32), cols]) for k, r in enumerate((r0, r1, r2, r3))]
-        pairs.append(pair)
     copies = fetch(pairs, sems)
-    for k, (start, size) in enumerate(logit_chunks):
+    for k, (at, size) in enumerate(chunks):
         for copy in copies[k]:
             copy.wait()
-        cols = pl.ds(start, size)
+        cols = pl.ds(at, size)
         for slot, out in enumerate((own_ref, other_ref)):
             part = lax.dot_general(
                 weights[slot, :, cols], rows[:, cols], (((1,), (1,)), ((), ())), preferred_element_type=f32
             )
-            out[...] = part if k == 0 else out[...] + part
+            if k:
+                part = out[...] + part
+            elif half:
+                part = (own_in, other_in)[slot][...] + part
+            out[...] = part
+    if half == 0:
+        return
 
     i, j, me = place_ref[0], place_ref[1], place_ref[2]
-    target = digits_ref[0:1] + 256 * digits_ref[1:2] + 65536 * digits_ref[2:3] - 1
+    digits = rows[:, pl.ds(middle, 128)].astype(f32).T
+    target = (digits[0:1] + 256 * digits[1:2] + 65536 * digits[2:3]).astype(i32) - 1
     top = jnp.maximum(jnp.max(own_ref[...], axis=0, keepdims=True), jnp.max(other_ref[...], axis=0, keepdims=True))
     total, pick = 0.0, 0.0
     for out, base in ((own_ref, me), (other_ref, me ^ 8)):
@@ -130,51 +151,55 @@
     row = lax.broadcasted_iota(i32, (8, 128), 0)
     stats = jnp.where(row == 0, top + jnp.log(total), pick)
     stats_ref[...] = jnp.broadcast_to(by_rank(stats, i, j)[None, :2], stats_ref.shape)
-
-
-def logits_call(place, digits, rows, own, other):
+    target_ref[...] = target
+
+
+def logits_call(half, place, partial, rows, own, other):
     vocab_rows = own.shape[0]
+    partial_shape = [jax.ShapeDtypeStruct((vocab_rows, 128), f32)] * 2
+    stats_shape = [jax.ShapeDtypeStruct((128, 2, 128), f32), jax.ShapeDtypeStruct((1, 128), i32)]
     return pl.pallas_call(
-        functools.partial(logits_kernel, vocab_rows),
-        in_specs=[smem, vmem()] + [anywhere] * 6,
-        out_specs=[vmem()] * 3,
-        out_shape=[jax.ShapeDtypeStruct((vocab_rows, 128), f32)] * 2 + [jax.ShapeDtypeStruct((128, 2, 128), f32)],
+        functools.partial(logits_kernel, half, vocab_rows),
+        in_specs=([smem] + [vmem()] * 2) * half + [anywhere] * 6,
+        out_specs=[vmem()] * (4 if half else 2),
+        out_shape=partial_shape + stats_shape * half,
         scratch_shapes=[
-            pltpu.VMEM((128, width), bf16),
-            pltpu.VMEM((2, vocab_rows, width), bf16),
-            pltpu.SemaphoreType.DMA((len(logit_chunks), 6)),
+            pltpu.VMEM((128, middle + (wide - width) * half), bf16),
+            pltpu.VMEM((2, vocab_rows, middle), bf16),
+            pltpu.SemaphoreType.DMA((3, 6)),
         ],
-        name="logits",
-    )(place, digits, *rows, own, other)
-
-
-def grad_kernel(
-    vocab_rows, place_ref, digits_ref, stats_ref, own_ref, other_ref, w_ref, v_ref, g0, g1, g2, g3, loss_ref, coefs, weights, grads, sems, sent
-):
-    pairs = []
-    for start, size in grad_chunks:
-        cols = pl.ds(start, size)
-        pairs.append([(w_ref.at[:, cols], weights.at[0, :, cols]), (v_ref.at[:, cols], weights.at[1, :, cols])])
-    copies = fetch(pairs, sems)
-
-    i, j, me = place_ref[0], place_ref[1], place_ref[2]
-    lse = stats_ref[:, 0, :]
-    top = jnp.max(lse, axis=0, keepdims=True)
-    log_total = top + jnp.log(jnp.sum(jnp.exp(lse - top), axis=0, keepdims=True))
-    picked = jnp.sum(stats_ref[:, 1, :], axis=0, keepdims=True)
-    target = digits_ref[0:1] + 256 * digits_ref[1:2] + 65536 * digits_ref[2:3] - 1
-    loss_ref[...] = log_total - picked
-    log_total = by_arrival(jnp.broadcast_to(log_total, (8, 128)), i, j)[0:1]
-    for slot, (out, base) in enumerate(((own_ref, me), (other_ref, me ^ 8))):
-        ids = lax.broadcasted_iota(i32, (vocab_rows, 128), 0) + base * vocab_rows
-        hit = (ids == target).astype(f32)
-        coefs[slot] = jnp.where(target >= 0, jnp.exp(out[...] - log_total) - hit, 0.0).T.astype(bf16)
+    )(*(([place] + list(partial)) if half else []), *rows, own, other)
+
+
+def grad_kernel(half, vocab_rows, *refs):
+    if half == 0:
+        place_ref, target_ref, stats_ref, own_ref, other_ref, w_ref, v_ref = refs[:7]
+        g0, g1, g2, g3, loss_ref, coefs, weights, grads, sems, sent = refs[7:]
+        chunks = spans([1024, 2048, 1024])
+    else:
+        coefs, w_ref, v_ref, g0, g1, g2, g3, weights, grads, sems, sent = refs
+        chunks = spans([1024, 2048, 1024])
+    copies = fetch(weight_copies(chunks, half * middle, w_ref, v_ref, weights), sems)
+
+    if half == 0:
+        i, j, me = place_ref[0], place_ref[1], place_ref[2]
+        lse = stats_ref[:, 0, :]
+        top = jnp.max(lse, axis=0, keepdims=True)
+        log_total = top + jnp.log(jnp.sum(jnp.exp(lse - top), axis=0, keepdims=True))
+        picked = jnp.sum(stats_ref[:, 1, :], axis=0, keepdims=True)
+        target = target_ref[...]
+        loss_ref[...] = log_total - picked
+        log_total = by_arrival(jnp.broadcast_to(log_total, (8, 128)), i, j)[0:1]
+        for slot, (out, base) in enumerate(((own_ref, me), (other_ref, me ^ 8))):
+            ids = lax.broadcasted_iota(i32, (vocab_rows, 128), 0) + base * vocab_rows
+            hit = (ids == target).astype(f32)
+            coefs[slot] = jnp.where(target >= 0, jnp.exp(out[...] - log_total) - hit, 0.0).T.astype(bf16)
 
     out_copies = []
-    for k, (start, size) in enumerate(grad_chunks):
+    for k, (at, size) in enumerate(chunks):
         for copy in copies[k]:
             copy.wait()
-        cols = pl.ds(start, size)
+        cols = pl.ds(at, size)
         grad = jnp.dot(coefs[0], weights[0, :, cols], preferred_element_type=f32)
         grad += jnp.dot(coefs[1], weights[1, :, cols], preferred_element_type=f32)
         grads[:, cols] = grad * (loss_scale * send_scale)
@@ -186,22 +211,21 @@
         copy.wait()
 
 
-def grad_call(place, digits, stats, logits, own, other):
+def grad_call(half, args, own, other):
     vocab_rows = own.shape[0]
+    shapes = [jax.ShapeDtypeStruct((1, 128), f32), jax.ShapeDtypeStruct((2, 128, vocab_rows), bf16)]
     return pl.pallas_call(
-        functools.partial(grad_kernel, vocab_rows),
-        in_specs=[smem] + [vmem()] * 4 + [anywhere] * 2,
-        out_specs=[anywhere] * 4 + [vmem()],
-        out_shape=[jax.ShapeDtypeStruct((32, width), f32)] * 4 + [jax.ShapeDtypeStruct((1, 128), f32)],
+        functools.partial(grad_kernel, half, vocab_rows),
+        in_specs=([vmem()] if half else [smem] + [vmem()] * 4) + [anywhere] * 2,
+        out_specs=[anywhere] * 4 + [vmem()] * (0 if half else 2),
+        out_shape=[jax.ShapeDtypeStruct((32, middle), f32)] * 4 + ([] if half else shapes),
         scratch_shapes=[
-            pltpu.VMEM((2, 128, vocab_rows), bf16),
-            pltpu.VMEM((2, vocab_rows, width), bf16),
-            pltpu.VMEM((128, width), f32),
-            pltpu.SemaphoreType.DMA((len(grad_chunks), 2)),
-            pltpu.SemaphoreType.DMA((len(grad_chunks), 4)),
+            pltpu.VMEM((2, vocab_rows, middle), bf16),
+            pltpu.VMEM((128, middle), f32),
+            pltpu.SemaphoreType.DMA((3, 2)),
+            pltpu.SemaphoreType.DMA((3, 4)),
         ],
-        name="grad",
-    )(place, digits, stats, *logits, own, other)
+    )(*args, own, other)
 
 
 def exchange(value, groups):
@@ -226,15 +250,17 @@
     other_weight = lax.ppermute(out_weight, "d", partner)
 
     packed, kept = pack(kept_count, loss_mask, targets, hidden)
-    rows = exchange(packed, along_z).reshape(8, wide)
-    rows = jnp.concatenate(gather4(rows, False), axis=0)
-    rows = gather4(rows, True)
-    digits = jnp.concatenate([r[:, width:width + 4] for r in rows], axis=0).T.astype(i32)
-    *logits, stats = logits_call(place, digits, rows, out_weight, other_weight)
+    rows = gather4(exchange(packed, along_z).reshape(8, wide), False)
+    halves = [jnp.concatenate([r[:, a:b] for r in rows], axis=0) for a, b in ((0, middle), (middle, wide))]
+    first = gather4(halves[0], True)
+    halves = [first, gather4(halves[1], True)]
+    partial = logits_call(0, place, None, halves[0], out_weight, other_weight)
+    *logits, stats, target = logits_call(1, place, partial, halves[1], out_weight, other_weight)
     stats = exchange(stats, same_core)
-    *parts, loss = grad_call(place, digits, stats, logits, out_weight, other_weight)
-    part = reduce4([p.astype(send_type) for p in parts], True)
-    part = part.astype(send_type)
+    *first, loss, coefs = grad_call(0, (place, target, stats, *logits), out_weight, other_weight)
+    second = grad_call(1, (coefs,), out_weight, other_weight)
+    parts = [reduce4([p.astype(send_type) for p in blocks], True) for blocks in (first, second)]
+    part = jnp.concatenate(parts, axis=1).astype(send_type)
     part = reduce4([part[k * 8:(k + 1) * 8] for k in R4], False)
     part = exchange(part.astype(send_type).reshape(8, width // 128, 128), along_z)
     own_grad = (jnp.sum(part.astype(f32), axis=0) * (1.0 / send_scale)).reshape(1, width)

time: 136 us -> 148 us (1.088)
  starting transfers between devices: 20.4 us -> 27.7 us
  Pallas kernels: 21.8 us -> 28.3 us
  waiting for transfers between devices: 44.8 us -> 39.1 us
  other arithmetic: 7.25 us -> 10.5 us
    ppermute x12 -> x18, starting transfers between devices: 16.9 us -> 24.2 us  [shift(): return lax.ppermute(value, 'd', pairs)]
    pallas_call x2 -> x4, Pallas kernels: 19.4 us -> 25.9 us  [the longest x2 13 us: logits_call(): pl.pallas_call(functools.partial(logits_kernel, half, vocab_rows), in_spe...]
    ppermute x12 -> x18, waiting for transfers between devices: 37.6 us -> 32 us  [shift(): return lax.ppermute(value, 'd', pairs)]
    convert_element_type x5 -> x6, other arithmetic: 3.75 us -> 6.5 us  [shards(): p.astype(send_type)]
  transfers between devices with their start and end apart: 14 -> 20, of which waited for: 10 -> 13; matrix products, arithmetic and copies ran while one was open for 3% -> 6% of each run, Pallas kernels for 2% -> 10%
where the time goes in v4:
time: 148 us; the launch traced here: 147 us
  waiting for transfers between devices  39.1 us (26%)
  blocking collectives  37 us (25%)
  Pallas kernels  28.3 us (19%)
  starting transfers between devices  27.7 us (19%)
  other arithmetic  10.5 us (7%)
  local copies, waits for them, and re-layouts  3.08 us (2%)
  between operations  1.61 us (1%)
    all_to_all x2, blocking collectives, exchange(): return lax.all_to_all(value, 'd', 0, 0, axis_index_groups=groups)  37 us
    ppermute x18, waiting for transfers between devices, shift(): return lax.ppermute(value, 'd', pairs)  32 us
    ppermute x18, starting transfers between devices, shift(): return lax.ppermute(value, 'd', pairs)  24.2 us
    pallas_call x2, Pallas kernels, logits_call(): pl.pallas_call(functools.partial(logits_kernel, half, vocab_rows), in_spe...  13 us
    pallas_call x2, Pallas kernels, grad_call(): pl.pallas_call(functools.partial(grad_kernel, half, vocab_rows), in_specs...  12.9 us
    all_to_all x1, waiting for transfers between devices, exchange(): return lax.all_to_all(value, 'd', 0, 0, axis_index_groups=groups)  7.11 us
    convert_element_type x6, other arithmetic, shards(): p.astype(send_type)  6.5 us
    all_to_all x1, starting transfers between devices, exchange(): return lax.all_to_all(value, 'd', 0, 0, axis_index_groups=groups)  3.37 us
  transfers between devices with their start and end apart: 20, of which 13 were waited for; matrix products, arithmetic and copies ran while one was open for 6% of the time, Pallas kernels for 10%

profile of v4, /device:TPU:2, one launch (start us, length us, event | category | flops | bytes accessed | tf_op | source)
XLA Modules:
  0.0 147.4 jit_solution(13752041463919085559)
XLA Ops:
  0.6 0.1 collective-permute-start.6
  1.4 2.5 %pack.1 = (bf16[8,2,4224]{2,1,0:T(2,128)(2,1)}, s32[1,128]{1,0:T(1,128)}) custom-call(s32[1]{0:T(128)S(6)} %copy.9.count_ref, s32[1,128]{1,0:T(1,128)} %bitcast.22, s32[1,128]{1,0:T(1,128)} %bitcast.23, bf16[128,8192]{1,0:T(8,128)(2,1)} %hidden_ref.1), custom_call_target="tpu_custom_call" | custom-call | tf_op jit(solution)/shard_map/pack/pallas_call | solution.py:74
  3.9 18.3 %all_to_all.15 = bf16[8,2,4224]{2,1,0:T(2,128)(2,1)S(1)} all-to-all(bf16[8,2,4224]{2,1,0:T(2,128)(2,1)} %get-tuple-element.21), channel_id=1, replica_groups={{0,1,2,3,4,5,6,7},{8,9,10,11,12,13,14,15},{16,17,18,19,20,21,22,23},{24..., dimensions={0} | all-to-all | bytes 270336 | tf_op jit(solution)/shard_map/all_to_all | solution.py:232
  22.2 1.6 %collective-permute-start.2 = (bf16[8,8448]{1,0:T(8,128)(2,1)S(1)}, bf16[8,8448]{1,0:T(8,128)(2,1)S(1)}, u32[]{:S(2)}, u32[]{:S(2)}) collective-permute-start(bf16[8,8448]{1,0:T(8,128)(2,1)S(1)} %bitcast.16), channel_id=1, source_target_pairs={{0,64},{1,65},{2,66},{3,67},{4,68},{5,69},{6,70},{7,71},{8,24},{9,... | collective-permute-start | bytes 405512 | tf_op jit(solution)/shard_map/ppermute | solution.py:42
  23.7 1.1 collective-permute-start.1
  24.8 2.2 %collective-permute-start = (bf16[8,8448]{1,0:T(8,128)(2,1)S(1)}, bf16[8,8448]{1,0:T(8,128)(2,1)S(1)}, u32[]{:S(2)}, u32[]{:S(2)}) collective-permute-start(bf16[8,8448]{1,0:T(8,128)(2,1)S(1)} %bitcast.18), channel_id=1, source_target_pairs={{0,192},{1,193},{2,194},{3,195},{4,196},{5,197},{6,198},{7,199},{8... | collective-permute-start | bytes 405512 | tf_op jit(solution)/shard_map/ppermute | solution.py:42
  27.0 0.2 collective-permute-done.2
  27.3 3.1 %collective-permute-done.1 = bf16[8,8448]{1,0:T(8,128)(2,1)S(1)} collective-permute-done((bf16[8,8448]{1,0:T(8,128)(2,1)S(1)}, bf16[8,8448]{1,0:T(8,128)(2,1)S(1)}, u32[]{:S(2)}, u32[]{:S(2)}) %collective-permute-start.1) | collective-permute-done | bytes 135200 | tf_op jit(solution)/shard_map/ppermute | solution.py:42
  30.4 0.9 collective-permute-done
  31.3 3.2 %collective-permute-start.3 = (bf16[32,4096]{1,0:T(8,128)(2,1)S(1)}, bf16[32,4096]{1,0:T(8,128)(2,1)S(1)}, u32[]{:S(2)}, u32[]{:S(2)}) collective-permute-start(bf16[32,4096]{1,0:T(8,128)(2,1)S(1)} %pad_maximum_fusion.1.refs_0_), channel_id=1, source_target_pairs={{0,48},{1,49},{2,50},{3,51},{4,52},{5,53},{6,54},{7,55},{8,200},{9... | collective-permute-start | bytes 786440 | tf_op jit(solution)/shard_map/ppermute | solution.py:42
  34.5 0.6 collective-permute-start.4
  35.1 0.0 copy-start
  35.1 1.1 collective-permute-start.7
  36.3 2.0 %collective-permute-start.8 = (bf16[32,4352]{1,0:T(8,128)(2,1)S(1)}, bf16[32,4352]{1,0:T(8,128)(2,1)S(1)}, u32[]{:S(2)}, u32[]{:S(2)}) collective-permute-start(bf16[32,4352]{1,0:T(8,128)(2,1)S(1)} %pad_maximum_fusion.refs_3_), channel_id=1, source_target_pairs={{0,32},{1,33},{2,34},{3,35},{4,36},{5,37},{6,38},{7,39},{8,136},{9... | collective-permute-start | bytes 835592 | tf_op jit(solution)/shard_map/ppermute | solution.py:42
  38.3 2.9 %collective-permute-done.3.refs_1_ = bf16[32,4096]{1,0:T(8,128)(2,1)S(1)} collective-permute-done((bf16[32,4096]{1,0:T(8,128)(2,1)S(1)}, bf16[32,4096]{1,0:T(8,128)(2,1)S(1)}, u32[]{:S(2)}, u32[]{:S(2)}) %collective-permute-start.3) | collective-permute-done | bytes 262176 | tf_op jit(solution)/shard_map/ppermute | solution.py:42
  41.2 0.0 collective-permute-start.9
  41.2 1.2 collective-permute-done.4.refs_2_
  42.4 0.9 collective-permute-start.5
  43.3 0.7 pad_add_fusion.refs_0_
  44.0 8.3 %collective-permute-done.5.refs_3_ = bf16[32,4096]{1,0:T(8,128)(2,1)S(1)} collective-permute-done((bf16[32,4096]{1,0:T(8,128)(2,1)S(1)}, bf16[32,4096]{1,0:T(8,128)(2,1)S(1)}, u32[]{:S(2)}, u32[]{:S(2)}) %collective-permute-start.5) | collective-permute-done | bytes 262176 | tf_op jit(solution)/shard_map/ppermute | solution.py:42
  52.3 0.7 copy-done.9
  53.0 5.8 %shard_map.68 = (f32[501,128]{1,0:T(8,128)}, f32[501,128]{1,0:T(8,128)}) custom-call(bf16[32,4096]{1,0:T(8,128)(2,1)} %copy-done.1, bf16[32,4096]{1,0:T(8,128)(2,1)} %copy-done.7, bf16[32,4096]{1,0:T(8,128)(2,1)} %copy-done.8, bf16[32,4096]{1,0:T(8,128)(2,1)} %copy-done.9, bf16[501,8192]{1,0:T(8,128)(2,1)} %refs_1_.1, ...), custom_call_target="tpu_custom_call" | custom-call | tf_op jit(solution)/shard_map/pallas_call | solution.py:161
  58.8 0.0 collective-permute-done.7.refs_4_
  58.9 0.7 copy-done.4
  59.5 0.2 copy-done.5
  59.7 0.1 copy-done.6
  59.8 7.2 %shard_map.69 = (f32[501,128]{1,0:T(8,128)}, f32[501,128]{1,0:T(8,128)}, f32[128,2,128]{2,1,0:T(2,128)}, s32[1,128]{1,0:T(1,128)}) custom-call(s32[3]{0:T(128)} %pad_add_fusion.refs_0_, f32[501,128]{1,0:T(8,128)} %get-tuple-element.22.refs_1_, f32[501,128]{1,0:T(8,128)} %get-tuple-element.23.refs_2_, bf16[32,4352]{1,0:T(8,128)(2,1)} %copy-done, ...), custom_call_target="tpu_custom_call" | custom-call | tf_op jit(solution)/shard_map/pallas_call | solution.py:161
  67.0 18.7 %all_to_all.16.refs_2_ = f32[128,2,128]{2,1,0:T(2,128)} all-to-all(f32[128,2,128]{2,1,0:T(2,128)} %get-tuple-element.25), channel_id=1, replica_groups={{0,1,2,3,4,5,6,7,16,17,18,19,20,21,22,23,32,33,34,35,36,37,38,39,48,49,..., dimensions={0} | all-to-all | bytes 262144 | tf_op jit(solution)/shard_map/all_to_all | solution.py:232
  85.7 6.9 %shard_map.70 = (f32[32,4096]{1,0:T(8,128)}, f32[32,4096]{1,0:T(8,128)}, f32[32,4096]{1,0:T(8,128)}, f32[32,4096]{1,0:T(8,128)}, f32[1,128]{1,0:T(1,128)}, /*index=5*/bf16[2,128,501]{2,1,0:T(8,128)(2,1)}) custom-call(s32[3]{0:T(128)} %pad_add_fusion.refs_0_, s32[1,128]{1,0:T(1,128)} %get-tuple-element.24.refs_1_, f32[128,2,128]{2,1,0:T(2,128)} %all_to_all.16.refs_2_, ...), custom_call_target="tpu_custom_call" | custom-call | tf_op jit(solution)/shard_map/pallas_call | solution.py:217
  92.7 1.1 convert_element_type.76
  93.7 1.5 %collective-permute-start.12 = (f16[32,4096]{1,0:T(8,128)(2,1)S(1)}, f16[32,4096]{1,0:T(8,128)(2,1)S(1)}, u32[]{:S(2)}, u32[]{:S(2)}) collective-permute-start(f16[32,4096]{1,0:T(8,128)(2,1)S(1)} %convert_element_type.76), channel_id=1, source_target_pairs={{0,48},{1,49},{2,50},{3,51},{4,52},{5,53},{6,54},{7,55},{8,200},{9... | collective-permute-start | bytes 786440 | tf_op jit(solution)/shard_map/ppermute | solution.py:42
  95.2 1.1 convert_element_type.74
  96.3 1.1 collective-permute-start.11
  97.4 1.1 convert_element_type.72
  98.5 0.9 collective-permute-start.10
  99.4 6.0 %shard_map.71 = (f32[32,4096]{1,0:T(8,128)}, f32[32,4096]{1,0:T(8,128)}, f32[32,4096]{1,0:T(8,128)}, f32[32,4096]{1,0:T(8,128)}) custom-call(bf16[2,128,501]{2,1,0:T(8,128)(2,1)} %get-tuple-element.32.refs_0_, bf16[501,8192]{1,0:T(8,128)(2,1)} %refs_1_.1, bf16[501,8192]{1,0:T(8,128)(2,1)} %collective-permute-done.6.refs_5_.refs_8_.refs_6_.refs_2_), custom_call_target="tpu_custom_call" | custom-call | tf_op jit(solution)/shard_map/pallas_call | solution.py:217
  105.3 0.0 copy-start.2
  105.4 1.2 convert_element_type.84
  106.5 2.5 %collective-permute-start.15 = (f16[32,4096]{1,0:T(8,128)(2,1)S(1)}, f16[32,4096]{1,0:T(8,128)(2,1)S(1)}, u32[]{:S(2)}, u32[]{:S(2)}) collective-permute-start(f16[32,4096]{1,0:T(8,128)(2,1)S(1)} %convert_element_type.84), channel_id=1, source_target_pairs={{0,48},{1,49},{2,50},{3,51},{4,52},{5,53},{6,54},{7,55},{8,200},{9... | collective-permute-start | bytes 786440 | tf_op jit(solution)/shard_map/ppermute | solution.py:42
  109.0 1.1 convert_element_type.82
  110.1 1.4 collective-permute-start.14
  111.5 1.1 convert_element_type.80
  112.5 0.7 collective-permute-start.13
  113.2 0.0 collective-permute-done.11
  113.2 0.0 collective-permute-done.10
  113.2 0.1 add_convert_fusion.1
  113.4 1.9 %collective-permute-done.15 = f16[32,4096]{1,0:T(8,128)(2,1)S(1)} collective-permute-done((f16[32,4096]{1,0:T(8,128)(2,1)S(1)}, f16[32,4096]{1,0:T(8,128)(2,1)S(1)}, u32[]{:S(2)}, u32[]{:S(2)}) %collective-permute-start.15) | collective-permute-done | bytes 262176 | tf_op jit(solution)/shard_map/ppermute | solution.py:42
  115.3 3.4 %collective-permute-done.14 = f16[32,4096]{1,0:T(8,128)(2,1)S(1)} collective-permute-done((f16[32,4096]{1,0:T(8,128)(2,1)S(1)}, f16[32,4096]{1,0:T(8,128)(2,1)S(1)}, u32[]{:S(2)}, u32[]{:S(2)}) %collective-permute-start.14) | collective-permute-done | bytes 262176 | tf_op jit(solution)/shard_map/ppermute | solution.py:42
  118.7 5.0 %collective-permute-done.13 = f16[32,4096]{1,0:T(8,128)(2,1)S(1)} collective-permute-done((f16[32,4096]{1,0:T(8,128)(2,1)S(1)}, f16[32,4096]{1,0:T(8,128)(2,1)S(1)}, u32[]{:S(2)}, u32[]{:S(2)}) %collective-permute-start.13) | collective-permute-done | bytes 262176 | tf_op jit(solution)/shard_map/ppermute | solution.py:42
  123.7 0.1 add_convert_fusion
  123.8 0.1 fusion.3
  123.9 1.9 %collective-permute-start.18 = (f16[8,8192]{1,0:T(8,128)(2,1)S(1)}, f16[8,8192]{1,0:T(8,128)(2,1)S(1)}, u32[]{:S(2)}, u32[]{:S(2)}) collective-permute-start(f16[8,8192]{1,0:T(8,128)(2,1)S(1)} %get-tuple-element.39), channel_id=1, source_target_pairs={{0,192},{1,193},{2,194},{3,195},{4,196},{5,197},{6,198},{7,199},{8... | collective-permute-start | bytes 393224 | tf_op jit(solution)/shard_map/ppermute | solution.py:42
  125.8 0.9 collective-permute-start.17
  126.7 0.8 collective-permute-start.16
  127.5 1.5 %collective-permute-done.18 = f16[8,8192]{1,0:T(8,128)(2,1)S(1)} collective-permute-done((f16[8,8192]{1,0:T(8,128)(2,1)S(1)}, f16[8,8192]{1,0:T(8,128)(2,1)S(1)}, u32[]{:S(2)}, u32[]{:S(2)}) %collective-permute-start.18) | collective-permute-done | bytes 131104 | tf_op jit(solution)/shard_map/ppermute | solution.py:42
  129.0 3.3 %collective-permute-done.17 = f16[8,8192]{1,0:T(8,128)(2,1)S(1)} collective-permute-done((f16[8,8192]{1,0:T(8,128)(2,1)S(1)}, f16[8,8192]{1,0:T(8,128)(2,1)S(1)}, u32[]{:S(2)}, u32[]{:S(2)}) %collective-permute-start.17) | collective-permute-done | bytes 131104 | tf_op jit(solution)/shard_map/ppermute | solution.py:42
  132.3 0.2 collective-permute-done.16
  132.5 0.1 fusion
  132.6 0.7 copy.7
  133.3 3.4 %all-to-all-start.2 = ((f16[8,64,128]{2,1,0:T(8,128)(2,1)}), f16[8,64,128]{2,1,0:T(8,128)(2,1)S(1)}, u32[]{:S(2)}, u32[]{:S(2)}) async-start(f16[8,64,128]{2,1,0:T(8,128)(2,1)} %copy.7), calls=%async_computation.2 | async-start | bytes 262144 | tf_op jit(solution)/shard_map/all_to_all | solution.py:232
  136.7 0.6 constant_dynamic-slice_fusion
  137.4 1.2 broadcast_select_fusion
  138.6 7.1 %all-to-all-done.2 = f16[8,64,128]{2,1,0:T(8,128)(2,1)S(1)} async-done(((f16[8,64,128]{2,1,0:T(8,128)(2,1)}), f16[8,64,128]{2,1,0:T(8,128)(2,1)S(1)}, u32[]{:S(2)}, u32[]{:S(2)}) %all-to-all-start.2) | async-done | bytes 131104 | tf_op jit(solution)/shard_map/all_to_all | solution.py:232
  145.7 1.7 %select_convert_fusion = bf16[128,8192]{1,0:T(8,128)(2,1)} fusion(bf16[8192]{0:T(1024)(128)(2,1)S(1)} %multiply_bitcast_fusion, pred[128]{0:T(512)(128)(4,1)S(1)} %compare_bitcast_fusion), kind=kLoop, calls=%fused_computation | loop fusion | flops 1048576 | bytes 2113664 | tf_op jit(solution)/shard_map/convert_element_type | solution.py:270
  (36 shorter events, 0.2 us)
Async XLA Ops:
  0.6 51.6 %collective-permute-start.6 = (bf16[501,8192]{1,0:T(8,128)(2,1)}, bf16[501,8192]{1,0:T(8,128)(2,1)}, u32[]{:S(2)}, u32[]{:S(2)}) collective-permute-start(bf16[501,8192]{1,0:T(8,128)(2,1)} %refs_1_.1), channel_id=1, source_target_pairs={{0,8},{1,9},{2,10},{3,11},{4,12},{5,13},{6,14},{7,15},{8,0},{9,1},... | collective-permute-start | bytes 24625160 | tf_op jit(solution)/shard_map/ppermute | solution.py:250
  22.2 5.1 %collective-permute-start.2 = (bf16[8,8448]{1,0:T(8,128)(2,1)S(1)}, bf16[8,8448]{1,0:T(8,128)(2,1)S(1)}, u32[]{:S(2)}, u32[]{:S(2)}) collective-permute-start(bf16[8,8448]{1,0:T(8,128)(2,1)S(1)} %bitcast.16), channel_id=1, source_target_pairs={{0,64},{1,65},{2,66},{3,67},{4,68},{5,69},{6,70},{7,71},{8,24},{9,... | collective-permute-start | bytes 405512 | tf_op jit(solution)/shard_map/ppermute | solution.py:42
  23.7 6.6 %collective-permute-start.1 = (bf16[8,8448]{1,0:T(8,128)(2,1)S(1)}, bf16[8,8448]{1,0:T(8,128)(2,1)S(1)}, u32[]{:S(2)}, u32[]{:S(2)}) collective-permute-start(bf16[8,8448]{1,0:T(8,128)(2,1)S(1)} %bitcast.17), channel_id=1, source_target_pairs={{0,128},{1,129},{2,130},{3,131},{4,132},{5,133},{6,134},{7,135},{8... | collective-permute-start | bytes 405512 | tf_op jit(solution)/shard_map/ppermute | solution.py:42
  24.8 6.5 %collective-permute-start = (bf16[8,8448]{1,0:T(8,128)(2,1)S(1)}, bf16[8,8448]{1,0:T(8,128)(2,1)S(1)}, u32[]{:S(2)}, u32[]{:S(2)}) collective-permute-start(bf16[8,8448]{1,0:T(8,128)(2,1)S(1)} %bitcast.18), channel_id=1, source_target_pairs={{0,192},{1,193},{2,194},{3,195},{4,196},{5,197},{6,198},{7,199},{8... | collective-permute-start | bytes 405512 | tf_op jit(solution)/shard_map/ppermute | solution.py:42
  31.3 20.9 %copy-start.1 = (bf16[32,4096]{1,0:T(8,128)(2,1)}, bf16[32,4096]{1,0:T(8,128)(2,1)S(1)}, u32[]{:S(2)}) copy-start(bf16[32,4096]{1,0:T(8,128)(2,1)S(1)} %pad_maximum_fusion.1.refs_0_) | copy-start | bytes 786436
  31.3 9.9 %collective-permute-start.3 = (bf16[32,4096]{1,0:T(8,128)(2,1)S(1)}, bf16[32,4096]{1,0:T(8,128)(2,1)S(1)}, u32[]{:S(2)}, u32[]{:S(2)}) collective-permute-start(bf16[32,4096]{1,0:T(8,128)(2,1)S(1)} %pad_maximum_fusion.1.refs_0_), channel_id=1, source_target_pairs={{0,48},{1,49},{2,50},{3,51},{4,52},{5,53},{6,54},{7,55},{8,200},{9... | collective-permute-start | bytes 786440 | tf_op jit(solution)/shard_map/ppermute | solution.py:42
  34.5 7.9 %collective-permute-start.4 = (bf16[32,4096]{1,0:T(8,128)(2,1)S(1)}, bf16[32,4096]{1,0:T(8,128)(2,1)S(1)}, u32[]{:S(2)}, u32[]{:S(2)}) collective-permute-start(bf16[32,4096]{1,0:T(8,128)(2,1)S(1)} %pad_maximum_fusion.1.refs_0_), channel_id=1, source_target_pairs={{0,32},{1,33},{2,34},{3,35},{4,36},{5,37},{6,38},{7,39},{8,136},{9... | collective-permute-start | bytes 786440 | tf_op jit(solution)/shard_map/ppermute | solution.py:42
  35.1 23.7 %copy-start = (bf16[32,4352]{1,0:T(8,128)(2,1)}, bf16[32,4352]{1,0:T(8,128)(2,1)S(1)}, u32[]{:S(2)}) copy-start(bf16[32,4352]{1,0:T(8,128)(2,1)S(1)} %pad_maximum_fusion.refs_3_) | copy-start | bytes 835588
  35.1 23.7 %collective-permute-start.7 = (bf16[32,4352]{1,0:T(8,128)(2,1)S(1)}, bf16[32,4352]{1,0:T(8,128)(2,1)S(1)}, u32[]{:S(2)}, u32[]{:S(2)}) collective-permute-start(bf16[32,4352]{1,0:T(8,128)(2,1)S(1)} %pad_maximum_fusion.refs_3_), channel_id=1, source_target_pairs={{0,48},{1,49},{2,50},{3,51},{4,52},{5,53},{6,54},{7,55},{8,200},{9... | collective-permute-start | bytes 835592 | tf_op jit(solution)/shard_map/ppermute | solution.py:42
  36.3 22.5 %collective-permute-start.8 = (bf16[32,4352]{1,0:T(8,128)(2,1)S(1)}, bf16[32,4352]{1,0:T(8,128)(2,1)S(1)}, u32[]{:S(2)}, u32[]{:S(2)}) collective-permute-start(bf16[32,4352]{1,0:T(8,128)(2,1)S(1)} %pad_maximum_fusion.refs_3_), channel_id=1, source_target_pairs={{0,32},{1,33},{2,34},{3,35},{4,36},{5,37},{6,38},{7,39},{8,136},{9... | collective-permute-start | bytes 835592 | tf_op jit(solution)/shard_map/ppermute | solution.py:42
  41.2 11.0 %copy-start.7 = (bf16[32,4096]{1,0:T(8,128)(2,1)}, bf16[32,4096]{1,0:T(8,128)(2,1)S(1)}, u32[]{:S(2)}) copy-start(bf16[32,4096]{1,0:T(8,128)(2,1)S(1)} %collective-permute-done.3.refs_1_) | copy-start | bytes 786436
  41.2 17.6 %collective-permute-start.9 = (bf16[32,4352]{1,0:T(8,128)(2,1)S(1)}, bf16[32,4352]{1,0:T(8,128)(2,1)S(1)}, u32[]{:S(2)}, u32[]{:S(2)}) collective-permute-start(bf16[32,4352]{1,0:T(8,128)(2,1)S(1)} %pad_maximum_fusion.refs_3_), channel_id=1, source_target_pairs={{0,16},{1,17},{2,18},{3,19},{4,20},{5,21},{6,22},{7,23},{8,72},{9,... | collective-permute-start | bytes 835592 | tf_op jit(solution)/shard_map/ppermute | solution.py:42
  42.4 9.9 %copy-start.8 = (bf16[32,4096]{1,0:T(8,128)(2,1)}, bf16[32,4096]{1,0:T(8,128)(2,1)S(1)}, u32[]{:S(2)}) copy-start(bf16[32,4096]{1,0:T(8,128)(2,1)S(1)} %collective-permute-done.4.refs_2_) | copy-start | bytes 786436
  42.4 9.8 %collective-permute-start.5 = (bf16[32,4096]{1,0:T(8,128)(2,1)S(1)}, bf16[32,4096]{1,0:T(8,128)(2,1)S(1)}, u32[]{:S(2)}, u32[]{:S(2)}) collective-permute-start(bf16[32,4096]{1,0:T(8,128)(2,1)S(1)} %pad_maximum_fusion.1.refs_0_), channel_id=1, source_target_pairs={{0,16},{1,17},{2,18},{3,19},{4,20},{5,21},{6,22},{7,23},{8,72},{9,... | collective-permute-start | bytes 786440 | tf_op jit(solution)/shard_map/ppermute | solution.py:42
  52.2 0.7 copy-start.9
  58.8 0.7 copy-start.4
  58.8 0.9 copy-start.5
  58.8 1.0 copy-start.6
  93.7 18.8 %collective-permute-start.12 = (f16[32,4096]{1,0:T(8,128)(2,1)S(1)}, f16[32,4096]{1,0:T(8,128)(2,1)S(1)}, u32[]{:S(2)}, u32[]{:S(2)}) collective-permute-start(f16[32,4096]{1,0:T(8,128)(2,1)S(1)} %convert_element_type.76), channel_id=1, source_target_pairs={{0,48},{1,49},{2,50},{3,51},{4,52},{5,53},{6,54},{7,55},{8,200},{9... | collective-permute-start | bytes 786440 | tf_op jit(solution)/shard_map/ppermute | solution.py:42
  96.3 16.9 %collective-permute-start.11 = (f16[32,4096]{1,0:T(8,128)(2,1)S(1)}, f16[32,4096]{1,0:T(8,128)(2,1)S(1)}, u32[]{:S(2)}, u32[]{:S(2)}) collective-permute-start(f16[32,4096]{1,0:T(8,128)(2,1)S(1)} %convert_element_type.74), channel_id=1, source_target_pairs={{0,32},{1,33},{2,34},{3,35},{4,36},{5,37},{6,38},{7,39},{8,136},{9... | collective-permute-start | bytes 786440 | tf_op jit(solution)/shard_map/ppermute | solution.py:42
  98.5 14.7 %collective-permute-start.10 = (f16[32,4096]{1,0:T(8,128)(2,1)S(1)}, f16[32,4096]{1,0:T(8,128)(2,1)S(1)}, u32[]{:S(2)}, u32[]{:S(2)}) collective-permute-start(f16[32,4096]{1,0:T(8,128)(2,1)S(1)} %convert_element_type.72), channel_id=1, source_target_pairs={{0,16},{1,17},{2,18},{3,19},{4,20},{5,21},{6,22},{7,23},{8,72},{9,... | collective-permute-start | bytes 786440 | tf_op jit(solution)/shard_map/ppermute | solution.py:42
  105.3 7.9 %copy-start.2 = (f32[32,4096]{1,0:T(8,128)S(1)}, f32[32,4096]{1,0:T(8,128)}, u32[]{:S(2)}) copy-start(f32[32,4096]{1,0:T(8,128)} %get-tuple-element.28) | copy-start | bytes 1572868
  105.3 18.3 %copy-start.3 = (f32[32,4096]{1,0:T(8,128)S(1)}, f32[32,4096]{1,0:T(8,128)}, u32[]{:S(2)}) copy-start(f32[32,4096]{1,0:T(8,128)} %get-tuple-element.33) | copy-start | bytes 1572868
  106.5 8.8 %collective-permute-start.15 = (f16[32,4096]{1,0:T(8,128)(2,1)S(1)}, f16[32,4096]{1,0:T(8,128)(2,1)S(1)}, u32[]{:S(2)}, u32[]{:S(2)}) collective-permute-start(f16[32,4096]{1,0:T(8,128)(2,1)S(1)} %convert_element_type.84), channel_id=1, source_target_pairs={{0,48},{1,49},{2,50},{3,51},{4,52},{5,53},{6,54},{7,55},{8,200},{9... | collective-permute-start | bytes 786440 | tf_op jit(solution)/shard_map/ppermute | solution.py:42
  110.1 8.6 %collective-permute-start.14 = (f16[32,4096]{1,0:T(8,128)(2,1)S(1)}, f16[32,4096]{1,0:T(8,128)(2,1)S(1)}, u32[]{:S(2)}, u32[]{:S(2)}) collective-permute-start(f16[32,4096]{1,0:T(8,128)(2,1)S(1)} %convert_element_type.82), channel_id=1, source_target_pairs={{0,32},{1,33},{2,34},{3,35},{4,36},{5,37},{6,38},{7,39},{8,136},{9... | collective-permute-start | bytes 786440 | tf_op jit(solution)/shard_map/ppermute | solution.py:42
  112.5 11.1 %collective-permute-start.13 = (f16[32,4096]{1,0:T(8,128)(2,1)S(1)}, f16[32,4096]{1,0:T(8,128)(2,1)S(1)}, u32[]{:S(2)}, u32[]{:S(2)}) collective-permute-start(f16[32,4096]{1,0:T(8,128)(2,1)S(1)} %convert_element_type.80), channel_id=1, source_target_pairs={{0,16},{1,17},{2,18},{3,19},{4,20},{5,21},{6,22},{7,23},{8,72},{9,... | collective-permute-start | bytes 786440 | tf_op jit(solution)/shard_map/ppermute | solution.py:42
  113.4 23.3 %copy-start.10 = (s32[1,128]{1,0:T(1,128)S(1)}, s32[1,128]{1,0:T(1,128)}, u32[]{:S(2)}) copy-start(s32[1,128]{1,0:T(1,128)} %get-tuple-element.20) | copy-start | bytes 1540
  113.4 23.3 %copy-start.11 = (f32[1,128]{1,0:T(1,128)S(1)}, f32[1,128]{1,0:T(1,128)}, u32[]{:S(2)}) copy-start(f32[1,128]{1,0:T(1,128)} %get-tuple-element.37) | copy-start | bytes 1540
  123.9 5.0 %collective-permute-start.18 = (f16[8,8192]{1,0:T(8,128)(2,1)S(1)}, f16[8,8192]{1,0:T(8,128)(2,1)S(1)}, u32[]{:S(2)}, u32[]{:S(2)}) collective-permute-start(f16[8,8192]{1,0:T(8,128)(2,1)S(1)} %get-tuple-element.39), channel_id=1, source_target_pairs={{0,192},{1,193},{2,194},{3,195},{4,196},{5,197},{6,198},{7,199},{8... | collective-permute-start | bytes 393224 | tf_op jit(solution)/shard_map/ppermute | solution.py:42
  125.8 6.5 %collective-permute-start.17 = (f16[8,8192]{1,0:T(8,128)(2,1)S(1)}, f16[8,8192]{1,0:T(8,128)(2,1)S(1)}, u32[]{:S(2)}, u32[]{:S(2)}) collective-permute-start(f16[8,8192]{1,0:T(8,128)(2,1)S(1)} %get-tuple-element.40), channel_id=1, source_target_pairs={{0,128},{1,129},{2,130},{3,131},{4,132},{5,133},{6,134},{7,135},{8... | collective-permute-start | bytes 393224 | tf_op jit(solution)/shard_map/ppermute | solution.py:42
  126.7 5.8 %collective-permute-start.16 = (f16[8,8192]{1,0:T(8,128)(2,1)S(1)}, f16[8,8192]{1,0:T(8,128)(2,1)S(1)}, u32[]{:S(2)}, u32[]{:S(2)}) collective-permute-start(f16[8,8192]{1,0:T(8,128)(2,1)S(1)} %get-tuple-element.38), channel_id=1, source_target_pairs={{0,64},{1,65},{2,66},{3,67},{4,68},{5,69},{6,70},{7,71},{8,24},{9,... | collective-permute-start | bytes 393224 | tf_op jit(solution)/shard_map/ppermute | solution.py:42
  133.3 12.4 %all-to-all-start.2 = ((f16[8,64,128]{2,1,0:T(8,128)(2,1)}), f16[8,64,128]{2,1,0:T(8,128)(2,1)S(1)}, u32[]{:S(2)}, u32[]{:S(2)}) async-start(f16[8,64,128]{2,1,0:T(8,128)(2,1)} %copy.7), calls=%async_computation.2 | async-start | bytes 262144 | tf_op jit(solution)/shard_map/all_to_all | solution.py:232

commit v5 on v4

--- a/solution.py
+++ b/solution.py
@@ -78,7 +78,11 @@
         out_shape=[jax.ShapeDtypeStruct((8, 2, wide // 2), bf16), jax.ShapeDtypeStruct((1, 128), i32)],
         scratch_shapes=[pltpu.VMEM((8, width), bf16), pltpu.SemaphoreType.DMA],
         name="pack",
-    )(count, mask.reshape(1, 128), target.reshape(1, 128), hidden)
+    )(count, mask.reshape(1, 128), target.reshape(1, 128), far(hidden))
+
+
+def far(value):
+    return pltpu.with_memory_space_constraint(value, pltpu.HBM)
 
 
 def by_rank(values, i, j):
@@ -105,22 +109,22 @@
     pairs = []
     for at, size in chunks:
         source, held = pl.ds(start + at, size), pl.ds(at, size)
-        pairs.append([(w_ref.at[:, source], weights.at[0, :, held]), (v_ref.at[:, source], weights.at[1, :, held])])
+        pairs.append([(w_ref.at[:, source], weights[0].at[:, held]), (v_ref.at[:, source], weights[1].at[:, held])])
     return pairs
 
 
 def logits_kernel(half, vocab_rows, *refs):
     if half == 0:
-        r0, r1, r2, r3, w_ref, v_ref, own_ref, other_ref, rows, weights, sems = refs
+        r0, r1, r2, r3, w_ref, v_ref, own_ref, other_ref, *weights, rows, sems = refs
         chunks = spans([1024, 1024, 2048])
     else:
         place_ref, own_in, other_in, r0, r1, r2, r3, w_ref, v_ref = refs[:9]
-        own_ref, other_ref, stats_ref, target_ref, rows, weights, sems = refs[9:]
+        own_ref, other_ref, *weights, stats_ref, target_ref, rows, sems = refs[9:]
         chunks = spans([2048, 1024, 1024])
     pairs = weight_copies(chunks, half * middle, w_ref, v_ref, weights)
     for pair, (at, size) in zip(pairs, chunks):
-        size += (wide - width) * (half == 1 and at + size == middle)
-        cols = pl.ds(at, size)
+        extra = (wide - width) * (half == 1 and at + size == middle)
+        cols = pl.ds(at, size + extra)
         pair += [(r.at[:, cols], rows.at[pl.ds(k * 32, 32), cols]) for k, r in enumerate((r0, r1, r2, r3))]
     copies = fetch(pairs, sems)
     for k, (at, size) in enumerate(chunks):
@@ -129,7 +133,7 @@
         cols = pl.ds(at, size)
         for slot, out in enumerate((own_ref, other_ref)):
             part = lax.dot_general(
-                weights[slot, :, cols], rows[:, cols], (((1,), (1,)), ((), ())), preferred_element_type=f32
+                weights[slot][:, cols], rows[:, cols], (((1,), (1,)), ((), ())), preferred_element_type=f32
             )
             if k:
                 part = out[...] + part
@@ -156,76 +160,46 @@
 
 def logits_call(half, place, partial, rows, own, other):
     vocab_rows = own.shape[0]
-    partial_shape = [jax.ShapeDtypeStruct((vocab_rows, 128), f32)] * 2
+    partial_shape = [jax.ShapeDtypeStruct((vocab_rows, 128), f32)] * 2 + [pltpu.VMEM((vocab_rows, middle), bf16)] * 2
     stats_shape = [jax.ShapeDtypeStruct((128, 2, 128), f32), jax.ShapeDtypeStruct((1, 128), i32)]
     return pl.pallas_call(
         functools.partial(logits_kernel, half, vocab_rows),
         in_specs=([smem] + [vmem()] * 2) * half + [anywhere] * 6,
-        out_specs=[vmem()] * (4 if half else 2),
+        out_specs=[vmem()] * (6 if half else 4),
         out_shape=partial_shape + stats_shape * half,
         scratch_shapes=[
             pltpu.VMEM((128, middle + (wide - width) * half), bf16),
-            pltpu.VMEM((2, vocab_rows, middle), bf16),
             pltpu.SemaphoreType.DMA((3, 6)),
         ],
-    )(*(([place] + list(partial)) if half else []), *rows, own, other)
-
-
-def grad_kernel(half, vocab_rows, *refs):
-    if half == 0:
-        place_ref, target_ref, stats_ref, own_ref, other_ref, w_ref, v_ref = refs[:7]
-        g0, g1, g2, g3, loss_ref, coefs, weights, grads, sems, sent = refs[7:]
-        chunks = spans([1024, 2048, 1024])
-    else:
-        coefs, w_ref, v_ref, g0, g1, g2, g3, weights, grads, sems, sent = refs
-        chunks = spans([1024, 2048, 1024])
-    copies = fetch(weight_copies(chunks, half * middle, w_ref, v_ref, weights), sems)
-
-    if half == 0:
-        i, j, me = place_ref[0], place_ref[1], place_ref[2]
-        lse = stats_ref[:, 0, :]
-        top = jnp.max(lse, axis=0, keepdims=True)
-        log_total = top + jnp.log(jnp.sum(jnp.exp(lse - top), axis=0, keepdims=True))
-        picked = jnp.sum(stats_ref[:, 1, :], axis=0, keepdims=True)
-        target = target_ref[...]
-        loss_ref[...] = log_total - picked
-        log_total = by_arrival(jnp.broadcast_to(log_total, (8, 128)), i, j)[0:1]
-        for slot, (out, base) in enumerate(((own_ref, me), (other_ref, me ^ 8))):
-            ids = lax.broadcasted_iota(i32, (vocab_rows, 128), 0) + base * vocab_rows
-            hit = (ids == target).astype(f32)
-            coefs[slot] = jnp.where(target >= 0, jnp.exp(out[...] - log_total) - hit, 0.0).T.astype(bf16)
-
-    out_copies = []
-    for k, (at, size) in enumerate(chunks):
-        for copy in copies[k]:
-            copy.wait()
-        cols = pl.ds(at, size)
-        grad = jnp.dot(coefs[0], weights[0, :, cols], preferred_element_type=f32)
-        grad += jnp.dot(coefs[1], weights[1, :, cols], preferred_element_type=f32)
-        grads[:, cols] = grad * (loss_scale * send_scale)
-        for n, out in enumerate((g0, g1, g2, g3)):
-            copy = pltpu.make_async_copy(grads.at[pl.ds(n * 32, 32), cols], out.at[:, cols], sent.at[k, n])
-            copy.start()
-            out_copies.append(copy)
-    for copy in out_copies:
-        copy.wait()
-
-
-def grad_call(half, args, own, other):
-    vocab_rows = own.shape[0]
-    shapes = [jax.ShapeDtypeStruct((1, 128), f32), jax.ShapeDtypeStruct((2, 128, vocab_rows), bf16)]
+        compiler_params=pltpu.CompilerParams(vmem_limit_bytes=8 << 20),
+    )(*(([place] + list(partial)) if half else []), *rows, far(own), far(other))
+
+
+def coefficient_kernel(vocab_rows, place_ref, target_ref, stats_ref, own_ref, other_ref, loss_ref, own_coef, other_coef):
+    i, j, me = place_ref[0], place_ref[1], place_ref[2]
+    lse = stats_ref[:, 0, :]
+    top = jnp.max(lse, axis=0, keepdims=True)
+    log_total = top + jnp.log(jnp.sum(jnp.exp(lse - top), axis=0, keepdims=True))
+    picked = jnp.sum(stats_ref[:, 1, :], axis=0, keepdims=True)
+    target = target_ref[...]
+    loss_ref[...] = log_total - picked
+    log_total = by_arrival(jnp.broadcast_to(log_total, (8, 128)), i, j)[0:1]
+    for logits, coef, base in ((own_ref, own_coef, me), (other_ref, other_coef, me ^ 8)):
+        ids = lax.broadcasted_iota(i32, (vocab_rows, 128), 0) + base * vocab_rows
+        hit = (ids == target).astype(f32)
+        coef[...] = jnp.where(target >= 0, jnp.exp(logits[...] - log_total) - hit, 0.0).T.astype(bf16)
+
+
+def coefficient_call(place, target, stats, logits):
+    vocab_rows = logits[0].shape[0]
     return pl.pallas_call(
-        functools.partial(grad_kernel, half, vocab_rows),
-        in_specs=([vmem()] if half else [smem] + [vmem()] * 4) + [anywhere] * 2,
-        out_specs=[anywhere] * 4 + [vmem()] * (0 if half else 2),
-        out_shape=[jax.ShapeDtypeStruct((32, middle), f32)] * 4 + ([] if half else shapes),
-        scratch_shapes=[
-            pltpu.VMEM((2, vocab_rows, middle), bf16),
-            pltpu.VMEM((128, middle), f32),
-            pltpu.SemaphoreType.DMA((3, 2)),
-            pltpu.SemaphoreType.DMA((3, 4)),
-        ],
-    )(*args, own, other)
+        functools.partial(coefficient_kernel, vocab_rows),
+        in_specs=[smem] + [vmem()] * 4,
+        out_specs=[vmem()] * 3,
+        out_shape=[jax.ShapeDtypeStruct((1, 128), f32)] + [jax.ShapeDtypeStruct((128, vocab_rows), bf16)] * 2,
+        compiler_params=pltpu.CompilerParams(vmem_limit_bytes=4 << 20),
+        name="coefficient",
+    )(place, target, stats, *logits)
 
 
 def exchange(value, groups):
@@ -254,12 +228,17 @@
     halves = [jnp.concatenate([r[:, a:b] for r in rows], axis=0) for a, b in ((0, middle), (middle, wide))]
     first = gather4(halves[0], True)
     halves = [first, gather4(halves[1], True)]
-    partial = logits_call(0, place, None, halves[0], out_weight, other_weight)
-    *logits, stats, target = logits_call(1, place, partial, halves[1], out_weight, other_weight)
+    *partial, own, other = logits_call(0, place, None, halves[0], out_weight, other_weight)
+    near = [(own, other)]
+    *logits, own, other, stats, target = logits_call(1, place, partial, halves[1], out_weight, other_weight)
+    near.append((own, other))
     stats = exchange(stats, same_core)
-    *first, loss, coefs = grad_call(0, (place, target, stats, *logits), out_weight, other_weight)
-    second = grad_call(1, (coefs,), out_weight, other_weight)
-    parts = [reduce4([p.astype(send_type) for p in blocks], True) for blocks in (first, second)]
+    loss, *coefs = coefficient_call(place, target, stats, logits)
+    parts = []
+    for weights in near:
+        grad = sum(jnp.dot(k, w, preferred_element_type=f32) for k, w in zip(coefs, weights))
+        grad = (grad * (loss_scale * send_scale)).astype(send_type)
+        parts.append(reduce4([grad[k * 32:(k + 1) * 32] for k in R4], True))
     part = jnp.concatenate(parts, axis=1).astype(send_type)
     part = reduce4([part[k * 8:(k + 1) * 8] for k in R4], False)
     part = exchange(part.astype(send_type).reshape(8, width // 128, 128), along_z)

time: 148 us -> 130 us (0.88); the launches traced: 147 us -> 128 us
  Pallas kernels: 28.3 us -> 14.3 us
  other arithmetic: 10.5 us -> 3.38 us
  waiting for transfers between devices: 39.1 us -> 34.1 us
  matrix products: 0 us -> 4.29 us
  starting transfers between devices: 27.7 us -> 31.2 us
    pallas_call x2 -> x1, Pallas kernels: 12.9 us -> 0.97 us  [coefficient_call(): pl.pallas_call(functools.partial(coefficient_kernel, vocab_rows), in_spec...]
    convert_element_type x6 -> x0, other arithmetic: 6.5 us -> none  [shards(): p.astype(send_type)]
    ppermute x18, waiting for transfers between devices: 32 us -> 26.8 us  [shift(): return lax.ppermute(value, 'd', pairs)]
    dot_general x0 -> x4, matrix products: none -> 4.29 us  [shards(): jnp.dot(k, w, preferred_element_type=f32)]
    ppermute x18, starting transfers between devices: 24.2 us -> 27.7 us  [shift(): return lax.ppermute(value, 'd', pairs)]
    pallas_call x2, Pallas kernels: 13 us -> 10.9 us  [logits_call(): pl.pallas_call(functools.partial(logits_kernel, half, vocab_rows), in_spe...]
    unnamed x25 -> x3, local copies, waits for them, and re-layouts: 1.68 us -> 0.02 us
  transfers between devices with their start and end apart: 20 -> 20, of which waited for: 13 -> 14; matrix products, arithmetic and copies ran while one was open for 6% -> 3% of each run, Pallas kernels for 10% -> 6%
where the time goes in v5:
time: 130 us; the launch traced here: 128 us
  blocking collectives  37.4 us (29%)
  waiting for transfers between devices  34.1 us (26%)
  starting transfers between devices  31.2 us (24%)
  Pallas kernels  14.3 us (11%)
  matrix products  4.29 us (3%)
  other arithmetic  3.38 us (3%)
  local copies, waits for them, and re-layouts  1.63 us (1%)
  between operations  1.52 us (1%)
    all_to_all x2, blocking collectives, exchange(): return lax.all_to_all(value, 'd', 0, 0, axis_index_groups=groups)  37.4 us
    ppermute x18, starting transfers between devices, shift(): return lax.ppermute(value, 'd', pairs)  27.7 us
    ppermute x18, waiting for transfers between devices, shift(): return lax.ppermute(value, 'd', pairs)  26.8 us
    pallas_call x2, Pallas kernels, logits_call(): pl.pallas_call(functools.partial(logits_kernel, half, vocab_rows), in_spe...  10.9 us
    all_to_all x1, waiting for transfers between devices, exchange(): return lax.all_to_all(value, 'd', 0, 0, axis_index_groups=groups)  7.28 us
    dot_general x4, matrix products, shards(): jnp.dot(k, w, preferred_element_type=f32)  4.29 us
    all_to_all x1, starting transfers between devices, exchange(): return lax.all_to_all(value, 'd', 0, 0, axis_index_groups=groups)  3.37 us
  transfers between devices with their start and end apart: 20, of which 14 were waited for; matrix products, arithmetic and copies ran while one was open for 3% of the time, Pallas kernels for 6%

profile of v5, /device:TPU:2, one launch (start us, length us, event | category | flops | bytes accessed | tf_op | source)
XLA Modules:
  0.0 127.8 jit_solution(10908757232762835090)
XLA Ops:
  0.6 0.1 collective-permute-start.6
  1.4 2.5 %pack.1 = (bf16[8,2,4224]{2,1,0:T(2,128)(2,1)}, s32[1,128]{1,0:T(1,128)}) custom-call(s32[1]{0:T(128)S(6)} %copy.9.count_ref, s32[1,128]{1,0:T(1,128)} %bitcast.30, s32[1,128]{1,0:T(1,128)} %bitcast.31, bf16[128,8192]{1,0:T(8,128)(2,1)} %hidden_ref.1), custom_call_target="tpu_custom_call" | custom-call | tf_op jit(solution)/shard_map/pack/pallas_call | solution.py:74
  3.9 18.3 %all_to_all.15 = bf16[8,2,4224]{2,1,0:T(2,128)(2,1)S(1)} all-to-all(bf16[8,2,4224]{2,1,0:T(2,128)(2,1)} %get-tuple-element.18), channel_id=1, replica_groups={{0,1,2,3,4,5,6,7},{8,9,10,11,12,13,14,15},{16,17,18,19,20,21,22,23},{24..., dimensions={0} | all-to-all | bytes 270336 | tf_op jit(solution)/shard_map/all_to_all | solution.py:206
  22.2 1.6 %collective-permute-start.2 = (bf16[8,8448]{1,0:T(8,128)(2,1)S(1)}, bf16[8,8448]{1,0:T(8,128)(2,1)S(1)}, u32[]{:S(2)}, u32[]{:S(2)}) collective-permute-start(bf16[8,8448]{1,0:T(8,128)(2,1)S(1)} %bitcast.24), channel_id=1, source_target_pairs={{0,64},{1,65},{2,66},{3,67},{4,68},{5,69},{6,70},{7,71},{8,24},{9,... | collective-permute-start | bytes 405512 | tf_op jit(solution)/shard_map/ppermute | solution.py:42
  23.7 1.1 collective-permute-start.1
  24.8 2.2 %collective-permute-start = (bf16[8,8448]{1,0:T(8,128)(2,1)S(1)}, bf16[8,8448]{1,0:T(8,128)(2,1)S(1)}, u32[]{:S(2)}, u32[]{:S(2)}) collective-permute-start(bf16[8,8448]{1,0:T(8,128)(2,1)S(1)} %bitcast.26), channel_id=1, source_target_pairs={{0,192},{1,193},{2,194},{3,195},{4,196},{5,197},{6,198},{7,199},{8... | collective-permute-start | bytes 405512 | tf_op jit(solution)/shard_map/ppermute | solution.py:42
  27.0 0.2 collective-permute-done.2
  27.3 3.1 %collective-permute-done.1 = bf16[8,8448]{1,0:T(8,128)(2,1)S(1)} collective-permute-done((bf16[8,8448]{1,0:T(8,128)(2,1)S(1)}, bf16[8,8448]{1,0:T(8,128)(2,1)S(1)}, u32[]{:S(2)}, u32[]{:S(2)}) %collective-permute-start.1) | collective-permute-done | bytes 135200 | tf_op jit(solution)/shard_map/ppermute | solution.py:42
  30.4 0.9 collective-permute-done
  31.3 1.7 %collective-permute-start.5 = (bf16[32,4096]{1,0:T(8,128)(2,1)S(1)}, bf16[32,4096]{1,0:T(8,128)(2,1)S(1)}, u32[]{:S(2)}, u32[]{:S(2)}) collective-permute-start(bf16[32,4096]{1,0:T(8,128)(2,1)S(1)} %pad_maximum_fusion.1.refs_0_), channel_id=1, source_target_pairs={{0,16},{1,17},{2,18},{3,19},{4,20},{5,21},{6,22},{7,23},{8,72},{9,... | collective-permute-start | bytes 786440 | tf_op jit(solution)/shard_map/ppermute | solution.py:42
  33.0 2.9 %collective-permute-start.4 = (bf16[32,4096]{1,0:T(8,128)(2,1)S(1)}, bf16[32,4096]{1,0:T(8,128)(2,1)S(1)}, u32[]{:S(2)}, u32[]{:S(2)}) collective-permute-start(bf16[32,4096]{1,0:T(8,128)(2,1)S(1)} %pad_maximum_fusion.1.refs_0_), channel_id=1, source_target_pairs={{0,32},{1,33},{2,34},{3,35},{4,36},{5,37},{6,38},{7,39},{8,136},{9... | collective-permute-start | bytes 786440 | tf_op jit(solution)/shard_map/ppermute | solution.py:42
  36.0 0.1 collective-permute-start.9
  36.0 2.8 %collective-permute-start.8 = (bf16[32,4352]{1,0:T(8,128)(2,1)S(1)}, bf16[32,4352]{1,0:T(8,128)(2,1)S(1)}, u32[]{:S(2)}, u32[]{:S(2)}) collective-permute-start(bf16[32,4352]{1,0:T(8,128)(2,1)S(1)} %pad_maximum_fusion.refs_3_), channel_id=1, source_target_pairs={{0,32},{1,33},{2,34},{3,35},{4,36},{5,37},{6,38},{7,39},{8,136},{9... | collective-permute-start | bytes 835592 | tf_op jit(solution)/shard_map/ppermute | solution.py:42
  38.8 0.2 collective-permute-done.5.refs_3_
  39.0 1.8 %collective-permute-start.7 = (bf16[32,4352]{1,0:T(8,128)(2,1)S(1)}, bf16[32,4352]{1,0:T(8,128)(2,1)S(1)}, u32[]{:S(2)}, u32[]{:S(2)}) collective-permute-start(bf16[32,4352]{1,0:T(8,128)(2,1)S(1)} %pad_maximum_fusion.refs_3_), channel_id=1, source_target_pairs={{0,48},{1,49},{2,50},{3,51},{4,52},{5,53},{6,54},{7,55},{8,200},{9... | collective-permute-start | bytes 835592 | tf_op jit(solution)/shard_map/ppermute | solution.py:42
  40.8 2.3 %collective-permute-done.4.refs_2_ = bf16[32,4096]{1,0:T(8,128)(2,1)S(1)} collective-permute-done((bf16[32,4096]{1,0:T(8,128)(2,1)S(1)}, bf16[32,4096]{1,0:T(8,128)(2,1)S(1)}, u32[]{:S(2)}, u32[]{:S(2)}) %collective-permute-start.4) | collective-permute-done | bytes 262176 | tf_op jit(solution)/shard_map/ppermute | solution.py:42
  43.1 0.0 collective-permute-start.3
  43.1 0.1 pad_add_fusion.refs_0_.place_ref
  43.2 7.2 %collective-permute-done.3.refs_1_ = bf16[32,4096]{1,0:T(8,128)(2,1)S(1)} collective-permute-done((bf16[32,4096]{1,0:T(8,128)(2,1)S(1)}, bf16[32,4096]{1,0:T(8,128)(2,1)S(1)}, u32[]{:S(2)}, u32[]{:S(2)}) %collective-permute-start.3) | collective-permute-done | bytes 262176 | tf_op jit(solution)/shard_map/ppermute | solution.py:42
  50.5 0.0 collective-permute-done.6.refs_5_.refs_8_
  50.5 4.9 %shard_map.68 = (f32[501,128]{1,0:T(8,128)S(1)}, f32[501,128]{1,0:T(8,128)S(1)}, bf16[501,4096]{1,0:T(8,128)(2,1)S(1)}, bf16[501,4096]{1,0:T(8,128)(2,1)S(1)}) custom-call(bf16[32,4096]{1,0:T(8,128)(2,1)S(1)} %pad_maximum_fusion.1.refs_0_, bf16[32,4096]{1,0:T(8,128)(2,1)S(1)} %collective-permute-done.3.refs_1_, ...), custom_call_target="tpu_custom_call" | custom-call | tf_op jit(solution)/shard_map/pallas_call | solution.py:165
  55.4 0.0 collective-permute-done.9.refs_6_
  55.4 0.0 collective-permute-done.8.refs_5_
  55.4 0.0 collective-permute-done.7.refs_4_
  55.4 6.0 %shard_map.69 = (f32[501,128]{1,0:T(8,128)S(1)}, f32[501,128]{1,0:T(8,128)S(1)}, bf16[501,4096]{1,0:T(8,128)(2,1)S(1)}, bf16[501,4096]{1,0:T(8,128)(2,1)S(1)}, f...) custom-call(s32[3]{0:T(128)S(1)} %pad_add_fusion.refs_0_.place_ref, f32[501,128]{1,0:T(8,128)S(1)} %get-tuple-element.19.refs_1_, ...), custom_call_target="tpu_custom_call" | custom-call | tf_op jit(solution)/shard_map/pallas_call | solution.py:165
  61.4 19.1 %all_to_all.16.stats_ref = f32[128,2,128]{2,1,0:T(2,128)S(1)} all-to-all(f32[128,2,128]{2,1,0:T(2,128)S(1)} %get-tuple-element.22), channel_id=1, replica_groups={{0,1,2,3,4,5,6,7,16,17,18,19,20,21,22,23,32,33,34,35,36,37,38,39,48,49,..., dimensions={0} | all-to-all | bytes 262144 | tf_op jit(solution)/shard_map/all_to_all | solution.py:206
  80.5 1.0 coefficient.1
  81.5 1.1 fusion.11
  82.6 1.1 fusion.10
  83.6 1.1 fusion.2
  84.7 0.1 fusion.8
  84.9 0.7 collective-permute-start.10
  85.5 2.7 %collective-permute-start.12 = (f16[32,4096]{1,0:T(8,128)(2,1)S(1)}, f16[32,4096]{1,0:T(8,128)(2,1)S(1)}, u32[]{:S(2)}, u32[]{:S(2)}) collective-permute-start(f16[32,4096]{1,0:T(8,128)(2,1)S(1)} %get-tuple-element.33), channel_id=1, source_target_pairs={{0,48},{1,49},{2,50},{3,51},{4,52},{5,53},{6,54},{7,55},{8,200},{9... | collective-permute-start | bytes 786440 | tf_op jit(solution)/shard_map/ppermute | solution.py:42
  88.2 0.6 collective-permute-start.11
  88.8 1.1 fusion.3
  89.9 0.0 copy-start
  89.9 0.1 fusion.9
  90.1 0.7 collective-permute-start.13
  90.7 2.7 %collective-permute-start.15 = (f16[32,4096]{1,0:T(8,128)(2,1)S(1)}, f16[32,4096]{1,0:T(8,128)(2,1)S(1)}, u32[]{:S(2)}, u32[]{:S(2)}) collective-permute-start(f16[32,4096]{1,0:T(8,128)(2,1)S(1)} %get-tuple-element.36), channel_id=1, source_target_pairs={{0,48},{1,49},{2,50},{3,51},{4,52},{5,53},{6,54},{7,55},{8,200},{9... | collective-permute-start | bytes 786440 | tf_op jit(solution)/shard_map/ppermute | solution.py:42
  93.4 0.0 collective-permute-done.10
  93.4 1.7 %collective-permute-start.14 = (f16[32,4096]{1,0:T(8,128)(2,1)S(1)}, f16[32,4096]{1,0:T(8,128)(2,1)S(1)}, u32[]{:S(2)}, u32[]{:S(2)}) collective-permute-start(f16[32,4096]{1,0:T(8,128)(2,1)S(1)} %get-tuple-element.37), channel_id=1, source_target_pairs={{0,32},{1,33},{2,34},{3,35},{4,36},{5,37},{6,38},{7,39},{8,136},{9... | collective-permute-start | bytes 786440 | tf_op jit(solution)/shard_map/ppermute | solution.py:42
  95.1 0.0 collective-permute-done.12
  95.1 1.1 collective-permute-done.11
  96.2 0.1 add_convert_fusion.1
  96.3 2.6 %collective-permute-done.13 = f16[32,4096]{1,0:T(8,128)(2,1)S(1)} collective-permute-done((f16[32,4096]{1,0:T(8,128)(2,1)S(1)}, f16[32,4096]{1,0:T(8,128)(2,1)S(1)}, u32[]{:S(2)}, u32[]{:S(2)}) %collective-permute-start.13) | collective-permute-done | bytes 262176 | tf_op jit(solution)/shard_map/ppermute | solution.py:42
  98.9 1.3 %collective-permute-done.15 = f16[32,4096]{1,0:T(8,128)(2,1)S(1)} collective-permute-done((f16[32,4096]{1,0:T(8,128)(2,1)S(1)}, f16[32,4096]{1,0:T(8,128)(2,1)S(1)}, u32[]{:S(2)}, u32[]{:S(2)}) %collective-permute-start.15) | collective-permute-done | bytes 262176 | tf_op jit(solution)/shard_map/ppermute | solution.py:42
  100.2 3.3 %collective-permute-done.14 = f16[32,4096]{1,0:T(8,128)(2,1)S(1)} collective-permute-done((f16[32,4096]{1,0:T(8,128)(2,1)S(1)}, f16[32,4096]{1,0:T(8,128)(2,1)S(1)}, u32[]{:S(2)}, u32[]{:S(2)}) %collective-permute-start.14) | collective-permute-done | bytes 262176 | tf_op jit(solution)/shard_map/ppermute | solution.py:42
  103.5 0.1 add_convert_fusion
  103.7 0.1 fusion.7
  103.8 2.1 %collective-permute-start.16 = (f16[8,8192]{1,0:T(8,128)(2,1)S(1)}, f16[8,8192]{1,0:T(8,128)(2,1)S(1)}, u32[]{:S(2)}, u32[]{:S(2)}) collective-permute-start(f16[8,8192]{1,0:T(8,128)(2,1)S(1)} %get-tuple-element.38), channel_id=1, source_target_pairs={{0,64},{1,65},{2,66},{3,67},{4,68},{5,69},{6,70},{7,71},{8,24},{9,... | collective-permute-start | bytes 393224 | tf_op jit(solution)/shard_map/ppermute | solution.py:42
  105.9 0.6 collective-permute-start.18
  106.5 2.0 %collective-permute-start.17 = (f16[8,8192]{1,0:T(8,128)(2,1)S(1)}, f16[8,8192]{1,0:T(8,128)(2,1)S(1)}, u32[]{:S(2)}, u32[]{:S(2)}) collective-permute-start(f16[8,8192]{1,0:T(8,128)(2,1)S(1)} %get-tuple-element.40), channel_id=1, source_target_pairs={{0,128},{1,129},{2,130},{3,131},{4,132},{5,133},{6,134},{7,135},{8... | collective-permute-start | bytes 393224 | tf_op jit(solution)/shard_map/ppermute | solution.py:42
  108.4 0.9 collective-permute-done.16
  109.3 1.5 %collective-permute-done.18 = f16[8,8192]{1,0:T(8,128)(2,1)S(1)} collective-permute-done((f16[8,8192]{1,0:T(8,128)(2,1)S(1)}, f16[8,8192]{1,0:T(8,128)(2,1)S(1)}, u32[]{:S(2)}, u32[]{:S(2)}) %collective-permute-start.18) | collective-permute-done | bytes 131104 | tf_op jit(solution)/shard_map/ppermute | solution.py:42
  110.8 2.1 %collective-permute-done.17 = f16[8,8192]{1,0:T(8,128)(2,1)S(1)} collective-permute-done((f16[8,8192]{1,0:T(8,128)(2,1)S(1)}, f16[8,8192]{1,0:T(8,128)(2,1)S(1)}, u32[]{:S(2)}, u32[]{:S(2)}) %collective-permute-start.17) | collective-permute-done | bytes 131104 | tf_op jit(solution)/shard_map/ppermute | solution.py:42
  112.9 0.1 fusion.4
  113.0 0.7 copy.7
  113.7 3.4 %all-to-all-start.2 = ((f16[8,64,128]{2,1,0:T(8,128)(2,1)}), f16[8,64,128]{2,1,0:T(8,128)(2,1)S(1)}, u32[]{:S(2)}, u32[]{:S(2)}) async-start(f16[8,64,128]{2,1,0:T(8,128)(2,1)} %copy.7), calls=%async_computation.2 | async-start | bytes 262144 | tf_op jit(solution)/shard_map/all_to_all | solution.py:206
  117.1 0.0 copy-done
  117.1 0.6 constant_dynamic-slice_fusion
  117.7 1.1 broadcast_select_fusion
  118.8 7.3 %all-to-all-done.2 = f16[8,64,128]{2,1,0:T(8,128)(2,1)S(1)} async-done(((f16[8,64,128]{2,1,0:T(8,128)(2,1)}), f16[8,64,128]{2,1,0:T(8,128)(2,1)S(1)}, u32[]{:S(2)}, u32[]{:S(2)}) %all-to-all-start.2) | async-done | bytes 131104 | tf_op jit(solution)/shard_map/all_to_all | solution.py:206
  126.1 1.7 %select_convert_fusion = bf16[128,8192]{1,0:T(8,128)(2,1)} fusion(bf16[8192]{0:T(1024)(128)(2,1)S(1)} %multiply_bitcast_fusion, pred[128]{0:T(512)(128)(4,1)S(1)} %compare_bitcast_fusion), kind=kLoop, calls=%fused_computation.6 | loop fusion | flops 1048576 | bytes 2113664 | tf_op jit(solution)/shard_map/convert_element_type | solution.py:249
  (14 shorter events, 0.1 us)
Async XLA Ops:
  0.6 49.8 %collective-permute-start.6 = (bf16[501,8192]{1,0:T(8,128)(2,1)}, bf16[501,8192]{1,0:T(8,128)(2,1)}, u32[]{:S(2)}, u32[]{:S(2)}) collective-permute-start(bf16[501,8192]{1,0:T(8,128)(2,1)} %refs_7_.1), channel_id=1, source_target_pairs={{0,8},{1,9},{2,10},{3,11},{4,12},{5,13},{6,14},{7,15},{8,0},{9,1},... | collective-permute-start | bytes 24625160 | tf_op jit(solution)/shard_map/ppermute | solution.py:224
  22.2 5.1 %collective-permute-start.2 = (bf16[8,8448]{1,0:T(8,128)(2,1)S(1)}, bf16[8,8448]{1,0:T(8,128)(2,1)S(1)}, u32[]{:S(2)}, u32[]{:S(2)}) collective-permute-start(bf16[8,8448]{1,0:T(8,128)(2,1)S(1)} %bitcast.24), channel_id=1, source_target_pairs={{0,64},{1,65},{2,66},{3,67},{4,68},{5,69},{6,70},{7,71},{8,24},{9,... | collective-permute-start | bytes 405512 | tf_op jit(solution)/shard_map/ppermute | solution.py:42
  23.7 6.6 %collective-permute-start.1 = (bf16[8,8448]{1,0:T(8,128)(2,1)S(1)}, bf16[8,8448]{1,0:T(8,128)(2,1)S(1)}, u32[]{:S(2)}, u32[]{:S(2)}) collective-permute-start(bf16[8,8448]{1,0:T(8,128)(2,1)S(1)} %bitcast.25), channel_id=1, source_target_pairs={{0,128},{1,129},{2,130},{3,131},{4,132},{5,133},{6,134},{7,135},{8... | collective-permute-start | bytes 405512 | tf_op jit(solution)/shard_map/ppermute | solution.py:42
  24.8 6.5 %collective-permute-start = (bf16[8,8448]{1,0:T(8,128)(2,1)S(1)}, bf16[8,8448]{1,0:T(8,128)(2,1)S(1)}, u32[]{:S(2)}, u32[]{:S(2)}) collective-permute-start(bf16[8,8448]{1,0:T(8,128)(2,1)S(1)} %bitcast.26), channel_id=1, source_target_pairs={{0,192},{1,193},{2,194},{3,195},{4,196},{5,197},{6,198},{7,199},{8... | collective-permute-start | bytes 405512 | tf_op jit(solution)/shard_map/ppermute | solution.py:42
  31.3 7.7 %collective-permute-start.5 = (bf16[32,4096]{1,0:T(8,128)(2,1)S(1)}, bf16[32,4096]{1,0:T(8,128)(2,1)S(1)}, u32[]{:S(2)}, u32[]{:S(2)}) collective-permute-start(bf16[32,4096]{1,0:T(8,128)(2,1)S(1)} %pad_maximum_fusion.1.refs_0_), channel_id=1, source_target_pairs={{0,16},{1,17},{2,18},{3,19},{4,20},{5,21},{6,22},{7,23},{8,72},{9,... | collective-permute-start | bytes 786440 | tf_op jit(solution)/shard_map/ppermute | solution.py:42
  33.0 10.2 %collective-permute-start.4 = (bf16[32,4096]{1,0:T(8,128)(2,1)S(1)}, bf16[32,4096]{1,0:T(8,128)(2,1)S(1)}, u32[]{:S(2)}, u32[]{:S(2)}) collective-permute-start(bf16[32,4096]{1,0:T(8,128)(2,1)S(1)} %pad_maximum_fusion.1.refs_0_), channel_id=1, source_target_pairs={{0,32},{1,33},{2,34},{3,35},{4,36},{5,37},{6,38},{7,39},{8,136},{9... | collective-permute-start | bytes 786440 | tf_op jit(solution)/shard_map/ppermute | solution.py:42
  36.0 19.5 %collective-permute-start.9 = (bf16[32,4352]{1,0:T(8,128)(2,1)S(1)}, bf16[32,4352]{1,0:T(8,128)(2,1)S(1)}, u32[]{:S(2)}, u32[]{:S(2)}) collective-permute-start(bf16[32,4352]{1,0:T(8,128)(2,1)S(1)} %pad_maximum_fusion.refs_3_), channel_id=1, source_target_pairs={{0,16},{1,17},{2,18},{3,19},{4,20},{5,21},{6,22},{7,23},{8,72},{9,... | collective-permute-start | bytes 835592 | tf_op jit(solution)/shard_map/ppermute | solution.py:42
  36.0 19.4 %collective-permute-start.8 = (bf16[32,4352]{1,0:T(8,128)(2,1)S(1)}, bf16[32,4352]{1,0:T(8,128)(2,1)S(1)}, u32[]{:S(2)}, u32[]{:S(2)}) collective-permute-start(bf16[32,4352]{1,0:T(8,128)(2,1)S(1)} %pad_maximum_fusion.refs_3_), channel_id=1, source_target_pairs={{0,32},{1,33},{2,34},{3,35},{4,36},{5,37},{6,38},{7,39},{8,136},{9... | collective-permute-start | bytes 835592 | tf_op jit(solution)/shard_map/ppermute | solution.py:42
  39.0 16.4 %collective-permute-start.7 = (bf16[32,4352]{1,0:T(8,128)(2,1)S(1)}, bf16[32,4352]{1,0:T(8,128)(2,1)S(1)}, u32[]{:S(2)}, u32[]{:S(2)}) collective-permute-start(bf16[32,4352]{1,0:T(8,128)(2,1)S(1)} %pad_maximum_fusion.refs_3_), channel_id=1, source_target_pairs={{0,48},{1,49},{2,50},{3,51},{4,52},{5,53},{6,54},{7,55},{8,200},{9... | collective-permute-start | bytes 835592 | tf_op jit(solution)/shard_map/ppermute | solution.py:42
  43.1 7.3 %collective-permute-start.3 = (bf16[32,4096]{1,0:T(8,128)(2,1)S(1)}, bf16[32,4096]{1,0:T(8,128)(2,1)S(1)}, u32[]{:S(2)}, u32[]{:S(2)}) collective-permute-start(bf16[32,4096]{1,0:T(8,128)(2,1)S(1)} %pad_maximum_fusion.1.refs_0_), channel_id=1, source_target_pairs={{0,48},{1,49},{2,50},{3,51},{4,52},{5,53},{6,54},{7,55},{8,200},{9... | collective-permute-start | bytes 786440 | tf_op jit(solution)/shard_map/ppermute | solution.py:42
  84.9 8.5 %collective-permute-start.10 = (f16[32,4096]{1,0:T(8,128)(2,1)S(1)}, f16[32,4096]{1,0:T(8,128)(2,1)S(1)}, u32[]{:S(2)}, u32[]{:S(2)}) collective-permute-start(f16[32,4096]{1,0:T(8,128)(2,1)S(1)} %get-tuple-element.32), channel_id=1, source_target_pairs={{0,16},{1,17},{2,18},{3,19},{4,20},{5,21},{6,22},{7,23},{8,72},{9,... | collective-permute-start | bytes 786440 | tf_op jit(solution)/shard_map/ppermute | solution.py:42
  85.5 9.5 %collective-permute-start.12 = (f16[32,4096]{1,0:T(8,128)(2,1)S(1)}, f16[32,4096]{1,0:T(8,128)(2,1)S(1)}, u32[]{:S(2)}, u32[]{:S(2)}) collective-permute-start(f16[32,4096]{1,0:T(8,128)(2,1)S(1)} %get-tuple-element.33), channel_id=1, source_target_pairs={{0,48},{1,49},{2,50},{3,51},{4,52},{5,53},{6,54},{7,55},{8,200},{9... | collective-permute-start | bytes 786440 | tf_op jit(solution)/shard_map/ppermute | solution.py:42
  88.2 8.0 %collective-permute-start.11 = (f16[32,4096]{1,0:T(8,128)(2,1)S(1)}, f16[32,4096]{1,0:T(8,128)(2,1)S(1)}, u32[]{:S(2)}, u32[]{:S(2)}) collective-permute-start(f16[32,4096]{1,0:T(8,128)(2,1)S(1)} %get-tuple-element.34), channel_id=1, source_target_pairs={{0,32},{1,33},{2,34},{3,35},{4,36},{5,37},{6,38},{7,39},{8,136},{9... | collective-permute-start | bytes 786440 | tf_op jit(solution)/shard_map/ppermute | solution.py:42
  89.9 27.2 %copy-start = (s32[1,128]{1,0:T(1,128)S(1)}, s32[1,128]{1,0:T(1,128)}, u32[]{:S(2)}) copy-start(s32[1,128]{1,0:T(1,128)} %get-tuple-element.17) | copy-start | bytes 1540
  90.1 8.8 %collective-permute-start.13 = (f16[32,4096]{1,0:T(8,128)(2,1)S(1)}, f16[32,4096]{1,0:T(8,128)(2,1)S(1)}, u32[]{:S(2)}, u32[]{:S(2)}) collective-permute-start(f16[32,4096]{1,0:T(8,128)(2,1)S(1)} %get-tuple-element.35), channel_id=1, source_target_pairs={{0,16},{1,17},{2,18},{3,19},{4,20},{5,21},{6,22},{7,23},{8,72},{9,... | collective-permute-start | bytes 786440 | tf_op jit(solution)/shard_map/ppermute | solution.py:42
  90.7 9.5 %collective-permute-start.15 = (f16[32,4096]{1,0:T(8,128)(2,1)S(1)}, f16[32,4096]{1,0:T(8,128)(2,1)S(1)}, u32[]{:S(2)}, u32[]{:S(2)}) collective-permute-start(f16[32,4096]{1,0:T(8,128)(2,1)S(1)} %get-tuple-element.36), channel_id=1, source_target_pairs={{0,48},{1,49},{2,50},{3,51},{4,52},{5,53},{6,54},{7,55},{8,200},{9... | collective-permute-start | bytes 786440 | tf_op jit(solution)/shard_map/ppermute | solution.py:42
  93.4 10.1 %collective-permute-start.14 = (f16[32,4096]{1,0:T(8,128)(2,1)S(1)}, f16[32,4096]{1,0:T(8,128)(2,1)S(1)}, u32[]{:S(2)}, u32[]{:S(2)}) collective-permute-start(f16[32,4096]{1,0:T(8,128)(2,1)S(1)} %get-tuple-element.37), channel_id=1, source_target_pairs={{0,32},{1,33},{2,34},{3,35},{4,36},{5,37},{6,38},{7,39},{8,136},{9... | collective-permute-start | bytes 786440 | tf_op jit(solution)/shard_map/ppermute | solution.py:42
  103.8 5.5 %collective-permute-start.16 = (f16[8,8192]{1,0:T(8,128)(2,1)S(1)}, f16[8,8192]{1,0:T(8,128)(2,1)S(1)}, u32[]{:S(2)}, u32[]{:S(2)}) collective-permute-start(f16[8,8192]{1,0:T(8,128)(2,1)S(1)} %get-tuple-element.38), channel_id=1, source_target_pairs={{0,64},{1,65},{2,66},{3,67},{4,68},{5,69},{6,70},{7,71},{8,24},{9,... | collective-permute-start | bytes 393224 | tf_op jit(solution)/shard_map/ppermute | solution.py:42
  105.9 5.0 %collective-permute-start.18 = (f16[8,8192]{1,0:T(8,128)(2,1)S(1)}, f16[8,8192]{1,0:T(8,128)(2,1)S(1)}, u32[]{:S(2)}, u32[]{:S(2)}) collective-permute-start(f16[8,8192]{1,0:T(8,128)(2,1)S(1)} %get-tuple-element.39), channel_id=1, source_target_pairs={{0,192},{1,193},{2,194},{3,195},{4,196},{5,197},{6,198},{7,199},{8... | collective-permute-start | bytes 393224 | tf_op jit(solution)/shard_map/ppermute | solution.py:42
  106.5 6.5 %collective-permute-start.17 = (f16[8,8192]{1,0:T(8,128)(2,1)S(1)}, f16[8,8192]{1,0:T(8,128)(2,1)S(1)}, u32[]{:S(2)}, u32[]{:S(2)}) collective-permute-start(f16[8,8192]{1,0:T(8,128)(2,1)S(1)} %get-tuple-element.40), channel_id=1, source_target_pairs={{0,128},{1,129},{2,130},{3,131},{4,132},{5,133},{6,134},{7,135},{8... | collective-permute-start | bytes 393224 | tf_op jit(solution)/shard_map/ppermute | solution.py:42
  113.7 12.4 %all-to-all-start.2 = ((f16[8,64,128]{2,1,0:T(8,128)(2,1)}), f16[8,64,128]{2,1,0:T(8,128)(2,1)S(1)}, u32[]{:S(2)}, u32[]{:S(2)}) async-start(f16[8,64,128]{2,1,0:T(8,128)(2,1)} %copy.7), calls=%async_computation.2 | async-start | bytes 262144 | tf_op jit(solution)/shard_map/all_to_all | solution.py:206
